TPU v7x, 512 devices: a whole 4x8x8 slice. The times are simulated.
512 devices in a mesh: ha: 16 (over x, y_lo), wa: 32 (over y_hi, z, core).
Axes of the slice: x: 4, y: 8 (y_hi: 2, y_lo: 4; y = y_hi * 4 + y_lo), z: 8, core: 2. Of those that a mesh axis runs over, the one named last changes fastest.
Arguments:
- velocity: float32 [2, 1024, 4096], P(None, 'wa', 'ha'), may hold values from -6 to 6
- cotangent: float32 [2, 1024, 4096], P(None, 'wa', 'ha'), may hold values from -6 to 6
- lift_weight: float32 [64, 2], replicated, may hold values from -4 to 4
- depth_kernels: float32 [1, 64, 9], replicated, may hold values from -2 to 2
- point_weights: bfloat16 [1, 64, 64], replicated, may hold values from -0.75 to 0.75
- out_weight: bfloat16 [2, 64], replicated, may hold values from -0.75 to 0.75
Outputs:
- grad_velocity: float32 [2, 1024, 4096], P(None, 'wa', 'ha')
- grad_lift: float32 [64, 2], replicated
- grad_kernels: float32 [1, 64, 9], replicated
- grad_point: float32 [1, 64, 64], replicated
- grad_out: float32 [2, 64], replicated
All inputs are finite; a program needn't handle non-finite values.
Results may differ from a plain program's by a relative error of at most 0.012.
Values may be sent and summed in bfloat16 or wider, within the bound.
No kernel may reach another device: no remote copies, remote signals or barrier semaphores. Data moves between devices by JAX's collectives and lax.ppermute only.
A program may use at most 64 MiB of HBM per device.

v0:
```python
import math

import jax
import jax.numpy as jnp
import ml_dtypes
import numpy as np
from jax import lax
from jax.experimental import pallas as pl
from jax.experimental.pallas import tpu as pltpu
from jax.sharding import PartitionSpec as P

BF = jnp.bfloat16
F32 = jnp.float32
HA, WA = 16, 32
ROWS, COLS = 32, 256
NX, NY = WA * ROWS, HA * COLS
TWO_PI = 2.0 * math.pi
COL_ID = np.concatenate([np.arange(256), [-1, 256]])


def bf(table):
    return np.asarray(table).astype(ml_dtypes.bfloat16)


def pair(table):
    high = bf(table)
    return np.stack([high, bf(table - high.astype(np.float64))])


def make_tables():
    r = np.arange(256)
    k2 = np.arange(128)
    ang = TWO_PI * (np.outer(k2, r) % 256) / 256
    c, s = np.cos(ang), np.sin(ang)
    t1 = np.stack([np.concatenate([c, s], 1), np.concatenate([-s, c], 1)], 1)
    t1 = t1.reshape(32, 4, 2, 512).transpose(1, 0, 2, 3).reshape(256, 512)

    n32 = np.arange(32)
    a32 = TWO_PI * (np.outer(n32, n32) % 32) / 32
    c32, s32 = np.cos(a32), np.sin(a32)
    d1 = np.zeros((4, 32, 32, 2))
    d1[0, :, :, 0] = c32
    d1[1, :, :, 0] = -s32
    d1[2, :, :, 1] = c32
    d1[3, :, :, 1] = -s32
    d1 = d1.reshape(128, 64)
    tw = TWO_PI * np.outer(n32, np.tile(n32, 8)) / 1024
    tw1 = np.stack([np.cos(tw), np.sin(tw)]).astype(np.float32)

    kr = np.zeros((2, 4, 32, 2, 4, 32))
    ik = np.zeros((2, 4, 32, 2, 256))
    rows = np.concatenate([n32, [-1, 32]])
    a = TWO_PI * np.outer(n32, rows) / 32
    row_of = np.zeros(256)
    for j in range(4):
        kr[0, j, :, 0, j, :] = c32
        kr[1, j, :, 0, j, :] = s32
        kr[1, j, :, 1, j, :] = c32
        kr[0, j, :, 1, j, :] = -s32
        lanes = list(range(j * 32, j * 32 + 32)) + [128 + j * 2, 129 + j * 2]
        row_of[lanes] = rows
        ik[0, j, :, 0, lanes] = np.cos(a).T
        ik[1, j, :, 0, lanes] = -np.sin(a).T
        ik[0, j, :, 1, lanes] = np.sin(a).T
        ik[1, j, :, 1, lanes] = np.cos(a).T
    kr = kr.reshape(256, 256)
    ik = ik.reshape(256, 512)
    tw = TWO_PI * np.outer(n32, row_of) / 1024
    tw2 = np.stack([np.cos(tw), np.sin(tw)]).astype(np.float32)
    d2 = np.zeros((32, 2, 2, 32))
    d2[:, 0, 0] = c32
    d2[:, 0, 1] = -s32
    d2[:, 1, 0] = s32
    d2[:, 1, 1] = c32
    d2 = d2.reshape(64, 64)

    ang = TWO_PI * (np.outer(k2, COL_ID) % 256) / 256
    tk = np.zeros((128, 2, 2, 384))
    tk[:, 0, 0, :258] = 2 * np.cos(ang)
    tk[:, 1, 0, :258] = -2 * np.sin(ang)
    tk[:, 0, 1, :258] = 2 * np.sin(ang)
    tk[:, 1, 1, :258] = 2 * np.cos(ang)
    tk = tk.reshape(32, 4, 2, 768).transpose(1, 0, 2, 3).reshape(256, 768)
    return dict(t1=pair(t1), d1=pair(d1), tw1=tw1, kr=pair(kr), ik=pair(ik), tw2=tw2, d2=pair(d2), tk=pair(tk))


def mm(a, b, ca=1, cb=0):
    return lax.dot_general(a, b, (((ca,), (cb,)), ((), ())), preferred_element_type=F32)


def halves(value):
    high = value.astype(BF)
    return high, (value - high.astype(F32)).astype(BF)


def mm3(a, b, ca=1, cb=0):
    return mm(a[0], b[0], ca, cb) + (mm(a[1], b[0], ca, cb) + mm(a[0], b[1], ca, cb))


def y_forward(got, turn, sign, t1):
    re = jnp.zeros((64, 256), F32)
    im = jnp.zeros((64, 256), F32)
    for q in range(HA):
        part = got[q, :64].astype(F32)
        re = re + part * turn[0, q : q + 1]
        im = im - part * turn[1, q : q + 1]
    both = halves(jnp.concatenate([re, im], axis=1))
    row = lax.broadcasted_iota(jnp.int32, (64, 256), 0)
    pick = jnp.where(row == 1, sign, 0.0).astype(BF)
    out = []
    for j in range(4):
        block = mm3((t1[0, j * 64 : (j + 1) * 64], t1[1, j * 64 : (j + 1) * 64]), both, 1, 1)
        if j == 0:
            block = block + mm(pick, both[0][:, :256], 1, 1) + mm(pick, both[1][:, :256], 1, 1)
        out.append(block)
    pieces = [out[j][:, 32 * c : 32 * c + 32] for c in range(2) for j in range(4)]
    return jnp.concatenate(pieces, axis=1).astype(BF)


def x_project(lines, ky_lane, d1, tw1, kr, ik, tw2, d2):
    first = mm(d1[0], lines) + mm(d1[1], lines)
    cs, sn = tw1[0], tw1[1]
    turned = []
    for c in range(2):
        for p in range(2):
            re = first[64 * p : 64 * p + 32]
            im = first[64 * p + 32 : 64 * p + 64]
            span = slice(128 * c, 128 * c + 128)
            turned.append(
                jnp.concatenate([(re * cs + im * sn)[:, span], (im * cs - re * sn)[:, span]], axis=1)
            )
    spec = mm3(halves(jnp.concatenate(turned, axis=0)), kr)
    lane = lax.broadcasted_iota(jnp.int32, (32, 128), 1)
    kx = lax.broadcasted_iota(jnp.int32, (32, 128), 0) + 32 * (lane % 32)
    kx = jnp.where(2 * kx >= NX, kx - NX, kx).astype(F32)
    ky = jnp.broadcast_to(ky_lane, (32, 128))
    edge_x = kx == -float(NX // 2)

    def factors(wave_y, edge_y):
        inv = 1.0 / jnp.maximum(kx * kx + wave_y * wave_y, 1.0)
        scale = 1.0 / float(NX * NY)
        cross = jnp.where(edge_x != edge_y, 0.0, -kx * wave_y * inv)
        return (1.0 - kx * kx * inv) * scale, cross * scale, (1.0 - wave_y * wave_y * inv) * scale

    ar, br, dr = factors(ky, jnp.zeros((32, 128), jnp.bool_))
    packed = ky == 0.0
    ai, bi, di = factors(jnp.where(packed, -float(NY // 2), ky), packed)
    (r0, r0i), (i0, i0i), (r1, r1i), (i1, i1i) = (
        (spec[32 * i : 32 * i + 32, :128], spec[32 * i : 32 * i + 32, 128:]) for i in range(4)
    )
    first = jnp.concatenate(
        [ar * r0 + br * r1 - (ai * i0i + bi * i1i), ar * r0i + br * r1i + ai * i0 + bi * i1], axis=1
    )
    second = jnp.concatenate(
        [br * r0 + dr * r1 - (bi * i0i + di * i1i), br * r0i + dr * r1i + bi * i0 + di * i1], axis=1
    )
    back = mm3(halves(jnp.concatenate([first, second], axis=0)), ik)
    cs, sn = tw2[0], tw2[1]
    main, rim = [], []
    for c in range(2):
        re = back[32 * c : 32 * c + 32, :256]
        im = back[32 * c : 32 * c + 32, 256:]
        value = jnp.concatenate([re * cs - im * sn, re * sn + im * cs], axis=0)
        main.append(value[:, :128])
        rim.append(value[:, 128:136])
    stack = jnp.concatenate(main + rim + [jnp.zeros((64, 112), F32)], axis=1)
    return mm3(d2, halves(stack)).astype(BF)


def regroup(lines):
    a = lax.broadcasted_iota(jnp.int32, (64, 64), 0)
    b = lax.broadcasted_iota(jnp.int32, (64, 64), 1)
    eye = jnp.where(a == b, 1.0, 0.0).astype(BF)
    turned = mm(lines, eye, 0, 0)
    main = jnp.concatenate(
        [
            jnp.concatenate([turned[32 * j : 32 * j + 32] for j in range(4)], axis=1),
            jnp.concatenate([turned[128 + 32 * j : 160 + 32 * j] for j in range(4)], axis=1),
        ],
        axis=0,
    )
    rim = jnp.concatenate(
        [jnp.concatenate([turned[256 + 8 * c + 2 * j : 258 + 8 * c + 2 * j] for j in range(4)], axis=1) for c in range(2)],
        axis=0,
    )
    return jnp.concatenate([main, rim, jnp.zeros((12, 256), F32)], axis=0).astype(BF)


def y_inverse(got, turn, tk):
    lane = lax.broadcasted_iota(jnp.int32, (1, 384), 1)
    odd = jnp.where(lane < 256, lane % 2, (lane == 256).astype(jnp.int32)).astype(F32)
    own = got[0].astype(F32)
    acc = own[:, 1:2] * (1.0 - 2.0 * odd) - own[:, 0:1]
    acc = acc + mm(got[0], tk[0, :, :384]) + mm(got[0], tk[1, :, :384])
    for q in range(1, HA):
        part = mm(got[q], tk[0]) + mm(got[q], tk[1])
        acc = acc + part[:, :384] * turn[0, q : q + 1] - part[:, 384:] * turn[1, q : q + 1]
    return acc


def network(proj, planes, center, point, lift18, out_cols):
    mix = lax.dot_general(point, lift18, (((1,), (0,)), ((), ())), precision=lax.Precision.HIGHEST, preferred_element_type=F32)
    mix_b = mix.astype(BF)
    proj_b = proj.astype(BF).astype(F32)
    taps = [None] * 34
    sums = jnp.zeros((32, 128), F32)
    for i in range(-1, 33):
        view = planes[(i + 1) * 8 : (i + 4) * 8].astype(BF)
        t_b = jnp.tanh(mm(mix_b, view)).astype(BF)
        t = t_b.astype(F32)
        ids = (64, 66) if i < 0 else (65, 67) if i >= 32 else (i, 32 + i)
        g0 = proj_b[ids[0] : ids[0] + 1]
        g1 = proj_b[ids[1] : ids[1] + 1]
        grad = out_cols[:, 0:1] * g0 + out_cols[:, 1:2] * g1
        gz = (grad * (1.0 - t * t)).astype(BF)
        tap = mm(mix_b, gz, 0, 0)
        for a in range(3):
            k = i + a - 1
            if 0 <= k < 32:
                piece = tap[a * 8 : a * 8 + 8]
                taps[k] = piece if taps[k] is None else taps[k] + piece
        if 0 <= i < 32:
            g8 = jnp.concatenate([g0[:, :256], g1[:, :256], jnp.zeros((6, 256), F32)], axis=0).astype(BF)
            left = jnp.concatenate([view[:, :256], g8], axis=0)
            right = jnp.concatenate([gz[:, :256], t_b[:, :256]], axis=0)
            sums = sums + mm(left, right, 1, 1)
    tail = sums[24:32, 64:]
    row = lax.broadcasted_iota(jnp.int32, (8, 64), 0)
    lane = lax.broadcasted_iota(jnp.int32, (8, 64), 1)
    for s in range(2):
        for v in range(2):
            prod = proj_b[32 * s : 32 * s + 32, :256] * center[32 * v : 32 * v + 32]
            total = jnp.sum(jnp.sum(prod, axis=0, keepdims=True), axis=1, keepdims=True)
            tail = jnp.where((row == 2) & (lane == 2 * s + v), total, tail)
    packed = jnp.concatenate(
        [
            jnp.concatenate([sums[0:8, :64], sums[8:16, :64]], axis=1),
            jnp.concatenate([sums[16:24, :64], tail], axis=1),
        ],
        axis=0,
    )
    return jnp.concatenate(taps[:32], axis=0), packed


def call(body, out_shapes, *args):
    single = not isinstance(out_shapes, (tuple, list))

    def kernel(*refs):
        ins = [ref[...] for ref in refs[: len(args)]]
        outs = body(*ins)
        for ref, value in zip(refs[len(args) :], [outs] if single else outs):
            ref[...] = value

    return pl.pallas_call(
        kernel,
        out_shape=out_shapes,
        compiler_params=pltpu.CompilerParams(vmem_limit_bytes=40 * 1024 * 1024),
    )(*args)


def sds(shape, dtype):
    return jax.ShapeDtypeStruct(shape, dtype)


def everyone(value, axis, count):
    spread = jnp.broadcast_to(value[None], (count,) + value.shape)
    return lax.all_to_all(spread, axis, split_axis=0, concat_axis=0)


def prepare(velocity, cotangent):
    vel = velocity.astype(BF)
    edges = jnp.concatenate([vel[:, :, 0:2], vel[:, :, 254:256]], axis=2).reshape(1, 256)
    return jnp.concatenate(
        [cotangent.astype(BF).reshape(64, 256), edges, jnp.zeros((15, 256), BF)], axis=0
    )


def turns(own, cols):
    ang = TWO_PI / NY * (own * cols % NY).astype(F32)
    return jnp.stack([jnp.cos(ang), jnp.sin(ang)])


def wide(got, velocity, h):
    left = lax.dynamic_index_in_dim(got, (h + 15) % 16, 0, False)[64].reshape(2, 32, 4)
    right = lax.dynamic_index_in_dim(got, (h + 1) % 16, 0, False)[64].reshape(2, 32, 4)
    return jnp.concatenate([left[:, :, 2:4], velocity.astype(BF), right[:, :, 0:2]], axis=2)


def second_send(spec, vel_y, w):
    first, last = vel_y[:, :2], vel_y[:, 30:]

    def rows(v):
        v = v.reshape(4, 260)
        corner = jnp.concatenate([v[:, :2], v[:, 258:]], axis=1).reshape(1, 16)
        return jnp.concatenate(
            [v[:, 2:258], jnp.pad(corner, ((0, 0), (0, 240))), jnp.zeros((1, 256), BF)], axis=0
        )

    dest = jnp.arange(WA)[:, None, None]
    rims = jnp.where(dest == (w + 1) % WA, rows(last)[None], rows(first)[None])
    return jnp.concatenate([spec.reshape(32, 2, 256), rims], axis=1)


def velocity_planes(got2, vel_y, w):
    def rows(src):
        v = lax.dynamic_index_in_dim(got2, src, 0, False)[2:7]
        corner = v[4, :16].reshape(4, 4)
        v = jnp.concatenate([corner[:, :2], v[:4], corner[:, 2:]], axis=1)
        return v.reshape(2, 2, 260)

    full = jnp.concatenate([rows((w + 31) % WA), vel_y, rows((w + 1) % WA)], axis=1)
    moved = []
    for s in range(2):
        for b in (-1, 0, 1):
            v = full[s]
            moved.append(
                jnp.concatenate(
                    [v[:, 2 + b : 258 + b], v[:, 1 + b : 2 + b], v[:, 258 + b : 259 + b], jnp.zeros((36, 126), BF)],
                    axis=1,
                )
            )
    moved += [jnp.zeros((36, 384), BF)] * 2
    return jnp.stack(moved, axis=1).reshape(288, 384).astype(F32)


def lift_matrix(lift, kernels):
    parts = []
    for a in range(3):
        for s in range(2):
            for b in range(3):
                parts.append(kernels[:, 3 * a + b] * lift[:, s])
        parts += [jnp.zeros_like(parts[0])] * 2
    return jnp.stack(parts, axis=1)


def finish_velocity(proj, taps, lift, out_w):
    hi = lax.Precision.HIGHEST
    main = proj[:64, :256].reshape(2, 32, 256)
    main_b = main.astype(BF).astype(F32)
    m2 = jnp.dot(lift.T, out_w.astype(F32).T, precision=hi)
    taps = taps.reshape(32, 8, 384)
    out = []
    for s in range(2):
        left, mid, right = taps[:, 3 * s], taps[:, 3 * s + 1], taps[:, 3 * s + 2]
        value = main[s] + m2[s, 0] * main_b[0] + m2[s, 1] * main_b[1] + mid[:, :256]
        value = value + jnp.concatenate([right[:, 256:257], right[:, :255]], axis=1)
        value = value + jnp.concatenate([left[:, 1:256], left[:, 257:258]], axis=1)
        out.append(value)
    return jnp.stack(out)


def finish_weights(total, lift, kernels, point, out_w, lift18):
    hi = lax.Precision.HIGHEST
    scale = 1.0 / math.sqrt(NX * NY)
    total = total * scale
    q = jnp.concatenate([total[:8, :64], total[:8, 64:], total[8:, :64]], axis=0)
    gpt = total[8:10, 64:]
    gpv = total[10, 64:68].reshape(2, 2)
    grad_out = gpt + jnp.dot(gpv, lift.T, precision=hi)
    grad_point = jnp.einsum("ko,ck->oc", q, lift18, precision=hi)
    gv = jnp.einsum("ko,oc->ck", q, point.astype(F32), precision=hi)
    gv = gv.reshape(64, 3, 8)[:, :, :6].reshape(64, 3, 2, 3)
    grad_kernels = jnp.sum(gv * lift[:, None, :, None], axis=2).reshape(64, 9)
    grad_lift = jnp.sum(gv * kernels.reshape(64, 3, 1, 3), axis=(1, 3))
    grad_lift = grad_lift + jnp.dot(out_w.astype(F32).T, gpv, precision=hi)
    return grad_lift, grad_kernels[None], grad_point[None], grad_out


def local(velocity, cotangent, lift_weight, depth_kernels, point_weights, out_weight):
    tab = make_tables()
    h = lax.axis_index("ha")
    w = lax.axis_index("wa")
    kernels = depth_kernels[0]
    point = point_weights[0]
    col = jnp.arange(256)[None, :]
    peer = jnp.arange(HA)[:, None]
    turn1 = turns(h, col + 256 * peer)
    sign = jnp.where(h == 0, (1 - 2 * (col % 2)).astype(F32), 0.0)
    ky_lane = (h + 16 * (4 * w + jnp.arange(128) // 32)).astype(F32)[None, :]
    cols4 = jnp.asarray(np.concatenate([COL_ID, np.zeros(126, np.int64)]).astype(np.int32))[None, :]
    turn4 = turns(peer, cols4 + 256 * h + NY)
    lift18 = lift_matrix(lift_weight, kernels)

    got1 = everyone(prepare(velocity, cotangent), "ha", HA)
    spec = call(y_forward, sds((64, 256), BF), got1, turn1, sign, tab["t1"])
    vel_y = wide(got1, velocity, h)
    got2 = lax.all_to_all(second_send(spec, vel_y, w), "wa", split_axis=0, concat_axis=0)
    lines = got2[:, :2].reshape(64, 256)
    sent3 = call(
        x_project, sds((64, 384), BF), lines, ky_lane, tab["d1"], tab["tw1"], tab["kr"], tab["ik"], tab["tw2"], tab["d2"]
    )
    got3 = lax.all_to_all(sent3.reshape(32, 2, 384), "wa", split_axis=0, concat_axis=0)
    planes = velocity_planes(got2, vel_y, w)
    sent4 = call(regroup, sds((80, 256), BF), got3.reshape(64, 384))
    got4 = everyone(sent4, "ha", HA)

    def last(got, turn, tk, planes, center, point, lift18, out_cols):
        proj = y_inverse(got, turn, tk)
        taps, packed = network(proj, planes, center, point, lift18, out_cols)
        return proj, taps, packed

    proj, taps, packed = call(
        last,
        (sds((80, 384), F32), sds((256, 384), F32), sds((16, 128), F32)),
        got4, turn4, tab["tk"], planes, velocity.reshape(64, 256), point.astype(F32), lift18, out_weight.astype(F32).T,
    )
    part = jnp.sum(everyone(packed, "ha", HA), axis=0)
    total = jnp.sum(everyone(part, "wa", WA), axis=0)
    grad_velocity = finish_velocity(proj, taps, lift_weight, out_weight)
    return (grad_velocity,) + finish_weights(total, lift_weight, kernels, point, out_weight, lift18)


def solution(mesh):
    return jax.shard_map(
        local,
        mesh=mesh,
        in_specs=(P(None, "wa", "ha"), P(None, "wa", "ha"), P(), P(), P(), P()),
        out_specs=(P(None, "wa", "ha"), P(), P(), P(), P()),
        check_vma=False,
    )
```

profile of v0, /device:TPU:8, one launch (start us, length us, event | category | flops | bytes accessed | tf_op | source)
XLA Modules:
  0.0 147.5 jit_solution(15281066625177886470)
XLA Ops:
  0.6 0.8 convert_element_type.78
  1.5 0.1 fusion.42
  1.6 0.1 pad_maximum_fusion.4
  1.6 0.1 reshape.414
  1.8 0.6 copy-done.10
  2.4 0.1 maximum_maximum_fusion.1
  2.5 0.9 broadcast_in_dim.41
  3.4 9.3 %all-to-all-start = ((bf16[16,80,256]{2,1,0:T(8,128)(2,1)}), bf16[16,80,256]{2,1,0:T(8,128)(2,1)S(1)}, u32[]{:S(2)}, u32[]{:S(2)}) async-start(bf16[16,80,256]{2,1,0:T(8,128)(2,1)} %broadcast_in_dim.41), calls=%async_computation | async-start | bytes 1310720 | tf_op jit(solution)/shard_map/all_to_all | solution.py:267
  12.9 0.2 fusion.22
  13.1 0.1 fusion.54
  13.2 0.6 fusion.51
  13.8 0.1 fusion.20
  14.0 14.2 %all-to-all-done.refs_0_ = bf16[16,80,256]{2,1,0:T(8,128)(2,1)S(1)} async-done(((bf16[16,80,256]{2,1,0:T(8,128)(2,1)}), bf16[16,80,256]{2,1,0:T(8,128)(2,1)S(1)}, u32[]{:S(2)}, u32[]{:S(2)}) %all-to-all-start) | async-done | bytes 655392 | tf_op jit(solution)/shard_map/all_to_all | solution.py:267
  28.2 0.1 reshape_squeeze.16
  28.3 0.1 slice.402
  28.4 0.1 reshape_squeeze.17
  28.5 0.1 pad_maximum_fusion.10
  28.8 0.1 fusion.50
  29.0 0.1 reshape.419
  29.2 0.1 reshape.417
  29.3 0.6 shard_map.182
  30.0 0.1 broadcast_select_fusion
  30.2 0.7 pad_maximum_fusion
  30.9 13.2 %all-to-all-start.1 = ((bf16[32,8,256]{2,1,0:T(8,128)(2,1)}), bf16[32,8,256]{2,1,0:T(8,128)(2,1)S(1)}, u32[]{:S(2)}, u32[]{:S(2)}) async-start(bf16[32,8,256]{2,1,0:T(8,128)(2,1)} %pad_maximum_fusion), calls=%async_computation.1 | async-start | bytes 262144 | tf_op jit(solution)/shard_map/all_to_all | solution.py:387
  44.1 0.1 copy.233
  44.3 0.1 pad.45.clone
  44.4 0.1 copy.234.refs_6_
  44.6 13.7 %all-to-all-done.1 = bf16[32,8,256]{2,1,0:T(8,128)(2,1)S(1)} async-done(((bf16[32,8,256]{2,1,0:T(8,128)(2,1)}), bf16[32,8,256]{2,1,0:T(8,128)(2,1)S(1)}, u32[]{:S(2)}, u32[]{:S(2)}) %all-to-all-start.1) | async-done | bytes 131104 | tf_op jit(solution)/shard_map/all_to_all | solution.py:387
  58.4 0.1 reshape_squeeze.18
  58.5 0.1 reshape_squeeze.19
  58.8 0.7 copy-done.5
  59.6 0.9 shard_map.183
  60.5 0.6 reshape.421
  61.2 3.9 %all-to-all-start.2 = ((bf16[32,2,384]{2,1,0:T(2,128)(2,1)}), bf16[32,2,384]{2,1,0:T(2,128)(2,1)S(1)}, u32[]{:S(2)}, u32[]{:S(2)}) async-start(bf16[32,2,384]{2,1,0:T(2,128)(2,1)} %reshape.421), calls=%async_computation.2 | async-start | bytes 98304 | tf_op jit(solution)/shard_map/all_to_all | solution.py:392
  65.0 0.1 maximum_maximum_fusion
  65.2 12.3 %all-to-all-done.2 = bf16[32,2,384]{2,1,0:T(2,128)(2,1)S(1)} async-done(((bf16[32,2,384]{2,1,0:T(2,128)(2,1)}), bf16[32,2,384]{2,1,0:T(2,128)(2,1)S(1)}, u32[]{:S(2)}, u32[]{:S(2)}) %all-to-all-start.2) | async-done | bytes 49184 | tf_op jit(solution)/shard_map/all_to_all | solution.py:392
  77.5 0.3 shard_map.184
  77.8 0.9 broadcast_in_dim.72
  78.7 5.0 %all-to-all-start.3 = ((bf16[16,80,256]{2,1,0:T(8,128)(2,1)}), bf16[16,80,256]{2,1,0:T(8,128)(2,1)S(1)}, u32[]{:S(2)}, u32[]{:S(2)}) async-start(bf16[16,80,256]{2,1,0:T(8,128)(2,1)} %broadcast_in_dim.72), calls=%async_computation.3 | async-start | bytes 1310720 | tf_op jit(solution)/shard_map/all_to_all | solution.py:267
  83.6 0.1 fusion.44
  83.7 0.1 fusion.46
  83.8 0.1 fusion.43
  83.9 0.1 fusion.45
  84.0 0.1 maximum_bitcast_fusion.5
  84.5 0.7 stack.73
  85.2 15.2 %all-to-all-done.3.refs_0_ = bf16[16,80,256]{2,1,0:T(8,128)(2,1)S(1)} async-done(((bf16[16,80,256]{2,1,0:T(8,128)(2,1)}), bf16[16,80,256]{2,1,0:T(8,128)(2,1)S(1)}, u32[]{:S(2)}, u32[]{:S(2)}) %all-to-all-start.3) | async-done | bytes 655392 | tf_op jit(solution)/shard_map/all_to_all | solution.py:267
  100.5 7.7 %shard_map.185 = (f32[80,384]{1,0:T(8,128)S(1)}, f32[256,384]{1,0:T(8,128)S(1)}, f32[16,128]{1,0:T(8,128)S(1)}) custom-call(bf16[16,80,256]{2,1,0:T(8,128)(2,1)S(1)} %all-to-all-done.3.refs_0_, f32[2,16,384]{2,1,0:T(8,128)S(1)} %pad_maximum_fusion.2.refs_1_, bf16[2,256,768]{2,1,0:T(8,128)(2,1)S(1)} %copy-done, f32[288,384]{1,0:T(8,128)S(1)} %bitcast_convert_fusion.refs_3_, ...), custom_call_target="tpu_custom_call" | custom-call | tf_op jit(solution)/shard_map/pallas_call | solution.py:254
  108.1 0.7 broadcast_in_dim.73
  108.8 6.1 %all-to-all-start.4 = ((f32[16,16,128]{2,1,0:T(8,128)}), f32[16,16,128]{2,1,0:T(8,128)S(1)}, u32[]{:S(2)}, u32[]{:S(2)}) async-start(f32[16,16,128]{2,1,0:T(8,128)} %broadcast_in_dim.73), calls=%async_computation.4 | async-start | bytes 262144 | tf_op jit(solution)/shard_map/all_to_all | solution.py:267
  114.9 0.2 fusion.41
  115.5 6.7 %all-to-all-done.4 = f32[16,16,128]{2,1,0:T(8,128)S(1)} async-done(((f32[16,16,128]{2,1,0:T(8,128)}), f32[16,16,128]{2,1,0:T(8,128)S(1)}, u32[]{:S(2)}, u32[]{:S(2)}) %all-to-all-start.4) | async-done | bytes 131104 | tf_op jit(solution)/shard_map/all_to_all | solution.py:267
  122.3 0.7 broadcast_in_dim.74
  123.0 3.9 %all-to-all-start.5 = ((f32[32,16,128]{2,1,0:T(8,128)}), f32[32,16,128]{2,1,0:T(8,128)S(1)}, u32[]{:S(2)}, u32[]{:S(2)}) async-start(f32[32,16,128]{2,1,0:T(8,128)} %broadcast_in_dim.74), calls=%async_computation.5 | async-start | bytes 524288 | tf_op jit(solution)/shard_map/all_to_all | solution.py:267
  126.9 1.4 fusion.7
  128.3 1.4 fusion.4
  129.6 0.6 pad_maximum_fusion.1
  130.3 13.8 %all-to-all-done.5 = f32[32,16,128]{2,1,0:T(8,128)S(1)} async-done(((f32[32,16,128]{2,1,0:T(8,128)}), f32[32,16,128]{2,1,0:T(8,128)S(1)}, u32[]{:S(2)}, u32[]{:S(2)}) %all-to-all-start.5) | async-done | bytes 262176 | tf_op jit(solution)/shard_map/all_to_all | solution.py:267
  144.2 0.1 slice_reduce_fusion
  144.3 0.9 convolution_bitcast_fusion
  145.2 0.1 convolution_bitcast_fusion.1
  145.3 0.1 reshape_squeeze.20
  145.4 0.7 convolution_add_fusion
  146.1 0.6 broadcast_in_dim_reshape.4
  146.8 0.8 fusion
  (102 shorter events, 2.1 us)
Async XLA Ops:
  1.5 0.8 copy-start.10
  3.4 9.7 %copy-start.11 = (f32[1,64,9]{1,0,2:T(1,128)S(1)}, f32[1,64,9]{1,0,2:T(1,128)}, u32[]{:S(2)}) copy-start(f32[1,64,9]{1,0,2:T(1,128)} %param.18) | copy-start | bytes 6916
  3.4 9.7 %copy-start.12 = (f32[64,2]{0,1:T(2,128)S(1)}, f32[64,2]{0,1:T(2,128)}, u32[]{:S(2)}) copy-start(f32[64,2]{0,1:T(2,128)} %param.17) | copy-start | bytes 1540
  3.4 9.7 %copy-start.14 = (bf16[2,64]{1,0:T(2,128)(2,1)S(1)}, bf16[2,64]{1,0:T(2,128)(2,1)}, u32[]{:S(2)}) copy-start(bf16[2,64]{1,0:T(2,128)(2,1)} %param.20) | copy-start | bytes 772
  3.4 10.4 %copy-start.13 = (s32[384]{0:T(512)S(1)}, s32[384]{0:T(512)}, u32[]{:S(2)}) copy-start(s32[384]{0:T(512)} %constant.150.clone) | copy-start | bytes 4612
  3.4 24.8 %all-to-all-start = ((bf16[16,80,256]{2,1,0:T(8,128)(2,1)}), bf16[16,80,256]{2,1,0:T(8,128)(2,1)S(1)}, u32[]{:S(2)}, u32[]{:S(2)}) async-start(bf16[16,80,256]{2,1,0:T(8,128)(2,1)} %broadcast_in_dim.41), calls=%async_computation | async-start | bytes 1310720 | tf_op jit(solution)/shard_map/all_to_all | solution.py:267
  12.7 16.5 %copy-start.2 = (bf16[2,256,512]{2,1,0:T(8,128)(2,1)S(1)}, bf16[2,256,512]{2,1,0:T(8,128)(2,1)}, u32[]{:S(2)}) copy-start(bf16[2,256,512]{2,1,0:T(8,128)(2,1)} %constant.151.clone.refs_3_) | copy-start | bytes 1572868
  30.0 14.5 %copy-start.9 = (bf16[1,64,64]{2,1,0:T(8,128)(2,1)S(1)}, bf16[1,64,64]{2,1,0:T(8,128)(2,1)}, u32[]{:S(2)}) copy-start(bf16[1,64,64]{2,1,0:T(8,128)(2,1)} %param.19) | copy-start | bytes 24580
  30.1 28.7 %copy-start.1 = (bf16[2,256,512]{2,1,0:T(8,128)(2,1)S(1)}, bf16[2,256,512]{2,1,0:T(8,128)(2,1)}, u32[]{:S(2)}) copy-start(bf16[2,256,512]{2,1,0:T(8,128)(2,1)} %constant.155.clone.refs_5_) | copy-start | bytes 1572868
  30.9 27.9 %copy-start.8 = (bf16[2,64,64]{2,1,0:T(8,128)(2,1)S(1)}, bf16[2,64,64]{2,1,0:T(8,128)(2,1)}, u32[]{:S(2)}) copy-start(bf16[2,64,64]{2,1,0:T(8,128)(2,1)} %constant.157.clone.refs_7_) | copy-start | bytes 49156
  30.9 27.5 %all-to-all-start.1 = ((bf16[32,8,256]{2,1,0:T(8,128)(2,1)}), bf16[32,8,256]{2,1,0:T(8,128)(2,1)S(1)}, u32[]{:S(2)}, u32[]{:S(2)}) async-start(bf16[32,8,256]{2,1,0:T(8,128)(2,1)} %pad_maximum_fusion), calls=%async_computation.1 | async-start | bytes 262144 | tf_op jit(solution)/shard_map/all_to_all | solution.py:387
  44.1 14.7 %copy-start.4 = (bf16[2,256,256]{2,1,0:T(8,128)(2,1)S(1)}, bf16[2,256,256]{2,1,0:T(8,128)(2,1)}, u32[]{:S(2)}) copy-start(bf16[2,256,256]{2,1,0:T(8,128)(2,1)} %constant.154.clone.refs_4_) | copy-start | bytes 786436
  44.5 14.3 %copy-start.7 = (f32[2,32,256]{2,1,0:T(8,128)S(1)}, f32[2,32,256]{2,1,0:T(8,128)}, u32[]{:S(2)}) copy-start(f32[2,32,256]{2,1,0:T(8,128)} %constant.156.clone.refs_6_) | copy-start | bytes 196612
  58.7 0.8 copy-start.5
  58.7 0.9 copy-start.6
  61.2 16.3 %all-to-all-start.2 = ((bf16[32,2,384]{2,1,0:T(2,128)(2,1)}), bf16[32,2,384]{2,1,0:T(2,128)(2,1)S(1)}, u32[]{:S(2)}, u32[]{:S(2)}) async-start(bf16[32,2,384]{2,1,0:T(2,128)(2,1)} %reshape.421), calls=%async_computation.2 | async-start | bytes 98304 | tf_op jit(solution)/shard_map/all_to_all | solution.py:392
  78.7 21.8 %all-to-all-start.3 = ((bf16[16,80,256]{2,1,0:T(8,128)(2,1)}), bf16[16,80,256]{2,1,0:T(8,128)(2,1)S(1)}, u32[]{:S(2)}, u32[]{:S(2)}) async-start(bf16[16,80,256]{2,1,0:T(8,128)(2,1)} %broadcast_in_dim.72), calls=%async_computation.3 | async-start | bytes 1310720 | tf_op jit(solution)/shard_map/all_to_all | solution.py:267
  84.3 16.2 %copy-start = (bf16[2,256,768]{2,1,0:T(8,128)(2,1)S(1)}, bf16[2,256,768]{2,1,0:T(8,128)(2,1)}, u32[]{:S(2)}) copy-start(bf16[2,256,768]{2,1,0:T(8,128)(2,1)} %constant.158.clone.refs_2_) | copy-start | bytes 2359300
  85.2 15.3 %copy-start.3 = (f32[2,32,256]{2,1,0:T(8,128)S(1)}, f32[2,32,256]{2,1,0:T(8,128)}, u32[]{:S(2)}) copy-start(f32[2,32,256]{2,1,0:T(8,128)} %param.15) | copy-start | bytes 196612
  108.8 13.4 %all-to-all-start.4 = ((f32[16,16,128]{2,1,0:T(8,128)}), f32[16,16,128]{2,1,0:T(8,128)S(1)}, u32[]{:S(2)}, u32[]{:S(2)}) async-start(f32[16,16,128]{2,1,0:T(8,128)} %broadcast_in_dim.73), calls=%async_computation.4 | async-start | bytes 262144 | tf_op jit(solution)/shard_map/all_to_all | solution.py:267
  123.0 21.1 %all-to-all-start.5 = ((f32[32,16,128]{2,1,0:T(8,128)}), f32[32,16,128]{2,1,0:T(8,128)S(1)}, u32[]{:S(2)}, u32[]{:S(2)}) async-start(f32[32,16,128]{2,1,0:T(8,128)} %broadcast_in_dim.74), calls=%async_computation.5 | async-start | bytes 524288 | tf_op jit(solution)/shard_map/all_to_all | solution.py:267
where the time goes:
time: 148 us
  waiting for transfers between devices  76 us (51%)
  starting transfers between devices  41.3 us (28%)
  local copies, waits for them, and re-layouts  10.6 us (7%)
  Pallas kernels  9.53 us (6%)
  other arithmetic  6.27 us (4%)
  matrix products  2.56 us (2%)
    all_to_all x4, waiting for transfers between devices, everyone(): return lax.all_to_all(spread, axis, split_axis=0, concat_axis=0)  50 us
    all_to_all x4, starting transfers between devices, everyone(): return lax.all_to_all(spread, axis, split_axis=0, concat_axis=0)  24.2 us
    all_to_all x1, waiting for transfers between devices, local(): lax.all_to_all(second_send(spec, vel_y, w), 'wa', split_axis=0, concat_ax...  13.7 us
    all_to_all x1, starting transfers between devices, local(): lax.all_to_all(second_send(spec, vel_y, w), 'wa', split_axis=0, concat_ax...  13.2 us
    all_to_all x1, waiting for transfers between devices, local(): lax.all_to_all(sent3.reshape(32, 2, 384), 'wa', split_axis=0, concat_axis=0)  12.3 us
    pallas_call x4, Pallas kernels, call(): pl.pallas_call(kernel, out_shape=out_shapes, compiler_params=pltpu.Compil...  9.53 us
    all_to_all x1, starting transfers between devices, local(): lax.all_to_all(sent3.reshape(32, 2, 384), 'wa', split_axis=0, concat_axis=0)  3.86 us
    another operation x3, other arithmetic, finish_velocity(): return jnp.stack(out)  3.39 us
  transfers between devices with their start and end apart: 6, of which 6 were waited for; matrix products, arithmetic and copies ran while one was open for 5% of the time, Pallas kernels for 0%

commit v1 on v0

--- a/solution.py
+++ b/solution.py
@@ -12,6 +12,10 @@
 BF = jnp.bfloat16
 F32 = jnp.float32
 HA, WA = 16, 32
+AXES = ("x", "yl", "yh", "z", "c")
+SIZES = (4, 4, 2, 8, 2)
+IN_H = ("x", "yl")
+IN_W = ("yh", "z", "c")
 ROWS, COLS = 32, 256
 NX, NY = WA * ROWS, HA * COLS
 TWO_PI = 2.0 * math.pi
@@ -81,7 +85,7 @@
     tk[:, 0, 1, :258] = 2 * np.sin(ang)
     tk[:, 1, 1, :258] = 2 * np.cos(ang)
     tk = tk.reshape(32, 4, 2, 768).transpose(1, 0, 2, 3).reshape(256, 768)
-    return dict(t1=pair(t1), d1=pair(d1), tw1=tw1, kr=pair(kr), ik=pair(ik), tw2=tw2, d2=pair(d2), tk=pair(tk))
+    return dict(t1=pair(t1), d1=pair(d1), tw1=tw1, kr=pair(kr), ik=pair(ik), tw2=tw2, d2=pair(d2), tk=bf(tk))
 
 
 def mm(a, b, ca=1, cb=0):
@@ -98,27 +102,28 @@
 
 
 def y_forward(got, turn, sign, t1):
-    re = jnp.zeros((64, 256), F32)
-    im = jnp.zeros((64, 256), F32)
-    for q in range(HA):
-        part = got[q, :64].astype(F32)
-        re = re + part * turn[0, q : q + 1]
-        im = im - part * turn[1, q : q + 1]
-    both = halves(jnp.concatenate([re, im], axis=1))
+    parts = [got[q, :64].astype(F32) for q in range(4)]
     row = lax.broadcasted_iota(jnp.int32, (64, 256), 0)
     pick = jnp.where(row == 1, sign, 0.0).astype(BF)
-    out = []
-    for j in range(4):
-        block = mm3((t1[0, j * 64 : (j + 1) * 64], t1[1, j * 64 : (j + 1) * 64]), both, 1, 1)
-        if j == 0:
-            block = block + mm(pick, both[0][:, :256], 1, 1) + mm(pick, both[1][:, :256], 1, 1)
-        out.append(block)
-    pieces = [out[j][:, 32 * c : 32 * c + 32] for c in range(2) for j in range(4)]
-    return jnp.concatenate(pieces, axis=1).astype(BF)
+    result = []
+    for e in range(4):
+        re = sum(parts[q] * turn[0, 4 * e + q : 4 * e + q + 1] for q in range(4))
+        im = -sum(parts[q] * turn[1, 4 * e + q : 4 * e + q + 1] for q in range(4))
+        both = halves(jnp.concatenate([re, im], axis=1))
+        out = []
+        for j in range(4):
+            block = mm3((t1[0, j * 64 : (j + 1) * 64], t1[1, j * 64 : (j + 1) * 64]), both, 1, 1)
+            if e == 0 and j == 0:
+                block = block + mm(pick, both[0][:, :256], 1, 1) + mm(pick, both[1][:, :256], 1, 1)
+            out.append(block)
+        pieces = [out[j][:, 32 * c : 32 * c + 32] for c in range(2) for j in range(4)]
+        result.append(jnp.concatenate(pieces, axis=1).astype(BF))
+    return jnp.concatenate(result, axis=0)
 
 
 def x_project(lines, ky_lane, d1, tw1, kr, ik, tw2, d2):
-    first = mm(d1[0], lines) + mm(d1[1], lines)
+    lines = lines.astype(F32)
+    first = mm3(d1, halves((lines[0] + lines[1]) + (lines[2] + lines[3])))
     cs, sn = tw1[0], tw1[1]
     turned = []
     for c in range(2):
@@ -183,37 +188,46 @@
         [jnp.concatenate([turned[256 + 8 * c + 2 * j : 258 + 8 * c + 2 * j] for j in range(4)], axis=1) for c in range(2)],
         axis=0,
     )
-    return jnp.concatenate([main, rim, jnp.zeros((12, 256), F32)], axis=0).astype(BF)
-
-
-def y_inverse(got, turn, tk):
+    return jnp.concatenate([main, rim, jnp.zeros((4, 256), F32)], axis=0).astype(BF)
+
+
+def y_inverse(got, turn, zero, tk):
     lane = lax.broadcasted_iota(jnp.int32, (1, 384), 1)
     odd = jnp.where(lane < 256, lane % 2, (lane == 256).astype(jnp.int32)).astype(F32)
-    own = got[0].astype(F32)
-    acc = own[:, 1:2] * (1.0 - 2.0 * odd) - own[:, 0:1]
-    acc = acc + mm(got[0], tk[0, :, :384]) + mm(got[0], tk[1, :, :384])
-    for q in range(1, HA):
-        part = mm(got[q], tk[0]) + mm(got[q], tk[1])
-        acc = acc + part[:, :384] * turn[0, q : q + 1] - part[:, 384:] * turn[1, q : q + 1]
-    return acc
+    acc = [None] * 4
+    for e in range(4):
+        lines = regroup(got[e])
+        part = mm(lines, tk)
+        re, im = part[:, :384], part[:, 384:]
+        if e == 0:
+            own = lines.astype(F32)
+            once = zero * (own[:, 1:2] * (1.0 - 2.0 * odd) - own[:, 0:1])
+        for d in range(4):
+            i = 4 * e + d
+            piece = re * turn[0, i : i + 1] - im * turn[1, i : i + 1]
+            acc[d] = piece + once if e == 0 else acc[d] + piece
+    return jnp.concatenate(acc, axis=0).astype(BF)
 
 
 def network(proj, planes, center, point, lift18, out_cols):
     mix = lax.dot_general(point, lift18, (((1,), (0,)), ((), ())), precision=lax.Precision.HIGHEST, preferred_element_type=F32)
-    mix_b = mix.astype(BF)
+    mix_hi, mix_lo = halves(mix)
+    mix3 = jnp.concatenate([mix_hi, mix_lo, mix_hi], axis=1)
+    mix2 = mix3[:, :48]
     proj_b = proj.astype(BF).astype(F32)
     taps = [None] * 34
-    sums = jnp.zeros((32, 128), F32)
+    sums = jnp.zeros((56, 128), F32)
     for i in range(-1, 33):
-        view = planes[(i + 1) * 8 : (i + 4) * 8].astype(BF)
-        t_b = jnp.tanh(mm(mix_b, view)).astype(BF)
+        view, view_lo = halves(planes[(i + 1) * 8 : (i + 4) * 8])
+        t_b = jnp.tanh(mm(mix3, jnp.concatenate([view, view, view_lo], axis=0))).astype(BF)
         t = t_b.astype(F32)
         ids = (64, 66) if i < 0 else (65, 67) if i >= 32 else (i, 32 + i)
         g0 = proj_b[ids[0] : ids[0] + 1]
         g1 = proj_b[ids[1] : ids[1] + 1]
         grad = out_cols[:, 0:1] * g0 + out_cols[:, 1:2] * g1
         gz = (grad * (1.0 - t * t)).astype(BF)
-        tap = mm(mix_b, gz, 0, 0)
+        tap = mm(mix2, gz, 0, 0)
+        tap = tap[:24] + tap[24:]
         for a in range(3):
             k = i + a - 1
             if 0 <= k < 32:
@@ -221,10 +235,11 @@
                 taps[k] = piece if taps[k] is None else taps[k] + piece
         if 0 <= i < 32:
             g8 = jnp.concatenate([g0[:, :256], g1[:, :256], jnp.zeros((6, 256), F32)], axis=0).astype(BF)
-            left = jnp.concatenate([view[:, :256], g8], axis=0)
+            left = jnp.concatenate([view[:, :256], view_lo[:, :256], g8], axis=0)
             right = jnp.concatenate([gz[:, :256], t_b[:, :256]], axis=0)
             sums = sums + mm(left, right, 1, 1)
-    tail = sums[24:32, 64:]
+    tail = sums[48:56, 64:]
+    sums = sums[:24] + sums[24:48]
     row = lax.broadcasted_iota(jnp.int32, (8, 64), 0)
     lane = lax.broadcasted_iota(jnp.int32, (8, 64), 1)
     for s in range(2):
@@ -262,16 +277,19 @@
     return jax.ShapeDtypeStruct(shape, dtype)
 
 
-def everyone(value, axis, count):
-    spread = jnp.broadcast_to(value[None], (count,) + value.shape)
-    return lax.all_to_all(spread, axis, split_axis=0, concat_axis=0)
-
-
-def prepare(velocity, cotangent):
-    vel = velocity.astype(BF)
+def exchange(value, axes):
+    return lax.all_to_all(value, axes, split_axis=0, concat_axis=0)
+
+
+def everyone(value, axes):
+    count = math.prod(SIZES[AXES.index(a)] for a in axes)
+    return exchange(jnp.broadcast_to(value[None], (count,) + value.shape), axes)
+
+
+def prepare(vel, cotangent):
     edges = jnp.concatenate([vel[:, :, 0:2], vel[:, :, 254:256]], axis=2).reshape(1, 256)
     return jnp.concatenate(
-        [cotangent.astype(BF).reshape(64, 256), edges, jnp.zeros((15, 256), BF)], axis=0
+        [cotangent.astype(BF).reshape(64, 256), edges, jnp.zeros((7, 256), BF)], axis=0
     )
 
 
@@ -280,47 +298,46 @@
     return jnp.stack([jnp.cos(ang), jnp.sin(ang)])
 
 
-def wide(got, velocity, h):
-    left = lax.dynamic_index_in_dim(got, (h + 15) % 16, 0, False)[64].reshape(2, 32, 4)
-    right = lax.dynamic_index_in_dim(got, (h + 1) % 16, 0, False)[64].reshape(2, 32, 4)
-    return jnp.concatenate([left[:, :, 2:4], velocity.astype(BF), right[:, :, 0:2]], axis=2)
-
-
-def second_send(spec, vel_y, w):
-    first, last = vel_y[:, :2], vel_y[:, 30:]
-
-    def rows(v):
-        v = v.reshape(4, 260)
-        corner = jnp.concatenate([v[:, :2], v[:, 258:]], axis=1).reshape(1, 16)
-        return jnp.concatenate(
-            [v[:, 2:258], jnp.pad(corner, ((0, 0), (0, 240))), jnp.zeros((1, 256), BF)], axis=0
-        )
-
-    dest = jnp.arange(WA)[:, None, None]
-    rims = jnp.where(dest == (w + 1) % WA, rows(last)[None], rows(first)[None])
-    return jnp.concatenate([spec.reshape(32, 2, 256), rims], axis=1)
-
-
-def velocity_planes(got2, vel_y, w):
-    def rows(src):
-        v = lax.dynamic_index_in_dim(got2, src, 0, False)[2:7]
-        corner = v[4, :16].reshape(4, 4)
-        v = jnp.concatenate([corner[:, :2], v[:4], corner[:, 2:]], axis=1)
-        return v.reshape(2, 2, 260)
-
-    full = jnp.concatenate([rows((w + 31) % WA), vel_y, rows((w + 1) % WA)], axis=1)
+def rims_to_send(got, vel, x, yl, w):
+    def edges(src):
+        return lax.dynamic_index_in_dim(got, src, 0, False)[64].reshape(2, 32, 4)
+
+    def padded(v):
+        return jnp.pad(v.reshape(2, 64), ((0, 0), (0, 448)))
+
+    up = padded(edges(jnp.where(yl == 3, (x + 3) % 4, x))[:, :, 2:4])
+    down = padded(edges(jnp.where(yl == 0, (x + 1) % 4, x))[:, :, 0:2])
+    first, last = vel[:, :2].reshape(2, 512), vel[:, 30:].reshape(2, 512)
+    to_y = jnp.arange(4)[:, None, None, None]
+    to_w = jnp.arange(WA)[None, :, None, None]
+    rows = jnp.where(to_w == (w + 1) % WA, last, first)
+    return jnp.where(to_y == yl, rows, jnp.where(to_y == (yl + 1) % 4, up, down))
+
+
+def velocity_planes(rims, velocity, yl, w):
+    def piece(from_y, from_w):
+        return lax.dynamic_index_in_dim(rims, (from_y % 4) * WA + from_w % WA, 0, False).astype(F32)
+
+    def side(from_y):
+        above, own, below = (piece(from_y, w + d)[:, :64].reshape(2, 32, 2) for d in (31, 0, 1))
+        return jnp.concatenate([above[:, 30:], own, below[:, :2]], axis=1)
+
+    mid = jnp.concatenate(
+        [piece(yl, w + 31).reshape(2, 2, 256), velocity, piece(yl, w + 1).reshape(2, 2, 256)], axis=1
+    )
+    full = jnp.concatenate([side(yl + 3), mid, side(yl + 1)], axis=2)
     moved = []
     for s in range(2):
         for b in (-1, 0, 1):
             v = full[s]
             moved.append(
                 jnp.concatenate(
-                    [v[:, 2 + b : 258 + b], v[:, 1 + b : 2 + b], v[:, 258 + b : 259 + b], jnp.zeros((36, 126), BF)],
+                    [v[:, 2 + b : 258 + b], v[:, 1 + b : 2 + b], v[:, 258 + b : 259 + b], jnp.zeros((36, 126), F32)],
                     axis=1,
                 )
             )
-    moved += [jnp.zeros((36, 384), BF)] * 2
-    return jnp.stack(moved, axis=1).reshape(288, 384).astype(F32)
+    moved += [jnp.zeros((36, 384), F32)] * 2
+    return jnp.stack(moved, axis=1).reshape(288, 384)
 
 
 def lift_matrix(lift, kernels):
@@ -368,53 +385,59 @@
 
 def local(velocity, cotangent, lift_weight, depth_kernels, point_weights, out_weight):
     tab = make_tables()
-    h = lax.axis_index("ha")
-    w = lax.axis_index("wa")
+    x, yl, yh, z, core = (lax.axis_index(a) for a in AXES)
+    w = 16 * yh + 2 * z + core
     kernels = depth_kernels[0]
     point = point_weights[0]
     col = jnp.arange(256)[None, :]
-    peer = jnp.arange(HA)[:, None]
-    turn1 = turns(h, col + 256 * peer)
-    sign = jnp.where(h == 0, (1 - 2 * (col % 2)).astype(F32), 0.0)
-    ky_lane = (h + 16 * (4 * w + jnp.arange(128) // 32)).astype(F32)[None, :]
+    step = jnp.arange(16)[:, None]
+    klass = x + 4 * (step // 4)
+    turn1 = turns(klass, col + 1024 * (step % 4) + 256 * yl)
+    sign = jnp.where(x == 0, (1 - 2 * (col % 2)).astype(F32), 0.0)
+    zero = jnp.where(x == 0, jnp.ones((1, 384), F32), 0.0)
+    ky_lane = (x + 4 * yl + 16 * (4 * w + jnp.arange(128) // 32)).astype(F32)[None, :]
     cols4 = jnp.asarray(np.concatenate([COL_ID, np.zeros(126, np.int64)]).astype(np.int32))[None, :]
-    turn4 = turns(peer, cols4 + 256 * h + NY)
+    turn4 = turns(klass, cols4 + 1024 * (step % 4) + 256 * yl + NY)
     lift18 = lift_matrix(lift_weight, kernels)
 
-    got1 = everyone(prepare(velocity, cotangent), "ha", HA)
-    spec = call(y_forward, sds((64, 256), BF), got1, turn1, sign, tab["t1"])
-    vel_y = wide(got1, velocity, h)
-    got2 = lax.all_to_all(second_send(spec, vel_y, w), "wa", split_axis=0, concat_axis=0)
-    lines = got2[:, :2].reshape(64, 256)
+    vel = velocity.astype(BF)
+    got1 = everyone(prepare(vel, cotangent), ("x",))
+    spec = call(y_forward, sds((256, 256), BF), got1, turn1, sign, tab["t1"])
+    rims = rims_to_send(got1, vel, x, yl, w).reshape(128, 2, 512)
+    got2 = exchange(jnp.concatenate([spec.reshape(128, 2, 256), rims], axis=2), ("yl",) + IN_W)
     sent3 = call(
-        x_project, sds((64, 384), BF), lines, ky_lane, tab["d1"], tab["tw1"], tab["kr"], tab["ik"], tab["tw2"], tab["d2"]
-    )
-    got3 = lax.all_to_all(sent3.reshape(32, 2, 384), "wa", split_axis=0, concat_axis=0)
-    planes = velocity_planes(got2, vel_y, w)
-    sent4 = call(regroup, sds((80, 256), BF), got3.reshape(64, 384))
-    got4 = everyone(sent4, "ha", HA)
-
-    def last(got, turn, tk, planes, center, point, lift18, out_cols):
-        proj = y_inverse(got, turn, tk)
+        x_project, sds((64, 384), BF), got2[:, :, :256].reshape(4, 64, 256), ky_lane, tab["d1"], tab["tw1"], tab["kr"], tab["ik"], tab["tw2"], tab["d2"]
+    )
+    spread = jnp.broadcast_to(sent3.reshape(1, 32, 2, 384), (4, 32, 2, 384)).reshape(128, 2, 384)
+    got3 = exchange(spread, ("yl",) + IN_W)
+    planes = velocity_planes(got2[:, :, 256:], velocity, yl, w)
+    sent4 = call(y_inverse, sds((288, 384), BF), got3.reshape(4, 64, 384), turn4, zero, tab["tk"])
+    got4 = exchange(sent4.reshape(4, 72, 384), ("x",))
+
+    def last(got, planes, center, point, lift18, out_cols):
+        got = got.astype(F32)
+        proj = (got[0] + got[1]) + (got[2] + got[3])
         taps, packed = network(proj, planes, center, point, lift18, out_cols)
         return proj, taps, packed
 
     proj, taps, packed = call(
         last,
-        (sds((80, 384), F32), sds((256, 384), F32), sds((16, 128), F32)),
-        got4, turn4, tab["tk"], planes, velocity.reshape(64, 256), point.astype(F32), lift18, out_weight.astype(F32).T,
-    )
-    part = jnp.sum(everyone(packed, "ha", HA), axis=0)
-    total = jnp.sum(everyone(part, "wa", WA), axis=0)
+        (sds((72, 384), F32), sds((256, 384), F32), sds((16, 128), F32)),
+        got4, planes, velocity.reshape(64, 256), point.astype(F32), lift18, out_weight.astype(F32).T,
+    )
+    part = jnp.sum(everyone(packed, ("yl", "yh", "c")), axis=0)
+    total = jnp.sum(everyone(part, ("x", "z")), axis=0)
     grad_velocity = finish_velocity(proj, taps, lift_weight, out_weight)
     return (grad_velocity,) + finish_weights(total, lift_weight, kernels, point, out_weight, lift18)
 
 
 def solution(mesh):
+    split = jax.sharding.Mesh(mesh.devices.reshape(SIZES), AXES)
+    field = P(None, IN_W, IN_H)
     return jax.shard_map(
         local,
-        mesh=mesh,
-        in_specs=(P(None, "wa", "ha"), P(None, "wa", "ha"), P(), P(), P(), P()),
-        out_specs=(P(None, "wa", "ha"), P(), P(), P(), P()),
+        mesh=split,
+        in_specs=(field, field, P(), P(), P(), P()),
+        out_specs=(field, P(), P(), P(), P()),
         check_vma=False,
     )

time: 148 us -> 129 us (0.87)
  the two profiles are of different devices: /device:TPU:8 before, /device:TPU:64 now
where the time goes in v1:
time: 129 us
  waiting for transfers between devices  55.3 us (43%)
  starting transfers between devices  39.6 us (31%)
  local copies, waits for them, and re-layouts  13.4 us (10%)
  Pallas kernels  10 us (8%)
  other arithmetic  6.1 us (5%)
  matrix products  2.56 us (2%)
  between operations  1.65 us (1%)
    all_to_all x6, waiting for transfers between devices, exchange(): return lax.all_to_all(value, axes, split_axis=0, concat_axis=0)  55.3 us
    all_to_all x6, starting transfers between devices, exchange(): return lax.all_to_all(value, axes, split_axis=0, concat_axis=0)  39.6 us
    pallas_call x4, Pallas kernels, call(): pl.pallas_call(kernel, out_shape=out_shapes, compiler_params=pltpu.Compil...  10 us
    another operation x3, other arithmetic, finish_velocity(): return jnp.stack(out)  3.39 us
    unnamed x40, local copies, waits for them, and re-layouts  3.33 us
  transfers between devices with their start and end apart: 6, of which 6 were waited for; matrix products, arithmetic and copies ran while one was open for 6% of the time, Pallas kernels for 0%

profile of v1, /device:TPU:64, one launch (start us, length us, event | category | flops | bytes accessed | tf_op | source)
XLA Modules:
  0.0 128.6 jit_solution(15690028008741785540)
XLA Ops:
  0.6 1.0 copy.110
  1.8 0.1 reshape.636
  2.1 0.7 broadcast_in_dim.110
  2.8 4.3 %all-to-all-start = ((bf16[4,72,256]{2,1,0:T(8,128)(2,1)}), bf16[4,72,256]{2,1,0:T(8,128)(2,1)S(1)}, u32[]{:S(2)}, u32[]{:S(2)}) async-start(bf16[4,72,256]{2,1,0:T(8,128)(2,1)} %broadcast_in_dim.110), calls=%async_computation | async-start | bytes 294912 | tf_op jit(solution)/shard_map/all_to_all | solution.py:281
  7.4 0.5 copy-done.11
  8.1 0.1 fusion.52
  8.2 0.1 copy.112
  8.3 0.1 copy.113
  8.8 0.2 fusion.19
  9.2 0.1 broadcast_select_fusion.1
  9.3 3.8 %all-to-all-done.refs_0_ = bf16[4,72,256]{2,1,0:T(8,128)(2,1)S(1)} async-done(((bf16[4,72,256]{2,1,0:T(8,128)(2,1)}), bf16[4,72,256]{2,1,0:T(8,128)(2,1)S(1)}, u32[]{:S(2)}, u32[]{:S(2)}) %all-to-all-start) | async-done | bytes 147488 | tf_op jit(solution)/shard_map/all_to_all | solution.py:281
  13.1 0.1 reshape_squeeze.10
  13.3 0.1 reshape.640
  13.5 0.1 reshape_squeeze.11
  13.6 0.1 reshape.641
  13.7 1.1 shard_map.182
  15.0 0.3 broadcast_select_fusion
  15.3 1.1 pad_maximum_fusion
  16.4 16.6 %all-to-all-start.1 = ((bf16[128,2,768]{2,1,0:T(2,128)(2,1)}), bf16[128,2,768]{2,1,0:T(2,128)(2,1)S(1)}, u32[]{:S(2)}, u32[]{:S(2)}) async-start(bf16[128,2,768]{2,1,0:T(2,128)(2,1)} %pad_maximum_fusion), calls=%async_computation.1 | async-start | bytes 786432 | tf_op jit(solution)/shard_map/all_to_all | solution.py:281
  33.0 0.6 fusion.51
  33.7 0.2 fusion.17
  33.9 0.7 copy-done.9
  34.6 15.3 %all-to-all-done.1 = bf16[128,2,768]{2,1,0:T(2,128)(2,1)S(1)} async-done(((bf16[128,2,768]{2,1,0:T(2,128)(2,1)}), bf16[128,2,768]{2,1,0:T(2,128)(2,1)S(1)}, u32[]{:S(2)}, u32[]{:S(2)}) %all-to-all-start.1) | async-done | bytes 393248 | tf_op jit(solution)/shard_map/all_to_all | solution.py:281
  49.9 0.2 slice.385
  50.1 0.1 reshape.646
  50.2 0.1 copy.114
  50.4 0.1 reshape.648
  50.5 0.1 copy.116
  50.6 0.1 reshape.647
  50.9 0.1 copy.120
  51.0 0.1 reshape.649
  51.2 0.1 copy.117
  51.3 0.1 reshape.651
  51.5 0.1 reshape.650
  51.8 0.1 copy.121
  52.0 0.1 copy-done
  52.1 0.1 pad_maximum_fusion.1
  52.7 0.6 copy-done.2
  53.3 0.2 copy-done.4
  53.5 0.9 shard_map.183
  54.5 0.8 broadcast_in_dim.126
  55.2 6.7 %all-to-all-start.2 = ((bf16[128,2,384]{2,1,0:T(2,128)(2,1)}), bf16[128,2,384]{2,1,0:T(2,128)(2,1)S(1)}, u32[]{:S(2)}, u32[]{:S(2)}) async-start(bf16[128,2,384]{2,1,0:T(2,128)(2,1)} %bitcast.3), calls=%async_computation.2 | async-start | bytes 393216 | tf_op jit(solution)/shard_map/all_to_all | solution.py:281
  62.2 12.9 %all-to-all-done.2 = bf16[128,2,384]{2,1,0:T(2,128)(2,1)S(1)} async-done(((bf16[128,2,384]{2,1,0:T(2,128)(2,1)}), bf16[128,2,384]{2,1,0:T(2,128)(2,1)S(1)}, u32[]{:S(2)}, u32[]{:S(2)}) %all-to-all-start.2) | async-done | bytes 196640 | tf_op jit(solution)/shard_map/all_to_all | solution.py:281
  75.1 1.9 %shard_map.184 = bf16[288,384]{1,0:T(8,128)(2,1)} custom-call(bf16[4,64,384]{2,1,0:T(8,128)(2,1)S(1)} %reshape.644.refs_0_, f32[2,16,384]{2,1,0:T(8,128)S(1)} %pad_maximum_fusion.3.refs_1_, f32[1,384]{1,0:T(1,128)S(1)} %select_n.241.refs_2_, bf16[256,768]{1,0:T(8,128)(2,1)S(1)} %copy-done.3), custom_call_target="tpu_custom_call" | custom-call | tf_op jit(solution)/shard_map/pallas_call | solution.py:269
  77.1 3.6 %all-to-all-start.3 = ((bf16[4,72,384]{2,1,0:T(8,128)(2,1)}), bf16[4,72,384]{2,1,0:T(8,128)(2,1)S(1)}, u32[]{:S(2)}, u32[]{:S(2)}) async-start(bf16[4,72,384]{2,1,0:T(8,128)(2,1)} %bitcast.4), calls=%async_computation.3 | async-start | bytes 442368 | tf_op jit(solution)/shard_map/all_to_all | solution.py:281
  80.7 0.1 maximum_bitcast_fusion.5
  81.2 0.7 stack.73
  81.9 5.4 %all-to-all-done.3.refs_0_ = bf16[4,72,384]{2,1,0:T(8,128)(2,1)S(1)} async-done(((bf16[4,72,384]{2,1,0:T(8,128)(2,1)}), bf16[4,72,384]{2,1,0:T(8,128)(2,1)S(1)}, u32[]{:S(2)}, u32[]{:S(2)}) %all-to-all-start.3) | async-done | bytes 221216 | tf_op jit(solution)/shard_map/all_to_all | solution.py:281
  87.3 6.1 %shard_map.185 = (f32[72,384]{1,0:T(8,128)S(1)}, f32[256,384]{1,0:T(8,128)S(1)}, f32[16,128]{1,0:T(8,128)S(1)}) custom-call(bf16[4,72,384]{2,1,0:T(8,128)(2,1)S(1)} %all-to-all-done.3.refs_0_, f32[288,384]{1,0:T(8,128)S(1)} %bitcast.106, f32[64,256]{1,0:T(8,128)S(1)} %bitcast.107, f32[64,64]{1,0:T(8,128)S(1)} %bitcast_convert_fusion.refs_3_, ...), custom_call_target="tpu_custom_call" | custom-call | tf_op jit(solution)/shard_map/pallas_call | solution.py:269
  93.3 0.7 broadcast_in_dim.127
  94.0 3.5 %all-to-all-start.4 = ((f32[16,16,128]{2,1,0:T(8,128)}), f32[16,16,128]{2,1,0:T(8,128)S(1)}, u32[]{:S(2)}, u32[]{:S(2)}) async-start(f32[16,16,128]{2,1,0:T(8,128)} %broadcast_in_dim.127), calls=%async_computation.4 | async-start | bytes 262144 | tf_op jit(solution)/shard_map/all_to_all | solution.py:281
  97.5 0.2 fusion.42
  98.1 8.1 %all-to-all-done.4 = f32[16,16,128]{2,1,0:T(8,128)S(1)} async-done(((f32[16,16,128]{2,1,0:T(8,128)}), f32[16,16,128]{2,1,0:T(8,128)S(1)}, u32[]{:S(2)}, u32[]{:S(2)}) %all-to-all-start.4) | async-done | bytes 131104 | tf_op jit(solution)/shard_map/all_to_all | solution.py:281
  106.2 0.7 broadcast_in_dim.128
  107.0 4.9 %all-to-all-start.5 = ((f32[32,16,128]{2,1,0:T(8,128)}), f32[32,16,128]{2,1,0:T(8,128)S(1)}, u32[]{:S(2)}, u32[]{:S(2)}) async-start(f32[32,16,128]{2,1,0:T(8,128)} %broadcast_in_dim.128), calls=%async_computation.5 | async-start | bytes 524288 | tf_op jit(solution)/shard_map/all_to_all | solution.py:281
  111.9 1.4 %fusion.7 = f32[1,32,256]{2,1,0:T(8,128)S(1)} fusion(f32[32,384]{1,0:T(8,128)S(1)} %bitcast.119, f32[32,255]{1,0:T(8,128)S(1)} %slice.432, f32[32,1]{1,0:T(8,128)S(1)} %slice.431, f32[32,1]{1,0:T(8,128)S(1)} %slice.435, f32[32,255]{1,0:T(8,128)S(1)} %slice.434, f32[72,384]{1,0:T(8,128)S(1)} %get-tuple-element.8, f32[64,256]{1,0:T(8,128)S(1)} %fusion.1, ...), kind=kLoop, calls=%fused_computation.38 | loop fusion | flops 73728 | bytes 229384 | tf_op jit(solution)/shard_map/stack | solution.py:366
  113.3 1.4 %fusion.4 = f32[1,32,256]{2,1,0:T(8,128)S(1)} fusion(f32[32,384]{1,0:T(8,128)S(1)} %bitcast.118, f32[32,255]{1,0:T(8,128)S(1)} %slice.440, f32[32,1]{1,0:T(8,128)S(1)} %slice.439, f32[32,1]{1,0:T(8,128)S(1)} %slice.443, f32[32,255]{1,0:T(8,128)S(1)} %slice.442, f32[72,384]{1,0:T(8,128)S(1)} %get-tuple-element.8, f32[64,256]{1,0:T(8,128)S(1)} %fusion.1, ...), kind=kLoop, calls=%fused_computation.34 | loop fusion | flops 73728 | bytes 229384 | tf_op jit(solution)/shard_map/stack | solution.py:366
  114.6 0.6 pad_maximum_fusion.2
  115.3 9.9 %all-to-all-done.5 = f32[32,16,128]{2,1,0:T(8,128)S(1)} async-done(((f32[32,16,128]{2,1,0:T(8,128)}), f32[32,16,128]{2,1,0:T(8,128)S(1)}, u32[]{:S(2)}, u32[]{:S(2)}) %all-to-all-start.5) | async-done | bytes 262176 | tf_op jit(solution)/shard_map/all_to_all | solution.py:281
  125.4 0.9 convolution_bitcast_fusion
  126.2 0.1 convolution_bitcast_fusion.1
  126.5 0.7 convolution_add_fusion
  127.2 0.6 broadcast_in_dim_reshape.4
  127.8 0.8 fusion
  (125 shorter events, 3.8 us)
Async XLA Ops:
  0.6 1.3 copy-start.10
  2.8 10.4 %all-to-all-start = ((bf16[4,72,256]{2,1,0:T(8,128)(2,1)}), bf16[4,72,256]{2,1,0:T(8,128)(2,1)S(1)}, u32[]{:S(2)}, u32[]{:S(2)}) async-start(bf16[4,72,256]{2,1,0:T(8,128)(2,1)} %broadcast_in_dim.110), calls=%async_computation | async-start | bytes 294912 | tf_op jit(solution)/shard_map/all_to_all | solution.py:281
  7.2 0.8 copy-start.14
  7.2 0.7 copy-start.12
  7.2 0.7 copy-start.11
  7.2 6.5 %copy-start.1 = (bf16[2,256,512]{2,1,0:T(8,128)(2,1)S(1)}, bf16[2,256,512]{2,1,0:T(8,128)(2,1)}, u32[]{:S(2)}) copy-start(bf16[2,256,512]{2,1,0:T(8,128)(2,1)} %constant.241.clone.refs_3_) | copy-start | bytes 1572868
  16.4 33.5 %all-to-all-start.1 = ((bf16[128,2,768]{2,1,0:T(2,128)(2,1)}), bf16[128,2,768]{2,1,0:T(2,128)(2,1)S(1)}, u32[]{:S(2)}, u32[]{:S(2)}) async-start(bf16[128,2,768]{2,1,0:T(2,128)(2,1)} %pad_maximum_fusion), calls=%async_computation.1 | async-start | bytes 786432 | tf_op jit(solution)/shard_map/all_to_all | solution.py:281
  33.0 0.7 copy-start.13
  33.9 0.7 copy-start.9
  51.3 0.8 copy-start
  52.3 1.0 copy-start.2
  52.5 1.0 copy-start.4
  52.6 0.9 copy-start.5
  52.6 0.9 copy-start.6
  52.6 0.9 copy-start.7
  52.6 0.9 copy-start.8
  55.2 19.8 %all-to-all-start.2 = ((bf16[128,2,384]{2,1,0:T(2,128)(2,1)}), bf16[128,2,384]{2,1,0:T(2,128)(2,1)S(1)}, u32[]{:S(2)}, u32[]{:S(2)}) async-start(bf16[128,2,384]{2,1,0:T(2,128)(2,1)} %bitcast.3), calls=%async_computation.2 | async-start | bytes 393216 | tf_op jit(solution)/shard_map/all_to_all | solution.py:281
  61.9 13.2 %copy-start.3 = (bf16[256,768]{1,0:T(8,128)(2,1)S(1)}, bf16[256,768]{1,0:T(8,128)(2,1)}, u32[]{:S(2)}) copy-start(bf16[256,768]{1,0:T(8,128)(2,1)} %constant.248.clone.refs_3_) | copy-start | bytes 1179652
  77.1 10.2 %all-to-all-start.3 = ((bf16[4,72,384]{2,1,0:T(8,128)(2,1)}), bf16[4,72,384]{2,1,0:T(8,128)(2,1)S(1)}, u32[]{:S(2)}, u32[]{:S(2)}) async-start(bf16[4,72,384]{2,1,0:T(8,128)(2,1)} %bitcast.4), calls=%async_computation.3 | async-start | bytes 442368 | tf_op jit(solution)/shard_map/all_to_all | solution.py:281
  94.0 12.2 %all-to-all-start.4 = ((f32[16,16,128]{2,1,0:T(8,128)}), f32[16,16,128]{2,1,0:T(8,128)S(1)}, u32[]{:S(2)}, u32[]{:S(2)}) async-start(f32[16,16,128]{2,1,0:T(8,128)} %broadcast_in_dim.127), calls=%async_computation.4 | async-start | bytes 262144 | tf_op jit(solution)/shard_map/all_to_all | solution.py:281
  107.0 18.2 %all-to-all-start.5 = ((f32[32,16,128]{2,1,0:T(8,128)}), f32[32,16,128]{2,1,0:T(8,128)S(1)}, u32[]{:S(2)}, u32[]{:S(2)}) async-start(f32[32,16,128]{2,1,0:T(8,128)} %broadcast_in_dim.128), calls=%async_computation.5 | async-start | bytes 524288 | tf_op jit(solution)/shard_map/all_to_all | solution.py:281

commit v2 on v1

--- a/solution.py
+++ b/solution.py
@@ -102,7 +102,7 @@
 
 
 def y_forward(got, turn, sign, t1):
-    parts = [got[q, :64].astype(F32) for q in range(4)]
+    parts = [got[q, :64] for q in range(4)]
     row = lax.broadcasted_iota(jnp.int32, (64, 256), 0)
     pick = jnp.where(row == 1, sign, 0.0).astype(BF)
     result = []
@@ -117,12 +117,11 @@
                 block = block + mm(pick, both[0][:, :256], 1, 1) + mm(pick, both[1][:, :256], 1, 1)
             out.append(block)
         pieces = [out[j][:, 32 * c : 32 * c + 32] for c in range(2) for j in range(4)]
-        result.append(jnp.concatenate(pieces, axis=1).astype(BF))
+        result.append(jnp.concatenate(pieces, axis=1))
     return jnp.concatenate(result, axis=0)
 
 
-def x_project(lines, ky_lane, d1, tw1, kr, ik, tw2, d2):
-    lines = lines.astype(F32)
+def x_project(lines, ky_lane, columns, d1, tw1, kr, ik, tw2, d2):
     first = mm3(d1, halves((lines[0] + lines[1]) + (lines[2] + lines[3])))
     cs, sn = tw1[0], tw1[1]
     turned = []
@@ -169,7 +168,12 @@
         main.append(value[:, :128])
         rim.append(value[:, 128:136])
     stack = jnp.concatenate(main + rim + [jnp.zeros((64, 112), F32)], axis=1)
-    return mm3(d2, halves(stack)).astype(BF)
+    out = mm3(d2, halves(stack))
+    even = lax.broadcasted_iota(jnp.int32, (64, 384), 0) % 2 == 0
+    return jnp.concatenate(
+        [(out + jnp.where(even, columns[2 * y : 2 * y + 1], columns[2 * y + 1 : 2 * y + 2])).astype(BF) for y in range(4)],
+        axis=0,
+    )
 
 
 def regroup(lines):
@@ -206,7 +210,7 @@
             i = 4 * e + d
             piece = re * turn[0, i : i + 1] - im * turn[1, i : i + 1]
             acc[d] = piece + once if e == 0 else acc[d] + piece
-    return jnp.concatenate(acc, axis=0).astype(BF)
+    return jnp.concatenate(acc, axis=0)
 
 
 def network(proj, planes, center, point, lift18, out_cols):
@@ -214,19 +218,18 @@
     mix_hi, mix_lo = halves(mix)
     mix3 = jnp.concatenate([mix_hi, mix_lo, mix_hi], axis=1)
     mix2 = mix3[:, :48]
-    proj_b = proj.astype(BF).astype(F32)
+    mix4 = jnp.concatenate([mix2, mix2], axis=0)
     taps = [None] * 34
     sums = jnp.zeros((56, 128), F32)
     for i in range(-1, 33):
         view, view_lo = halves(planes[(i + 1) * 8 : (i + 4) * 8])
-        t_b = jnp.tanh(mm(mix3, jnp.concatenate([view, view, view_lo], axis=0))).astype(BF)
-        t = t_b.astype(F32)
+        t = jnp.tanh(mm(mix3, jnp.concatenate([view, view, view_lo], axis=0)))
         ids = (64, 66) if i < 0 else (65, 67) if i >= 32 else (i, 32 + i)
-        g0 = proj_b[ids[0] : ids[0] + 1]
-        g1 = proj_b[ids[1] : ids[1] + 1]
+        g0 = proj[ids[0] : ids[0] + 1]
+        g1 = proj[ids[1] : ids[1] + 1]
         grad = out_cols[:, 0:1] * g0 + out_cols[:, 1:2] * g1
-        gz = (grad * (1.0 - t * t)).astype(BF)
-        tap = mm(mix2, gz, 0, 0)
+        gz, gz_lo = halves(grad * (1.0 - t * t))
+        tap = mm(mix4, jnp.concatenate([gz, gz_lo], axis=0), 0, 0)
         tap = tap[:24] + tap[24:]
         for a in range(3):
             k = i + a - 1
@@ -234,17 +237,23 @@
                 piece = tap[a * 8 : a * 8 + 8]
                 taps[k] = piece if taps[k] is None else taps[k] + piece
         if 0 <= i < 32:
-            g8 = jnp.concatenate([g0[:, :256], g1[:, :256], jnp.zeros((6, 256), F32)], axis=0).astype(BF)
+            g = jnp.concatenate([g0[:, :256], g1[:, :256]], axis=0)
+            g_hi, g_lo = halves(g)
+            g8 = jnp.concatenate([g_hi.astype(F32), g_lo.astype(F32), jnp.zeros((4, 256), F32)], axis=0).astype(BF)
             left = jnp.concatenate([view[:, :256], view_lo[:, :256], g8], axis=0)
-            right = jnp.concatenate([gz[:, :256], t_b[:, :256]], axis=0)
-            sums = sums + mm(left, right, 1, 1)
-    tail = sums[48:56, 64:]
+            t_hi, t_lo = halves(t[:, :256])
+            sums = sums + (
+                mm(left, jnp.concatenate([gz[:, :256], t_hi], axis=0), 1, 1)
+                + mm(left, jnp.concatenate([gz_lo[:, :256], t_lo], axis=0), 1, 1)
+            )
+    tail = sums[48:50, 64:] + sums[50:52, 64:]
+    tail = jnp.concatenate([tail, jnp.zeros((6, 64), F32)], axis=0)
     sums = sums[:24] + sums[24:48]
     row = lax.broadcasted_iota(jnp.int32, (8, 64), 0)
     lane = lax.broadcasted_iota(jnp.int32, (8, 64), 1)
     for s in range(2):
         for v in range(2):
-            prod = proj_b[32 * s : 32 * s + 32, :256] * center[32 * v : 32 * v + 32]
+            prod = proj[32 * s : 32 * s + 32, :256] * center[32 * v : 32 * v + 32]
             total = jnp.sum(jnp.sum(prod, axis=0, keepdims=True), axis=1, keepdims=True)
             tail = jnp.where((row == 2) & (lane == 2 * s + v), total, tail)
     packed = jnp.concatenate(
@@ -254,7 +263,7 @@
         ],
         axis=0,
     )
-    return jnp.concatenate(taps[:32], axis=0), packed
+    return jnp.concatenate(taps[:32], axis=0), jnp.concatenate([packed] * 16, axis=0)
 
 
 def call(body, out_shapes, *args):
@@ -281,16 +290,21 @@
     return lax.all_to_all(value, axes, split_axis=0, concat_axis=0)
 
 
-def everyone(value, axes):
-    count = math.prod(SIZES[AXES.index(a)] for a in axes)
-    return exchange(jnp.broadcast_to(value[None], (count,) + value.shape), axes)
-
-
-def prepare(vel, cotangent):
-    edges = jnp.concatenate([vel[:, :, 0:2], vel[:, :, 254:256]], axis=2).reshape(1, 256)
-    return jnp.concatenate(
-        [cotangent.astype(BF).reshape(64, 256), edges, jnp.zeros((7, 256), BF)], axis=0
-    )
+def from_row_neighbour(value, step):
+    return lax.ppermute(value, IN_W, [(i, (i + step) % WA) for i in range(WA)])
+
+
+def pack_first(vel, cotangent):
+    edges = jnp.concatenate([vel[:, 0:2], vel[:, 254:256], jnp.zeros((64, 124), F32)], axis=1).T[:8]
+    rows = jnp.concatenate([edges, jnp.zeros((8, 192), F32)], axis=1)
+    return jnp.concatenate([cotangent, rows] * 4, axis=0)
+
+
+def sum_and_spread(got):
+    total = got[0]
+    for i in range(1, 16):
+        total = total + got[i]
+    return jnp.concatenate([total] * 32, axis=0)
 
 
 def turns(own, cols):
@@ -298,33 +312,27 @@
     return jnp.stack([jnp.cos(ang), jnp.sin(ang)])
 
 
-def rims_to_send(got, vel, x, yl, w):
-    def edges(src):
-        return lax.dynamic_index_in_dim(got, src, 0, False)[64].reshape(2, 32, 4)
-
-    def padded(v):
-        return jnp.pad(v.reshape(2, 64), ((0, 0), (0, 448)))
-
-    up = padded(edges(jnp.where(yl == 3, (x + 3) % 4, x))[:, :, 2:4])
-    down = padded(edges(jnp.where(yl == 0, (x + 1) % 4, x))[:, :, 0:2])
-    first, last = vel[:, :2].reshape(2, 512), vel[:, 30:].reshape(2, 512)
-    to_y = jnp.arange(4)[:, None, None, None]
-    to_w = jnp.arange(WA)[None, :, None, None]
-    rows = jnp.where(to_w == (w + 1) % WA, last, first)
-    return jnp.where(to_y == yl, rows, jnp.where(to_y == (yl + 1) % 4, up, down))
-
-
-def velocity_planes(rims, velocity, yl, w):
-    def piece(from_y, from_w):
-        return lax.dynamic_index_in_dim(rims, (from_y % 4) * WA + from_w % WA, 0, False).astype(F32)
-
+def columns_to_send(got, x, yl):
+    def edges(src, first):
+        rows = lax.dynamic_index_in_dim(got, src, 0, False)
+        return rows[64 + first : 66 + first, :64]
+
+    up = edges(jnp.where(yl == 3, (x + 3) % 4, x), 2)
+    down = edges(jnp.where(yl == 0, (x + 1) % 4, x), 0)
+    to_y = jnp.arange(4)[:, None, None]
+    cols = jnp.where(to_y == (yl + 1) % 4, up, down)
+    return jnp.pad(cols.reshape(8, 64), ((0, 0), (272, 48)))
+
+
+def velocity_planes(columns, above, velocity, below, yl, w):
     def side(from_y):
-        above, own, below = (piece(from_y, w + d)[:, :64].reshape(2, 32, 2) for d in (31, 0, 1))
-        return jnp.concatenate([above[:, 30:], own, below[:, :2]], axis=1)
-
-    mid = jnp.concatenate(
-        [piece(yl, w + 31).reshape(2, 2, 256), velocity, piece(yl, w + 1).reshape(2, 2, 256)], axis=1
-    )
+        def piece(from_w):
+            v = lax.dynamic_index_in_dim(columns, (from_y % 4) * WA + from_w % WA, 0, False)
+            return v.astype(F32).reshape(2, 2, 32).transpose(1, 2, 0)
+
+        return jnp.concatenate([piece(w + 31)[:, 30:], piece(w), piece(w + 1)[:, :2]], axis=1)
+
+    mid = jnp.concatenate([above, velocity, below], axis=1)
     full = jnp.concatenate([side(yl + 3), mid, side(yl + 1)], axis=2)
     moved = []
     for s in range(2):
@@ -353,34 +361,50 @@
 def finish_velocity(proj, taps, lift, out_w):
     hi = lax.Precision.HIGHEST
     main = proj[:64, :256].reshape(2, 32, 256)
-    main_b = main.astype(BF).astype(F32)
     m2 = jnp.dot(lift.T, out_w.astype(F32).T, precision=hi)
     taps = taps.reshape(32, 8, 384)
     out = []
     for s in range(2):
         left, mid, right = taps[:, 3 * s], taps[:, 3 * s + 1], taps[:, 3 * s + 2]
-        value = main[s] + m2[s, 0] * main_b[0] + m2[s, 1] * main_b[1] + mid[:, :256]
+        value = main[s] + m2[s, 0] * main[0] + m2[s, 1] * main[1] + mid[:, :256]
         value = value + jnp.concatenate([right[:, 256:257], right[:, :255]], axis=1)
         value = value + jnp.concatenate([left[:, 1:256], left[:, 257:258]], axis=1)
         out.append(value)
     return jnp.stack(out)
 
 
-def finish_weights(total, lift, kernels, point, out_w, lift18):
+def finish_weights(got, lift, lift_rows, kernels, point, out_cols, lift18_rows):
     hi = lax.Precision.HIGHEST
-    scale = 1.0 / math.sqrt(NX * NY)
-    total = total * scale
+    total = got[0]
+    for i in range(1, 32):
+        total = total + got[i]
+    total = total * (1.0 / math.sqrt(NX * NY))
     q = jnp.concatenate([total[:8, :64], total[:8, 64:], total[8:, :64]], axis=0)
-    gpt = total[8:10, 64:]
-    gpv = total[10, 64:68].reshape(2, 2)
-    grad_out = gpt + jnp.dot(gpv, lift.T, precision=hi)
-    grad_point = jnp.einsum("ko,ck->oc", q, lift18, precision=hi)
-    gv = jnp.einsum("ko,oc->ck", q, point.astype(F32), precision=hi)
-    gv = gv.reshape(64, 3, 8)[:, :, :6].reshape(64, 3, 2, 3)
-    grad_kernels = jnp.sum(gv * lift[:, None, :, None], axis=2).reshape(64, 9)
-    grad_lift = jnp.sum(gv * kernels.reshape(64, 3, 1, 3), axis=(1, 3))
-    grad_lift = grad_lift + jnp.dot(out_w.astype(F32).T, gpv, precision=hi)
-    return grad_lift, grad_kernels[None], grad_point[None], grad_out
+
+    def pair_sum(s, v):
+        return total[10:11, 64 + 2 * s + v : 65 + 2 * s + v]
+
+    grad_out = [
+        total[8 + s : 9 + s, 64:] + pair_sum(s, 0) * lift_rows[0:1] + pair_sum(s, 1) * lift_rows[1:2] for s in range(2)
+    ]
+    grad_point = lax.dot_general(q, lift18_rows, (((0,), (0,)), ((), ())), precision=hi, preferred_element_type=F32)
+    gv = lax.dot_general(point, q, (((0,), (1,)), ((), ())), precision=hi, preferred_element_type=F32)
+    grad_kernels = [
+        lift[:, 0:1] * gv[:, 8 * a : 8 * a + 3] + lift[:, 1:2] * gv[:, 8 * a + 3 : 8 * a + 6] for a in range(3)
+    ]
+    grad_lift = []
+    for s in range(2):
+        value = out_cols[:, 0:1] * pair_sum(0, s) + out_cols[:, 1:2] * pair_sum(1, s)
+        for a in range(3):
+            first = 8 * a + 3 * s
+            value = value + jnp.sum(kernels[:, 3 * a : 3 * a + 3] * gv[:, first : first + 3], axis=1, keepdims=True)
+        grad_lift.append(value)
+    return (
+        jnp.concatenate(grad_lift, axis=1),
+        jnp.concatenate(grad_kernels, axis=1),
+        grad_point,
+        jnp.concatenate(grad_out, axis=0),
+    )
 
 
 def local(velocity, cotangent, lift_weight, depth_kernels, point_weights, out_weight):
@@ -400,35 +424,43 @@
     turn4 = turns(klass, cols4 + 1024 * (step % 4) + 256 * yl + NY)
     lift18 = lift_matrix(lift_weight, kernels)
 
-    vel = velocity.astype(BF)
-    got1 = everyone(prepare(vel, cotangent), ("x",))
-    spec = call(y_forward, sds((256, 256), BF), got1, turn1, sign, tab["t1"])
-    rims = rims_to_send(got1, vel, x, yl, w).reshape(128, 2, 512)
-    got2 = exchange(jnp.concatenate([spec.reshape(128, 2, 256), rims], axis=2), ("yl",) + IN_W)
+    above = from_row_neighbour(velocity[:, 30:], 1)
+    below = from_row_neighbour(velocity[:, :2], -1)
+    sent1 = call(pack_first, sds((288, 256), F32), velocity.reshape(64, 256), cotangent.reshape(64, 256))
+    got1 = exchange(sent1.reshape(4, 72, 256), ("x",))
+    spec = call(y_forward, sds((256, 256), F32), got1, turn1, sign, tab["t1"])
+    got2 = exchange(spec.reshape(128, 2, 256), ("yl",) + IN_W)
+    columns = columns_to_send(got1, x, yl)
     sent3 = call(
-        x_project, sds((64, 384), BF), got2[:, :, :256].reshape(4, 64, 256), ky_lane, tab["d1"], tab["tw1"], tab["kr"], tab["ik"], tab["tw2"], tab["d2"]
-    )
-    spread = jnp.broadcast_to(sent3.reshape(1, 32, 2, 384), (4, 32, 2, 384)).reshape(128, 2, 384)
-    got3 = exchange(spread, ("yl",) + IN_W)
-    planes = velocity_planes(got2[:, :, 256:], velocity, yl, w)
-    sent4 = call(y_inverse, sds((288, 384), BF), got3.reshape(4, 64, 384), turn4, zero, tab["tk"])
+        x_project, sds((256, 384), BF), got2.reshape(4, 64, 256), ky_lane, columns, tab["d1"], tab["tw1"], tab["kr"], tab["ik"], tab["tw2"], tab["d2"]
+    )
+    got3 = exchange(sent3.reshape(128, 2, 384), ("yl",) + IN_W)
+    planes = velocity_planes(got3[:, :, 272:336], above, velocity, below, yl, w)
+    sent4 = call(y_inverse, sds((288, 384), F32), got3.reshape(4, 64, 384), turn4, zero, tab["tk"])
     got4 = exchange(sent4.reshape(4, 72, 384), ("x",))
 
     def last(got, planes, center, point, lift18, out_cols):
-        got = got.astype(F32)
         proj = (got[0] + got[1]) + (got[2] + got[3])
         taps, packed = network(proj, planes, center, point, lift18, out_cols)
         return proj, taps, packed
 
+    point_f = point.astype(F32)
+    out_cols = out_weight.astype(F32).T
     proj, taps, packed = call(
         last,
-        (sds((72, 384), F32), sds((256, 384), F32), sds((16, 128), F32)),
-        got4, planes, velocity.reshape(64, 256), point.astype(F32), lift18, out_weight.astype(F32).T,
-    )
-    part = jnp.sum(everyone(packed, ("yl", "yh", "c")), axis=0)
-    total = jnp.sum(everyone(part, ("x", "z")), axis=0)
+        (sds((72, 384), F32), sds((256, 384), F32), sds((256, 128), F32)),
+        got4, planes, velocity.reshape(64, 256), point_f, lift18, out_cols,
+    )
+    part = exchange(packed.reshape(16, 16, 128), ("yl", "yh", "c"))
+    part = call(sum_and_spread, sds((512, 128), F32), part)
+    total = exchange(part.reshape(32, 16, 128), ("x", "z"))
     grad_velocity = finish_velocity(proj, taps, lift_weight, out_weight)
-    return (grad_velocity,) + finish_weights(total, lift_weight, kernels, point, out_weight, lift18)
+    grad_lift, grad_kernels, grad_point, grad_out = call(
+        finish_weights,
+        (sds((64, 2), F32), sds((64, 9), F32), sds((64, 64), F32), sds((2, 64), F32)),
+        total, lift_weight, lift_weight.T, kernels, point_f, out_cols, lift18.T,
+    )
+    return grad_velocity, grad_lift, grad_kernels[None], grad_point[None], grad_out
 
 
 def solution(mesh):

time: 129 us -> 131 us (1.016)
  starting transfers between devices: 39.6 us -> 47.7 us
  waiting for transfers between devices: 55.3 us -> 50.1 us
  Pallas kernels: 10 us -> 14.1 us
  matrix products: 2.56 us -> 0.12 us
  other arithmetic: 6.1 us -> 4.19 us
    ppermute x0 -> x2, starting transfers between devices: none -> 5.56 us  [from_row_neighbour(): return lax.ppermute(value, IN_W, [(i, (i + step) % WA) for i in range(WA)])]
    all_to_all x6, waiting for transfers between devices: 55.3 us -> 50.1 us  [exchange(): return lax.all_to_all(value, axes, split_axis=0, concat_axis=0)]
    pallas_call x4 -> x7, Pallas kernels: 10 us -> 14.1 us  [call(): pl.pallas_call(kernel, out_shape=out_shapes, compiler_params=pltpu.Compil...]
    unnamed x40 -> x43, local copies, waits for them, and re-layouts: 3.33 us -> 6.54 us
    broadcast_in_dim x8 -> x4, local copies, waits for them, and re-layouts: 3 us -> 0.17 us  [columns_to_send(): cols = jnp.where(to_y == (yl + 1) % 4, up, down)]
    all_to_all x6, starting transfers between devices: 39.6 us -> 42.2 us  [exchange(): return lax.all_to_all(value, axes, split_axis=0, concat_axis=0)]
    dot_general x4 -> x0, matrix products: 2.44 us -> none  [the longest x1 0.85 us: finish_weights(): grad_point = jnp.einsum('ko,ck->oc', q, lift18, precision=hi)]
    another operation x3 -> x2, other arithmetic: 3.39 us -> 3.32 us  [finish_velocity(): return jnp.stack(out)]
  transfers between devices with their start and end apart: 6 -> 8, of which waited for: 6 -> 5; matrix products, arithmetic and copies ran while one was open for 6% -> 8% of each run, Pallas kernels for 0% -> 2%
where the time goes in v2:
time: 131 us; the launch traced here: 130 us
  waiting for transfers between devices  50.1 us (38%)
  starting transfers between devices  47.7 us (36%)
  Pallas kernels  14.1 us (11%)
  local copies, waits for them, and re-layouts  12.6 us (10%)
  other arithmetic  4.19 us (3%)
    all_to_all x6, waiting for transfers between devices, exchange(): return lax.all_to_all(value, axes, split_axis=0, concat_axis=0)  50.1 us
    all_to_all x6, starting transfers between devices, exchange(): return lax.all_to_all(value, axes, split_axis=0, concat_axis=0)  42.2 us
    pallas_call x7, Pallas kernels, call(): pl.pallas_call(kernel, out_shape=out_shapes, compiler_params=pltpu.Compil...  14.1 us
    unnamed x43, local copies, waits for them, and re-layouts  6.54 us
    ppermute x2, starting transfers between devices, from_row_neighbour(): return lax.ppermute(value, IN_W, [(i, (i + step) % WA) for i in range(WA)])  5.56 us
    another operation x2, other arithmetic, finish_velocity(): return jnp.stack(out)  3.32 us
  transfers between devices with their start and end apart: 8, of which 5 were waited for; matrix products, arithmetic and copies ran while one was open for 8% of the time, Pallas kernels for 2%

profile of v2, /device:TPU:64, one launch (start us, length us, event | category | flops | bytes accessed | tf_op | source)
XLA Modules:
  0.0 130.2 jit_solution(4248565314552477450)
XLA Ops:
  0.6 0.8 copy-done
  1.5 0.8 copy-done.9
  2.3 0.8 shard_map.182
  3.2 4.4 %all-to-all-start = ((f32[4,72,256]{2,1,0:T(8,128)}), f32[4,72,256]{2,1,0:T(8,128)S(1)}, u32[]{:S(2)}, u32[]{:S(2)}) async-start(f32[4,72,256]{2,1,0:T(8,128)} %bitcast.2), calls=%async_computation | async-start | bytes 589824 | tf_op jit(solution)/shard_map/all_to_all | solution.py:290
  7.6 1.9 %collective-permute-start = (f32[2,2,256]{2,1,0:T(2,128)S(1)}, f32[2,2,256]{2,1,0:T(2,128)S(1)}, u32[]{:S(2)}, u32[]{:S(2)}) collective-permute-start(f32[2,2,256]{2,1,0:T(2,128)S(1)} %get-tuple-element.42), channel_id=1, source_target_pairs={{0,1},{1,2},{2,3},{3,4},{4,5},{5,6},{6,7},{7,8},{8,9},{9,10},{10,1... | collective-permute-start | bytes 12296 | tf_op jit(solution)/shard_map/ppermute | solution.py:294
  9.5 3.6 %collective-permute-start.1 = (f32[2,2,256]{2,1,0:T(2,128)S(1)}, f32[2,2,256]{2,1,0:T(2,128)S(1)}, u32[]{:S(2)}, u32[]{:S(2)}) collective-permute-start(f32[2,2,256]{2,1,0:T(2,128)S(1)} %get-tuple-element.43), channel_id=1, source_target_pairs={{0,31},{1,0},{2,1},{3,2},{4,3},{5,4},{6,5},{7,6},{8,7},{9,8},{10,9... | collective-permute-start | bytes 12296 | tf_op jit(solution)/shard_map/ppermute | solution.py:294
  13.3 0.1 broadcast_in_dim.44
  13.5 0.7 copy-done.12
  14.1 0.2 fusion.17
  14.3 0.6 copy-done.14
  15.0 0.2 fusion.15
  15.2 1.1 shard_map.183
  16.3 0.9 reshape.554
  17.2 17.9 %all-to-all-start.1 = ((f32[128,2,256]{2,1,0:T(2,128)}), f32[128,2,256]{2,1,0:T(2,128)S(1)}, u32[]{:S(2)}, u32[]{:S(2)}) async-start(f32[128,2,256]{2,1,0:T(2,128)} %reshape.554), calls=%async_computation.1 | async-start | bytes 524288 | tf_op jit(solution)/shard_map/all_to_all | solution.py:290
  35.3 14.0 %all-to-all-done.1 = f32[128,2,256]{2,1,0:T(2,128)S(1)} async-done(((f32[128,2,256]{2,1,0:T(2,128)}), f32[128,2,256]{2,1,0:T(2,128)S(1)}, u32[]{:S(2)}, u32[]{:S(2)}) %all-to-all-start.1) | async-done | bytes 262176 | tf_op jit(solution)/shard_map/all_to_all | solution.py:290
  49.4 0.2 reshape.555.refs_0_
  49.6 0.9 shard_map.184
  50.5 0.7 reshape.556
  51.3 6.7 %all-to-all-start.2 = ((bf16[128,2,384]{2,1,0:T(2,128)(2,1)}), bf16[128,2,384]{2,1,0:T(2,128)(2,1)S(1)}, u32[]{:S(2)}, u32[]{:S(2)}) async-start(bf16[128,2,384]{2,1,0:T(2,128)(2,1)} %reshape.556), calls=%async_computation.2 | async-start | bytes 393216 | tf_op jit(solution)/shard_map/all_to_all | solution.py:290
  58.0 0.1 copy.47
  58.1 0.1 copy.36.refs_1_
  58.3 0.1 copy.29.refs_4_
  58.4 0.6 copy-done.15
  58.9 0.1 copy.28
  59.1 0.7 copy-done.13
  59.8 11.2 %all-to-all-done.2 = bf16[128,2,384]{2,1,0:T(2,128)(2,1)S(1)} async-done(((bf16[128,2,384]{2,1,0:T(2,128)(2,1)}), bf16[128,2,384]{2,1,0:T(2,128)(2,1)S(1)}, u32[]{:S(2)}, u32[]{:S(2)}) %all-to-all-start.2) | async-done | bytes 196640 | tf_op jit(solution)/shard_map/all_to_all | solution.py:290
  71.0 0.1 slice.292
  71.2 0.1 convert_element_type.92
  71.3 0.1 slice.293
  71.3 0.1 convert_element_type.94
  71.4 0.1 convert_element_type.93
  71.5 0.1 convert_element_type.95
  71.6 0.1 slice.295
  71.7 0.1 convert_element_type.96
  71.8 0.1 convert_element_type.97
  71.8 0.1 maximum_convert_fusion
  71.9 0.1 maximum_convert_fusion.1
  72.0 0.1 copy.20
  72.1 0.1 copy.21
  72.2 0.1 pad_maximum_fusion
  72.4 0.1 fusion.30
  72.5 0.1 fusion.31
  72.6 0.1 fusion.32
  72.8 0.7 copy-done.4
  73.5 2.0 %shard_map.185 = f32[288,384]{1,0:T(8,128)} custom-call(bf16[4,64,384]{2,1,0:T(8,128)(2,1)S(1)} %reshape.557.refs_0_, f32[2,16,384]{2,1,0:T(8,128)S(1)} %pad_maximum_fusion.2.refs_1_, f32[1,384]{1,0:T(1,128)S(1)} %select_n.202.refs_2_, bf16[256,768]{1,0:T(8,128)(2,1)S(1)} %copy-done.4), custom_call_target="tpu_custom_call" | custom-call | tf_op jit(solution)/shard_map/pallas_call | solution.py:278
  75.5 4.8 %all-to-all-start.3 = ((f32[4,72,384]{2,1,0:T(8,128)}), f32[4,72,384]{2,1,0:T(8,128)S(1)}, u32[]{:S(2)}, u32[]{:S(2)}) async-start(f32[4,72,384]{2,1,0:T(8,128)} %bitcast.7), calls=%async_computation.3 | async-start | bytes 884736 | tf_op jit(solution)/shard_map/all_to_all | solution.py:290
  80.3 0.1 fusion.33
  80.4 0.1 maximum_bitcast_fusion.5
  80.9 0.7 stack.73
  81.6 7.6 %all-to-all-done.3.refs_0_ = f32[4,72,384]{2,1,0:T(8,128)S(1)} async-done(((f32[4,72,384]{2,1,0:T(8,128)}), f32[4,72,384]{2,1,0:T(8,128)S(1)}, u32[]{:S(2)}, u32[]{:S(2)}) %all-to-all-start.3) | async-done | bytes 442400 | tf_op jit(solution)/shard_map/all_to_all | solution.py:290
  89.2 7.2 %shard_map.186 = (f32[72,384]{1,0:T(8,128)S(1)}, f32[256,384]{1,0:T(8,128)S(1)}, f32[256,128]{1,0:T(8,128)}) custom-call(f32[4,72,384]{2,1,0:T(8,128)S(1)} %all-to-all-done.3.refs_0_, f32[288,384]{1,0:T(8,128)S(1)} %bitcast.78, f32[64,256]{1,0:T(8,128)S(1)} %bitcast.80, f32[64,64]{1,0:T(8,128)S(1)} %bitcast_convert_fusion.refs_3_.refs_4_, ...), custom_call_target="tpu_custom_call" | custom-call | tf_op jit(solution)/shard_map/pallas_call | solution.py:278
  96.4 3.5 %all-to-all-start.4 = ((f32[16,16,128]{2,1,0:T(8,128)}), f32[16,16,128]{2,1,0:T(8,128)S(1)}, u32[]{:S(2)}, u32[]{:S(2)}) async-start(f32[16,16,128]{2,1,0:T(8,128)} %bitcast.38), calls=%async_computation.4 | async-start | bytes 262144 | tf_op jit(solution)/shard_map/all_to_all | solution.py:290
  99.9 0.1 fusion.35
  100.0 0.6 fusion.34
  100.7 8.0 %all-to-all-done.4.refs_0_ = f32[16,16,128]{2,1,0:T(8,128)S(1)} async-done(((f32[16,16,128]{2,1,0:T(8,128)}), f32[16,16,128]{2,1,0:T(8,128)S(1)}, u32[]{:S(2)}, u32[]{:S(2)}) %all-to-all-start.4) | async-done | bytes 131104 | tf_op jit(solution)/shard_map/all_to_all | solution.py:290
  108.6 0.7 shard_map.187
  109.4 4.9 %all-to-all-start.5 = ((f32[32,16,128]{2,1,0:T(8,128)}), f32[32,16,128]{2,1,0:T(8,128)S(1)}, u32[]{:S(2)}, u32[]{:S(2)}) async-start(f32[32,16,128]{2,1,0:T(8,128)} %bitcast.39), calls=%async_computation.5 | async-start | bytes 524288 | tf_op jit(solution)/shard_map/all_to_all | solution.py:290
  114.3 0.2 fusion.28
  114.9 2.7 %fusion.4 = (f32[1,32,256]{2,1,0:T(8,128)S(1)}, f32[1,32,256]{2,1,0:T(8,128)S(1)}) fusion(f32[32,384]{1,0:T(8,128)S(1)} %bitcast.98, f32[32,255]{1,0:T(8,128)S(1)} %slice.330, f32[32,1]{1,0:T(8,128)S(1)} %slice.329, f32[32,1]{1,0:T(8,128)S(1)} %slice.333, f32[32,255]{1,0:T(8,128)S(1)} %slice.332, f32[72,384]{1,0:T(8,128)S(1)} %get-tuple-element.12, ...), kind=kLoop, calls=%fused_computation.27 | loop fusion | flops 147456 | bytes 327696 | tf_op jit(solution)/shard_map/stack | solution.py:373
  117.6 0.6 pad_maximum_fusion.1
  118.2 9.4 %all-to-all-done.5.refs_0_ = f32[32,16,128]{2,1,0:T(8,128)S(1)} async-done(((f32[32,16,128]{2,1,0:T(8,128)}), f32[32,16,128]{2,1,0:T(8,128)S(1)}, u32[]{:S(2)}, u32[]{:S(2)}) %all-to-all-start.5) | async-done | bytes 262176 | tf_op jit(solution)/shard_map/all_to_all | solution.py:290
  127.6 1.3 %shard_map.188 = (f32[64,2]{1,0:T(8,128)S(1)}, f32[64,9]{1,0:T(8,128)S(1)}, f32[64,64]{1,0:T(8,128)}, f32[2,64]{1,0:T(2,128)}) custom-call(f32[32,16,128]{2,1,0:T(8,128)S(1)} %all-to-all-done.5.refs_0_, f32[64,2]{1,0:T(8,128)S(1)} %copy.36.refs_1_, f32[2,64]{1,0:T(2,128)S(1)} %bitcast.88, f32[64,9]{1,0:T(8,128)S(1)} %bitcast.84, ...), custom_call_target="tpu_custom_call" | custom-call | tf_op jit(solution)/shard_map/pallas_call | solution.py:278
  128.9 0.7 copy.39
  129.5 0.6 copy.38
  (76 shorter events, 1.4 us)
Async XLA Ops:
  0.6 0.8 copy-start
  1.5 0.8 copy-start.9
  3.2 12.0 %copy-start.2 = (bf16[2,256,512]{2,1,0:T(8,128)(2,1)S(1)}, bf16[2,256,512]{2,1,0:T(8,128)(2,1)}, u32[]{:S(2)}) copy-start(bf16[2,256,512]{2,1,0:T(8,128)(2,1)} %constant.221.clone.refs_3_) | copy-start | bytes 1572868
  3.2 4.4 %copy-start.1 = (f32[2,32,256]{2,1,0:T(8,128)S(1)}, f32[2,32,256]{2,1,0:T(8,128)}, u32[]{:S(2)}) copy-start(f32[2,32,256]{2,1,0:T(8,128)} %param.15) | copy-start | bytes 196612
  3.2 12.0 %all-to-all-start = ((f32[4,72,256]{2,1,0:T(8,128)}), f32[4,72,256]{2,1,0:T(8,128)S(1)}, u32[]{:S(2)}, u32[]{:S(2)}) async-start(f32[4,72,256]{2,1,0:T(8,128)} %bitcast.2), calls=%async_computation | async-start | bytes 589824 | tf_op jit(solution)/shard_map/all_to_all | solution.py:290
  7.6 64.6 %collective-permute-start = (f32[2,2,256]{2,1,0:T(2,128)S(1)}, f32[2,2,256]{2,1,0:T(2,128)S(1)}, u32[]{:S(2)}, u32[]{:S(2)}) collective-permute-start(f32[2,2,256]{2,1,0:T(2,128)S(1)} %get-tuple-element.42), channel_id=1, source_target_pairs={{0,1},{1,2},{2,3},{3,4},{4,5},{5,6},{6,7},{7,8},{8,9},{9,10},{10,1... | collective-permute-start | bytes 12296 | tf_op jit(solution)/shard_map/ppermute | solution.py:294
  9.5 62.7 %collective-permute-start.1 = (f32[2,2,256]{2,1,0:T(2,128)S(1)}, f32[2,2,256]{2,1,0:T(2,128)S(1)}, u32[]{:S(2)}, u32[]{:S(2)}) collective-permute-start(f32[2,2,256]{2,1,0:T(2,128)S(1)} %get-tuple-element.43), channel_id=1, source_target_pairs={{0,31},{1,0},{2,1},{3,2},{4,3},{5,4},{6,5},{7,6},{8,7},{9,8},{10,9... | collective-permute-start | bytes 12296 | tf_op jit(solution)/shard_map/ppermute | solution.py:294
  13.4 0.7 copy-start.12
  14.3 0.7 copy-start.14
  17.2 17.9 %copy-start.11 = (f32[64,2]{0,1:T(2,128)S(1)}, f32[64,2]{0,1:T(2,128)}, u32[]{:S(2)}) copy-start(f32[64,2]{0,1:T(2,128)} %param.17) | copy-start | bytes 1540
  17.2 32.4 %copy-start.7 = (f32[2,32,256]{2,1,0:T(8,128)S(1)}, f32[2,32,256]{2,1,0:T(8,128)}, u32[]{:S(2)}) copy-start(f32[2,32,256]{2,1,0:T(8,128)} %constant.223.clone.refs_4_) | copy-start | bytes 196612
  17.2 32.4 %copy-start.8 = (f32[2,32,256]{2,1,0:T(8,128)S(1)}, f32[2,32,256]{2,1,0:T(8,128)}, u32[]{:S(2)}) copy-start(f32[2,32,256]{2,1,0:T(8,128)} %constant.226.clone.refs_7_) | copy-start | bytes 196612
  17.2 32.4 %copy-start.10 = (bf16[2,64,64]{2,1,0:T(8,128)(2,1)S(1)}, bf16[2,64,64]{2,1,0:T(8,128)(2,1)}, u32[]{:S(2)}) copy-start(bf16[2,64,64]{2,1,0:T(8,128)(2,1)} %constant.227.clone.refs_8_) | copy-start | bytes 49156
  17.2 32.2 %all-to-all-start.1 = ((f32[128,2,256]{2,1,0:T(2,128)}), f32[128,2,256]{2,1,0:T(2,128)S(1)}, u32[]{:S(2)}, u32[]{:S(2)}) async-start(f32[128,2,256]{2,1,0:T(2,128)} %reshape.554), calls=%async_computation.1 | async-start | bytes 524288 | tf_op jit(solution)/shard_map/all_to_all | solution.py:290
  35.1 14.5 %copy-start.3 = (bf16[2,256,512]{2,1,0:T(8,128)(2,1)S(1)}, bf16[2,256,512]{2,1,0:T(8,128)(2,1)}, u32[]{:S(2)}) copy-start(bf16[2,256,512]{2,1,0:T(8,128)(2,1)} %constant.225.clone.refs_6_) | copy-start | bytes 1572868
  35.3 14.3 %copy-start.5 = (bf16[2,256,256]{2,1,0:T(8,128)(2,1)S(1)}, bf16[2,256,256]{2,1,0:T(8,128)(2,1)}, u32[]{:S(2)}) copy-start(bf16[2,256,256]{2,1,0:T(8,128)(2,1)} %constant.224.clone.refs_5_) | copy-start | bytes 786436
  35.3 14.3 %copy-start.6 = (bf16[2,128,64]{2,1,0:T(8,128)(2,1)S(1)}, bf16[2,128,64]{2,1,0:T(8,128)(2,1)}, u32[]{:S(2)}) copy-start(bf16[2,128,64]{2,1,0:T(8,128)(2,1)} %constant.222.clone.refs_3_) | copy-start | bytes 98308
  51.3 19.8 %all-to-all-start.2 = ((bf16[128,2,384]{2,1,0:T(2,128)(2,1)}), bf16[128,2,384]{2,1,0:T(2,128)(2,1)S(1)}, u32[]{:S(2)}, u32[]{:S(2)}) async-start(bf16[128,2,384]{2,1,0:T(2,128)(2,1)} %reshape.556), calls=%async_computation.2 | async-start | bytes 393216 | tf_op jit(solution)/shard_map/all_to_all | solution.py:290
  58.3 0.7 copy-start.15
  59.1 0.7 copy-start.13
  72.5 1.0 copy-start.4
  75.5 13.7 %all-to-all-start.3 = ((f32[4,72,384]{2,1,0:T(8,128)}), f32[4,72,384]{2,1,0:T(8,128)S(1)}, u32[]{:S(2)}, u32[]{:S(2)}) async-start(f32[4,72,384]{2,1,0:T(8,128)} %bitcast.7), calls=%async_computation.3 | async-start | bytes 884736 | tf_op jit(solution)/shard_map/all_to_all | solution.py:290
  96.4 12.2 %all-to-all-start.4 = ((f32[16,16,128]{2,1,0:T(8,128)}), f32[16,16,128]{2,1,0:T(8,128)S(1)}, u32[]{:S(2)}, u32[]{:S(2)}) async-start(f32[16,16,128]{2,1,0:T(8,128)} %bitcast.38), calls=%async_computation.4 | async-start | bytes 262144 | tf_op jit(solution)/shard_map/all_to_all | solution.py:290
  109.4 18.2 %all-to-all-start.5 = ((f32[32,16,128]{2,1,0:T(8,128)}), f32[32,16,128]{2,1,0:T(8,128)S(1)}, u32[]{:S(2)}, u32[]{:S(2)}) async-start(f32[32,16,128]{2,1,0:T(8,128)} %bitcast.39), calls=%async_computation.5 | async-start | bytes 524288 | tf_op jit(solution)/shard_map/all_to_all | solution.py:290

commit v3 on v2

--- a/solution.py
+++ b/solution.py
@@ -118,7 +118,7 @@
             out.append(block)
         pieces = [out[j][:, 32 * c : 32 * c + 32] for c in range(2) for j in range(4)]
         result.append(jnp.concatenate(pieces, axis=1))
-    return jnp.concatenate(result, axis=0)
+    return jnp.concatenate(result, axis=0).reshape(128, 2, 256)
 
 
 def x_project(lines, ky_lane, columns, d1, tw1, kr, ik, tw2, d2):
@@ -373,7 +373,7 @@
     return jnp.stack(out)
 
 
-def finish_weights(got, lift, lift_rows, kernels, point, out_cols, lift18_rows):
+def finish_weights(got, lift_rows, kernel_rows, point, out_rows, lift18_rows):
     hi = lax.Precision.HIGHEST
     total = got[0]
     for i in range(1, 32):
@@ -388,20 +388,20 @@
         total[8 + s : 9 + s, 64:] + pair_sum(s, 0) * lift_rows[0:1] + pair_sum(s, 1) * lift_rows[1:2] for s in range(2)
     ]
     grad_point = lax.dot_general(q, lift18_rows, (((0,), (0,)), ((), ())), precision=hi, preferred_element_type=F32)
-    gv = lax.dot_general(point, q, (((0,), (1,)), ((), ())), precision=hi, preferred_element_type=F32)
+    gv = lax.dot_general(q, point, (((1,), (0,)), ((), ())), precision=hi, preferred_element_type=F32)
     grad_kernels = [
-        lift[:, 0:1] * gv[:, 8 * a : 8 * a + 3] + lift[:, 1:2] * gv[:, 8 * a + 3 : 8 * a + 6] for a in range(3)
+        lift_rows[0:1] * gv[8 * a : 8 * a + 3] + lift_rows[1:2] * gv[8 * a + 3 : 8 * a + 6] for a in range(3)
     ]
     grad_lift = []
     for s in range(2):
-        value = out_cols[:, 0:1] * pair_sum(0, s) + out_cols[:, 1:2] * pair_sum(1, s)
+        value = out_rows[0:1] * pair_sum(0, s) + out_rows[1:2] * pair_sum(1, s)
         for a in range(3):
             first = 8 * a + 3 * s
-            value = value + jnp.sum(kernels[:, 3 * a : 3 * a + 3] * gv[:, first : first + 3], axis=1, keepdims=True)
+            value = value + jnp.sum(kernel_rows[3 * a : 3 * a + 3] * gv[first : first + 3], axis=0, keepdims=True)
         grad_lift.append(value)
     return (
-        jnp.concatenate(grad_lift, axis=1),
-        jnp.concatenate(grad_kernels, axis=1),
+        jnp.concatenate(grad_lift, axis=0),
+        jnp.concatenate(grad_kernels, axis=0).reshape(9, 1, 64),
         grad_point,
         jnp.concatenate(grad_out, axis=0),
     )
@@ -424,20 +424,22 @@
     turn4 = turns(klass, cols4 + 1024 * (step % 4) + 256 * yl + NY)
     lift18 = lift_matrix(lift_weight, kernels)
 
-    above = from_row_neighbour(velocity[:, 30:], 1)
-    below = from_row_neighbour(velocity[:, :2], -1)
     sent1 = call(pack_first, sds((288, 256), F32), velocity.reshape(64, 256), cotangent.reshape(64, 256))
     got1 = exchange(sent1.reshape(4, 72, 256), ("x",))
-    spec = call(y_forward, sds((256, 256), F32), got1, turn1, sign, tab["t1"])
-    got2 = exchange(spec.reshape(128, 2, 256), ("yl",) + IN_W)
+    spec = call(y_forward, sds((128, 2, 256), F32), got1, turn1, sign, tab["t1"])
+    spec, bottom, top = lax.optimization_barrier((spec, velocity[:, 30:], velocity[:, :2]))
+    got2 = exchange(spec, ("yl",) + IN_W)
+    above = from_row_neighbour(bottom, 1)
+    below = from_row_neighbour(top, -1)
     columns = columns_to_send(got1, x, yl)
     sent3 = call(
         x_project, sds((256, 384), BF), got2.reshape(4, 64, 256), ky_lane, columns, tab["d1"], tab["tw1"], tab["kr"], tab["ik"], tab["tw2"], tab["d2"]
     )
     got3 = exchange(sent3.reshape(128, 2, 384), ("yl",) + IN_W)
+    sent4 = call(y_inverse, sds((288, 384), F32), got3.reshape(4, 64, 384), turn4, zero, tab["tk"])
+    sent4, got3 = lax.optimization_barrier((sent4, got3))
+    got4 = exchange(sent4.reshape(4, 72, 384), ("x",))
     planes = velocity_planes(got3[:, :, 272:336], above, velocity, below, yl, w)
-    sent4 = call(y_inverse, sds((288, 384), F32), got3.reshape(4, 64, 384), turn4, zero, tab["tk"])
-    got4 = exchange(sent4.reshape(4, 72, 384), ("x",))
 
     def last(got, planes, center, point, lift18, out_cols):
         proj = (got[0] + got[1]) + (got[2] + got[3])
@@ -457,10 +459,10 @@
     grad_velocity = finish_velocity(proj, taps, lift_weight, out_weight)
     grad_lift, grad_kernels, grad_point, grad_out = call(
         finish_weights,
-        (sds((64, 2), F32), sds((64, 9), F32), sds((64, 64), F32), sds((2, 64), F32)),
-        total, lift_weight, lift_weight.T, kernels, point_f, out_cols, lift18.T,
-    )
-    return grad_velocity, grad_lift, grad_kernels[None], grad_point[None], grad_out
+        (sds((2, 64), F32), sds((9, 1, 64), F32), sds((64, 64), F32), sds((2, 64), F32)),
+        total, lift_weight.T, kernels.T, point_f, out_weight.astype(F32), lift18.T,
+    )
+    return grad_velocity, grad_lift.T, grad_kernels.transpose(1, 2, 0), grad_point[None], grad_out
 
 
 def solution(mesh):

time: 131 us -> 126 us (0.962)
  local copies, waits for them, and re-layouts: 12.6 us -> 9.49 us
  starting transfers between devices: 47.7 us -> 45.6 us
    unnamed x43 -> x39, local copies, waits for them, and re-layouts: 6.54 us -> 4.27 us
    all_to_all x6, starting transfers between devices: 42.2 us -> 40.1 us  [exchange(): return lax.all_to_all(value, axes, split_axis=0, concat_axis=0)]
  transfers between devices with their start and end apart: 8 -> 8, of which waited for: 5 -> 6; matrix products, arithmetic and copies ran while one was open for 8% -> 7% of each run, Pallas kernels for 2% -> 2%
where the time goes in v3:
time: 126 us; the launch traced here: 125 us
  waiting for transfers between devices  50 us (40%)
  starting transfers between devices  45.6 us (36%)
  Pallas kernels  14.5 us (12%)
  local copies, waits for them, and re-layouts  9.49 us (8%)
  other arithmetic  4.19 us (3%)
    all_to_all x6, waiting for transfers between devices, exchange(): return lax.all_to_all(value, axes, split_axis=0, concat_axis=0)  50 us
    all_to_all x6, starting transfers between devices, exchange(): return lax.all_to_all(value, axes, split_axis=0, concat_axis=0)  40.1 us
    pallas_call x7, Pallas kernels, call(): pl.pallas_call(kernel, out_shape=out_shapes, compiler_params=pltpu.Compil...  14.5 us
    ppermute x2, starting transfers between devices, from_row_neighbour(): return lax.ppermute(value, IN_W, [(i, (i + step) % WA) for i in range(WA)])  5.56 us
    unnamed x39, local copies, waits for them, and re-layouts  4.27 us
    another operation x2, other arithmetic, finish_velocity(): return jnp.stack(out)  3.32 us
  transfers between devices with their start and end apart: 8, of which 6 were waited for; matrix products, arithmetic and copies ran while one was open for 7% of the time, Pallas kernels for 2%

profile of v3, /device:TPU:64, one launch (start us, length us, event | category | flops | bytes accessed | tf_op | source)
XLA Modules:
  0.0 125.1 jit_solution(12991471158210861461)
XLA Ops:
  0.6 0.8 copy-done
  1.5 0.8 copy-done.9
  2.3 0.8 shard_map.182
  3.2 4.4 %all-to-all-start = ((f32[4,72,256]{2,1,0:T(8,128)}), f32[4,72,256]{2,1,0:T(8,128)S(1)}, u32[]{:S(2)}, u32[]{:S(2)}) async-start(f32[4,72,256]{2,1,0:T(8,128)} %bitcast.2), calls=%async_computation | async-start | bytes 589824 | tf_op jit(solution)/shard_map/all_to_all | solution.py:290
  7.6 0.8 copy-done.1
  8.4 0.1 broadcast_in_dim.40
  8.5 0.1 broadcast_in_dim.41
  8.6 0.2 fusion.17
  8.8 0.5 copy-done.14
  9.3 0.2 fusion.15
  9.5 0.5 copy-done.13
  10.0 0.7 copy-done.11
  10.7 3.9 %all-to-all-done.refs_0_ = f32[4,72,256]{2,1,0:T(8,128)S(1)} async-done(((f32[4,72,256]{2,1,0:T(8,128)}), f32[4,72,256]{2,1,0:T(8,128)S(1)}, u32[]{:S(2)}, u32[]{:S(2)}) %all-to-all-start) | async-done | bytes 294944 | tf_op jit(solution)/shard_map/all_to_all | solution.py:290
  14.6 1.8 %shard_map.183 = f32[128,2,256]{2,1,0:T(2,128)} custom-call(f32[4,72,256]{2,1,0:T(8,128)S(1)} %all-to-all-done.refs_0_, f32[2,16,256]{2,1,0:T(8,128)S(1)} %pad_maximum_fusion.3.refs_1_, f32[1,256]{1,0:T(1,128)S(1)} %broadcast_select_fusion.1.refs_2_, bf16[2,256,512]{2,1,0:T(8,128)(2,1)S(1)} %copy-done.2), custom_call_target="tpu_custom_call" | custom-call | tf_op jit(solution)/shard_map/pallas_call | solution.py:278
  16.4 16.7 %all-to-all-start.1 = ((f32[128,2,256]{2,1,0:T(2,128)}), f32[128,2,256]{2,1,0:T(2,128)S(1)}, u32[]{:S(2)}, u32[]{:S(2)}) async-start(f32[128,2,256]{2,1,0:T(2,128)} %shard_map.183), calls=%async_computation.1 | async-start | bytes 524288 | tf_op jit(solution)/shard_map/all_to_all | solution.py:290
  33.3 0.1 pad.4.refs_2_
  33.4 14.0 %all-to-all-done.1 = f32[128,2,256]{2,1,0:T(2,128)S(1)} async-done(((f32[128,2,256]{2,1,0:T(2,128)}), f32[128,2,256]{2,1,0:T(2,128)S(1)}, u32[]{:S(2)}, u32[]{:S(2)}) %all-to-all-start.1) | async-done | bytes 262176 | tf_op jit(solution)/shard_map/all_to_all | solution.py:290
  47.4 0.2 reshape.551.refs_0_
  47.7 0.9 shard_map.184
  48.6 0.8 reshape.552
  49.4 6.8 %all-to-all-start.2 = ((bf16[128,2,384]{2,1,0:T(2,128)(2,1)}), bf16[128,2,384]{2,1,0:T(2,128)(2,1)S(1)}, u32[]{:S(2)}, u32[]{:S(2)}) async-start(bf16[128,2,384]{2,1,0:T(2,128)(2,1)} %reshape.552), calls=%async_computation.2 | async-start | bytes 393216 | tf_op jit(solution)/shard_map/all_to_all | solution.py:290
  56.2 0.1 stack.74
  56.3 0.1 copy.28.refs_4_
  56.4 0.1 copy.29.refs_5_
  56.5 0.1 pad.38.clone
  56.6 2.1 %collective-permute-start = (f32[2,2,256]{2,1,0:T(2,128)S(1)}, f32[2,2,256]{2,1,0:T(2,128)S(1)}, u32[]{:S(2)}, u32[]{:S(2)}) collective-permute-start(f32[2,2,256]{2,1,0:T(2,128)S(1)} %get-tuple-element.20), channel_id=1, source_target_pairs={{0,1},{1,2},{2,3},{3,4},{4,5},{5,6},{6,7},{7,8},{8,9},{9,10},{10,1... | collective-permute-start | bytes 12296 | tf_op jit(solution)/shard_map/ppermute | solution.py:294
  58.7 3.5 %collective-permute-start.1 = (f32[2,2,256]{2,1,0:T(2,128)S(1)}, f32[2,2,256]{2,1,0:T(2,128)S(1)}, u32[]{:S(2)}, u32[]{:S(2)}) collective-permute-start(f32[2,2,256]{2,1,0:T(2,128)S(1)} %get-tuple-element.21), channel_id=1, source_target_pairs={{0,31},{1,0},{2,1},{3,2},{4,3},{5,4},{6,5},{7,6},{8,7},{9,8},{10,9... | collective-permute-start | bytes 12296 | tf_op jit(solution)/shard_map/ppermute | solution.py:294
  62.2 7.0 %all-to-all-done.2 = bf16[128,2,384]{2,1,0:T(2,128)(2,1)S(1)} async-done(((bf16[128,2,384]{2,1,0:T(2,128)(2,1)}), bf16[128,2,384]{2,1,0:T(2,128)(2,1)S(1)}, u32[]{:S(2)}, u32[]{:S(2)}) %all-to-all-start.2) | async-done | bytes 196640 | tf_op jit(solution)/shard_map/all_to_all | solution.py:290
  69.2 0.1 reshape.553.refs_0_
  69.3 2.0 %shard_map.185 = f32[288,384]{1,0:T(8,128)} custom-call(bf16[4,64,384]{2,1,0:T(8,128)(2,1)S(1)} %reshape.553.refs_0_, f32[2,16,384]{2,1,0:T(8,128)S(1)} %pad_maximum_fusion.2.refs_1_, f32[1,384]{1,0:T(1,128)S(1)} %select_n.202.refs_2_, bf16[256,768]{1,0:T(8,128)(2,1)S(1)} %copy-done.4), custom_call_target="tpu_custom_call" | custom-call | tf_op jit(solution)/shard_map/pallas_call | solution.py:278
  71.3 0.1 slice.232
  71.5 0.1 convert_element_type.95
  71.6 0.1 slice.292
  71.7 0.1 convert_element_type.97
  71.8 0.1 convert_element_type.96
  71.8 0.1 convert_element_type.98
  71.9 0.1 slice.294
  72.0 0.1 convert_element_type.99
  72.1 0.1 convert_element_type.100
  72.2 0.1 maximum_convert_fusion
  72.2 0.1 maximum_convert_fusion.1
  72.3 0.1 copy.20
  72.4 0.1 copy.21
  72.6 0.1 pad_maximum_fusion
  72.7 0.1 fusion.30
  72.8 0.1 fusion.31
  72.9 0.1 fusion.32
  73.0 3.7 %all-to-all-start.3 = ((f32[4,72,384]{2,1,0:T(8,128)}), f32[4,72,384]{2,1,0:T(8,128)S(1)}, u32[]{:S(2)}, u32[]{:S(2)}) async-start(f32[4,72,384]{2,1,0:T(8,128)} %bitcast.7), calls=%async_computation.3 | async-start | bytes 884736 | tf_op jit(solution)/shard_map/all_to_all | solution.py:290
  76.7 0.1 fusion.33
  76.8 0.1 maximum_bitcast_fusion.5
  77.3 0.7 stack.73
  78.0 7.6 %all-to-all-done.3.refs_0_ = f32[4,72,384]{2,1,0:T(8,128)S(1)} async-done(((f32[4,72,384]{2,1,0:T(8,128)}), f32[4,72,384]{2,1,0:T(8,128)S(1)}, u32[]{:S(2)}, u32[]{:S(2)}) %all-to-all-start.3) | async-done | bytes 442400 | tf_op jit(solution)/shard_map/all_to_all | solution.py:290
  85.7 7.2 %shard_map.186 = (f32[72,384]{1,0:T(8,128)S(1)}, f32[256,384]{1,0:T(8,128)S(1)}, f32[256,128]{1,0:T(8,128)}) custom-call(f32[4,72,384]{2,1,0:T(8,128)S(1)} %all-to-all-done.3.refs_0_, f32[288,384]{1,0:T(8,128)S(1)} %bitcast.82, f32[64,256]{1,0:T(8,128)S(1)} %bitcast.84, f32[64,64]{1,0:T(8,128)S(1)} %bitcast_convert_fusion.refs_3_, ...), custom_call_target="tpu_custom_call" | custom-call | tf_op jit(solution)/shard_map/pallas_call | solution.py:278
  92.8 3.5 %all-to-all-start.4 = ((f32[16,16,128]{2,1,0:T(8,128)}), f32[16,16,128]{2,1,0:T(8,128)S(1)}, u32[]{:S(2)}, u32[]{:S(2)}) async-start(f32[16,16,128]{2,1,0:T(8,128)} %bitcast.38), calls=%async_computation.4 | async-start | bytes 262144 | tf_op jit(solution)/shard_map/all_to_all | solution.py:290
  96.4 0.1 fusion.36
  96.5 0.6 fusion.34
  97.1 8.0 %all-to-all-done.4.refs_0_ = f32[16,16,128]{2,1,0:T(8,128)S(1)} async-done(((f32[16,16,128]{2,1,0:T(8,128)}), f32[16,16,128]{2,1,0:T(8,128)S(1)}, u32[]{:S(2)}, u32[]{:S(2)}) %all-to-all-start.4) | async-done | bytes 131104 | tf_op jit(solution)/shard_map/all_to_all | solution.py:290
  105.1 0.7 shard_map.187
  105.8 5.0 %all-to-all-start.5 = ((f32[32,16,128]{2,1,0:T(8,128)}), f32[32,16,128]{2,1,0:T(8,128)S(1)}, u32[]{:S(2)}, u32[]{:S(2)}) async-start(f32[32,16,128]{2,1,0:T(8,128)} %bitcast.39), calls=%async_computation.5 | async-start | bytes 524288 | tf_op jit(solution)/shard_map/all_to_all | solution.py:290
  110.8 0.2 fusion.28
  111.4 2.7 %fusion.4 = (f32[1,32,256]{2,1,0:T(8,128)S(1)}, f32[1,32,256]{2,1,0:T(8,128)S(1)}) fusion(f32[32,384]{1,0:T(8,128)S(1)} %bitcast.101, f32[32,255]{1,0:T(8,128)S(1)} %slice.329, f32[32,1]{1,0:T(8,128)S(1)} %slice.328, f32[32,1]{1,0:T(8,128)S(1)} %slice.332, f32[32,255]{1,0:T(8,128)S(1)} %slice.331, f32[72,384]{1,0:T(8,128)S(1)} %get-tuple-element.22, ...), kind=kLoop, calls=%fused_computation.27 | loop fusion | flops 147456 | bytes 327696 | tf_op jit(solution)/shard_map/stack | solution.py:373
  114.1 0.6 pad_maximum_fusion.1
  114.7 9.4 %all-to-all-done.5.refs_0_ = f32[32,16,128]{2,1,0:T(8,128)S(1)} async-done(((f32[32,16,128]{2,1,0:T(8,128)}), f32[32,16,128]{2,1,0:T(8,128)S(1)}, u32[]{:S(2)}, u32[]{:S(2)}) %all-to-all-start.5) | async-done | bytes 262176 | tf_op jit(solution)/shard_map/all_to_all | solution.py:290
  124.1 1.0 shard_map.188
  (72 shorter events, 1.0 us)
Async XLA Ops:
  0.6 0.8 copy-start
  1.5 0.8 copy-start.9
  3.2 11.4 %copy-start.2 = (bf16[2,256,512]{2,1,0:T(8,128)(2,1)S(1)}, bf16[2,256,512]{2,1,0:T(8,128)(2,1)}, u32[]{:S(2)}) copy-start(bf16[2,256,512]{2,1,0:T(8,128)(2,1)} %constant.221.clone.refs_3_) | copy-start | bytes 1572868
  3.2 11.4 %all-to-all-start = ((f32[4,72,256]{2,1,0:T(8,128)}), f32[4,72,256]{2,1,0:T(8,128)S(1)}, u32[]{:S(2)}, u32[]{:S(2)}) async-start(f32[4,72,256]{2,1,0:T(8,128)} %bitcast.2), calls=%async_computation | async-start | bytes 589824 | tf_op jit(solution)/shard_map/all_to_all | solution.py:290
  7.6 0.8 copy-start.1
  8.6 0.7 copy-start.14
  9.3 0.7 copy-start.13
  10.0 0.7 copy-start.11
  16.4 31.2 %copy-start.7 = (f32[2,32,256]{2,1,0:T(8,128)S(1)}, f32[2,32,256]{2,1,0:T(8,128)}, u32[]{:S(2)}) copy-start(f32[2,32,256]{2,1,0:T(8,128)} %constant.223.clone.refs_4_) | copy-start | bytes 196612
  16.4 31.2 %copy-start.8 = (f32[2,32,256]{2,1,0:T(8,128)S(1)}, f32[2,32,256]{2,1,0:T(8,128)}, u32[]{:S(2)}) copy-start(f32[2,32,256]{2,1,0:T(8,128)} %constant.226.clone.refs_7_) | copy-start | bytes 196612
  16.4 31.2 %copy-start.10 = (bf16[2,64,64]{2,1,0:T(8,128)(2,1)S(1)}, bf16[2,64,64]{2,1,0:T(8,128)(2,1)}, u32[]{:S(2)}) copy-start(bf16[2,64,64]{2,1,0:T(8,128)(2,1)} %constant.227.clone.refs_8_) | copy-start | bytes 49156
  16.4 31.0 %all-to-all-start.1 = ((f32[128,2,256]{2,1,0:T(2,128)}), f32[128,2,256]{2,1,0:T(2,128)S(1)}, u32[]{:S(2)}, u32[]{:S(2)}) async-start(f32[128,2,256]{2,1,0:T(2,128)} %shard_map.183), calls=%async_computation.1 | async-start | bytes 524288 | tf_op jit(solution)/shard_map/all_to_all | solution.py:290
  33.1 14.5 %copy-start.3 = (bf16[2,256,512]{2,1,0:T(8,128)(2,1)S(1)}, bf16[2,256,512]{2,1,0:T(8,128)(2,1)}, u32[]{:S(2)}) copy-start(bf16[2,256,512]{2,1,0:T(8,128)(2,1)} %constant.225.clone.refs_6_) | copy-start | bytes 1572868
  33.4 14.3 %copy-start.5 = (bf16[2,256,256]{2,1,0:T(8,128)(2,1)S(1)}, bf16[2,256,256]{2,1,0:T(8,128)(2,1)}, u32[]{:S(2)}) copy-start(bf16[2,256,256]{2,1,0:T(8,128)(2,1)} %constant.224.clone.refs_5_) | copy-start | bytes 786436
  33.4 14.3 %copy-start.6 = (bf16[2,128,64]{2,1,0:T(8,128)(2,1)S(1)}, bf16[2,128,64]{2,1,0:T(8,128)(2,1)}, u32[]{:S(2)}) copy-start(bf16[2,128,64]{2,1,0:T(8,128)(2,1)} %constant.222.clone.refs_3_) | copy-start | bytes 98308
  49.3 6.8 %copy-start.15 = (bf16[2,64]{1,0:T(2,128)(2,1)S(1)}, bf16[2,64]{1,0:T(2,128)(2,1)}, u32[]{:S(2)}) copy-start(bf16[2,64]{1,0:T(2,128)(2,1)} %param.20) | copy-start | bytes 772
  49.4 7.2 %copy-start.12 = (bf16[1,64,64]{2,1,0:T(8,128)(2,1)S(1)}, bf16[1,64,64]{2,1,0:T(8,128)(2,1)}, u32[]{:S(2)}) copy-start(bf16[1,64,64]{2,1,0:T(8,128)(2,1)} %param.19) | copy-start | bytes 24580
  49.4 19.9 %all-to-all-start.2 = ((bf16[128,2,384]{2,1,0:T(2,128)(2,1)}), bf16[128,2,384]{2,1,0:T(2,128)(2,1)S(1)}, u32[]{:S(2)}, u32[]{:S(2)}) async-start(bf16[128,2,384]{2,1,0:T(2,128)(2,1)} %reshape.552), calls=%async_computation.2 | async-start | bytes 393216 | tf_op jit(solution)/shard_map/all_to_all | solution.py:290
  56.2 13.1 %copy-start.4 = (bf16[256,768]{1,0:T(8,128)(2,1)S(1)}, bf16[256,768]{1,0:T(8,128)(2,1)}, u32[]{:S(2)}) copy-start(bf16[256,768]{1,0:T(8,128)(2,1)} %constant.228.clone.refs_3_) | copy-start | bytes 1179652
  56.6 16.0 %collective-permute-start = (f32[2,2,256]{2,1,0:T(2,128)S(1)}, f32[2,2,256]{2,1,0:T(2,128)S(1)}, u32[]{:S(2)}, u32[]{:S(2)}) collective-permute-start(f32[2,2,256]{2,1,0:T(2,128)S(1)} %get-tuple-element.20), channel_id=1, source_target_pairs={{0,1},{1,2},{2,3},{3,4},{4,5},{5,6},{6,7},{7,8},{8,9},{9,10},{10,1... | collective-permute-start | bytes 12296 | tf_op jit(solution)/shard_map/ppermute | solution.py:294
  58.7 13.9 %collective-permute-start.1 = (f32[2,2,256]{2,1,0:T(2,128)S(1)}, f32[2,2,256]{2,1,0:T(2,128)S(1)}, u32[]{:S(2)}, u32[]{:S(2)}) collective-permute-start(f32[2,2,256]{2,1,0:T(2,128)S(1)} %get-tuple-element.21), channel_id=1, source_target_pairs={{0,31},{1,0},{2,1},{3,2},{4,3},{5,4},{6,5},{7,6},{8,7},{9,8},{10,9... | collective-permute-start | bytes 12296 | tf_op jit(solution)/shard_map/ppermute | solution.py:294
  73.0 12.6 %all-to-all-start.3 = ((f32[4,72,384]{2,1,0:T(8,128)}), f32[4,72,384]{2,1,0:T(8,128)S(1)}, u32[]{:S(2)}, u32[]{:S(2)}) async-start(f32[4,72,384]{2,1,0:T(8,128)} %bitcast.7), calls=%async_computation.3 | async-start | bytes 884736 | tf_op jit(solution)/shard_map/all_to_all | solution.py:290
  92.8 12.2 %all-to-all-start.4 = ((f32[16,16,128]{2,1,0:T(8,128)}), f32[16,16,128]{2,1,0:T(8,128)S(1)}, u32[]{:S(2)}, u32[]{:S(2)}) async-start(f32[16,16,128]{2,1,0:T(8,128)} %bitcast.38), calls=%async_computation.4 | async-start | bytes 262144 | tf_op jit(solution)/shard_map/all_to_all | solution.py:290
  105.8 18.3 %all-to-all-start.5 = ((f32[32,16,128]{2,1,0:T(8,128)}), f32[32,16,128]{2,1,0:T(8,128)S(1)}, u32[]{:S(2)}, u32[]{:S(2)}) async-start(f32[32,16,128]{2,1,0:T(8,128)} %bitcast.39), calls=%async_computation.5 | async-start | bytes 524288 | tf_op jit(solution)/shard_map/all_to_all | solution.py:290

commit v4 on v3

--- a/solution.py
+++ b/solution.py
@@ -19,7 +19,8 @@
 ROWS, COLS = 32, 256
 NX, NY = WA * ROWS, HA * COLS
 TWO_PI = 2.0 * math.pi
-COL_ID = np.concatenate([np.arange(256), [-1, 256]])
+COL_ID = np.concatenate([np.arange(257), np.zeros(126, np.int64), [-1]])
+COL_USED = np.concatenate([np.ones(257), np.zeros(126), [1]])
 
 
 def bf(table):
@@ -80,10 +81,10 @@
 
     ang = TWO_PI * (np.outer(k2, COL_ID) % 256) / 256
     tk = np.zeros((128, 2, 2, 384))
-    tk[:, 0, 0, :258] = 2 * np.cos(ang)
-    tk[:, 1, 0, :258] = -2 * np.sin(ang)
-    tk[:, 0, 1, :258] = 2 * np.sin(ang)
-    tk[:, 1, 1, :258] = 2 * np.cos(ang)
+    tk[:, 0, 0] = 2 * np.cos(ang) * COL_USED
+    tk[:, 1, 0] = -2 * np.sin(ang) * COL_USED
+    tk[:, 0, 1] = 2 * np.sin(ang) * COL_USED
+    tk[:, 1, 1] = 2 * np.cos(ang) * COL_USED
     tk = tk.reshape(32, 4, 2, 768).transpose(1, 0, 2, 3).reshape(256, 768)
     return dict(t1=pair(t1), d1=pair(d1), tw1=tw1, kr=pair(kr), ik=pair(ik), tw2=tw2, d2=pair(d2), tk=bf(tk))
 
@@ -197,7 +198,7 @@
 
 def y_inverse(got, turn, zero, tk):
     lane = lax.broadcasted_iota(jnp.int32, (1, 384), 1)
-    odd = jnp.where(lane < 256, lane % 2, (lane == 256).astype(jnp.int32)).astype(F32)
+    odd = (lane % 2).astype(F32)
     acc = [None] * 4
     for e in range(4):
         lines = regroup(got[e])
@@ -213,17 +214,47 @@
     return jnp.concatenate(acc, axis=0)
 
 
-def network(proj, planes, center, point, lift18, out_cols):
+def activations(pieces, above, center, below, point, lift18):
     mix = lax.dot_general(point, lift18, (((1,), (0,)), ((), ())), precision=lax.Precision.HIGHEST, preferred_element_type=F32)
     mix_hi, mix_lo = halves(mix)
     mix3 = jnp.concatenate([mix_hi, mix_lo, mix_hi], axis=1)
+    a = lax.broadcasted_iota(jnp.int32, (64, 64), 0)
+    b = lax.broadcasted_iota(jnp.int32, (64, 64), 1)
+    eye = jnp.where(a == b, 1.0, 0.0).astype(BF)
+    lines = jnp.concatenate([p.astype(F32)[:, 272:336] for p in pieces] + [jnp.zeros((4, 64), F32)], axis=0)
+    turned = mm(eye, lines.astype(BF), 1, 1)
+    moved = []
+    for s in range(2):
+        rows = turned[32 * s : 32 * s + 32]
+
+        def side(k):
+            return jnp.concatenate(
+                [rows[30:, 2 * k : 2 * k + 2], rows[:, 2 * k + 2 : 2 * k + 4], rows[:2, 2 * k + 4 : 2 * k + 6]], axis=0
+            )
+
+        mid = jnp.concatenate([above[s], center[32 * s : 32 * s + 32], below[s]], axis=0)
+        full = jnp.concatenate([mid, side(3), jnp.zeros((36, 124), F32), side(0)], axis=1)
+        moved.append(jnp.concatenate([full[:, 383:], full[:, :383]], axis=1))
+        moved.append(full)
+        moved.append(jnp.concatenate([full[:, 1:], full[:, :1]], axis=1))
+    blocks = [
+        jnp.concatenate([m[r : r + 1] for m in moved] + [jnp.zeros((2, 384), F32)], axis=0) for r in range(36)
+    ]
+    result = []
+    for i in range(34):
+        view, view_lo = halves(jnp.concatenate(blocks[i : i + 3], axis=0))
+        result.append(jnp.tanh(mm(mix3, jnp.concatenate([view, view, view_lo], axis=0))).astype(BF))
     mix2 = mix3[:, :48]
-    mix4 = jnp.concatenate([mix2, mix2], axis=0)
+    return jnp.concatenate(blocks, axis=0), jnp.concatenate(result, axis=0), jnp.concatenate([mix2, mix2], axis=0)
+
+
+def network(proj, planes, squash, mix4, center, out_cols):
     taps = [None] * 34
     sums = jnp.zeros((56, 128), F32)
+    rest = jnp.zeros((56, 64), F32)
     for i in range(-1, 33):
-        view, view_lo = halves(planes[(i + 1) * 8 : (i + 4) * 8])
-        t = jnp.tanh(mm(mix3, jnp.concatenate([view, view, view_lo], axis=0)))
+        t_b = squash[(i + 1) * 64 : (i + 2) * 64]
+        t = t_b.astype(F32)
         ids = (64, 66) if i < 0 else (65, 67) if i >= 32 else (i, 32 + i)
         g0 = proj[ids[0] : ids[0] + 1]
         g1 = proj[ids[1] : ids[1] + 1]
@@ -237,18 +268,15 @@
                 piece = tap[a * 8 : a * 8 + 8]
                 taps[k] = piece if taps[k] is None else taps[k] + piece
         if 0 <= i < 32:
-            g = jnp.concatenate([g0[:, :256], g1[:, :256]], axis=0)
-            g_hi, g_lo = halves(g)
+            view, view_lo = halves(planes[(i + 1) * 8 : (i + 4) * 8, :256])
+            g_hi, g_lo = halves(jnp.concatenate([g0[:, :256], g1[:, :256]], axis=0))
             g8 = jnp.concatenate([g_hi.astype(F32), g_lo.astype(F32), jnp.zeros((4, 256), F32)], axis=0).astype(BF)
-            left = jnp.concatenate([view[:, :256], view_lo[:, :256], g8], axis=0)
-            t_hi, t_lo = halves(t[:, :256])
-            sums = sums + (
-                mm(left, jnp.concatenate([gz[:, :256], t_hi], axis=0), 1, 1)
-                + mm(left, jnp.concatenate([gz_lo[:, :256], t_lo], axis=0), 1, 1)
-            )
+            left = jnp.concatenate([view, view_lo, g8], axis=0)
+            sums = sums + mm(left, jnp.concatenate([gz[:, :256], t_b[:, :256]], axis=0), 1, 1)
+            rest = rest + mm(left, gz_lo[:, :256], 1, 1)
     tail = sums[48:50, 64:] + sums[50:52, 64:]
     tail = jnp.concatenate([tail, jnp.zeros((6, 64), F32)], axis=0)
-    sums = sums[:24] + sums[24:48]
+    sums = sums[:24, :64] + sums[24:48, :64] + (rest[:24] + rest[24:48])
     row = lax.broadcasted_iota(jnp.int32, (8, 64), 0)
     lane = lax.broadcasted_iota(jnp.int32, (8, 64), 1)
     for s in range(2):
@@ -258,8 +286,8 @@
             tail = jnp.where((row == 2) & (lane == 2 * s + v), total, tail)
     packed = jnp.concatenate(
         [
-            jnp.concatenate([sums[0:8, :64], sums[8:16, :64]], axis=1),
-            jnp.concatenate([sums[16:24, :64], tail], axis=1),
+            jnp.concatenate([sums[0:8], sums[8:16]], axis=1),
+            jnp.concatenate([sums[16:24], tail], axis=1),
         ],
         axis=0,
     )
@@ -282,6 +310,23 @@
     )(*args)
 
 
+def call_picked(body, out_shapes, index, picked, *args):
+    def kernel(index_ref, picked_ref, *refs):
+        pieces = [picked_ref[index_ref[k]] for k in range(index.shape[0])]
+        outs = body(pieces, *[ref[...] for ref in refs[: len(args)]])
+        for ref, value in zip(refs[len(args) :], outs):
+            ref[...] = value
+
+    vmem = pl.BlockSpec(memory_space=pltpu.VMEM)
+    return pl.pallas_call(
+        kernel,
+        in_specs=[pl.BlockSpec(memory_space=pltpu.SMEM)] + [vmem] * (1 + len(args)),
+        out_specs=[vmem] * len(out_shapes),
+        out_shape=out_shapes,
+        compiler_params=pltpu.CompilerParams(vmem_limit_bytes=40 * 1024 * 1024),
+    )(index, picked, *args)
+
+
 def sds(shape, dtype):
     return jax.ShapeDtypeStruct(shape, dtype)
 
@@ -322,30 +367,6 @@
     to_y = jnp.arange(4)[:, None, None]
     cols = jnp.where(to_y == (yl + 1) % 4, up, down)
     return jnp.pad(cols.reshape(8, 64), ((0, 0), (272, 48)))
-
-
-def velocity_planes(columns, above, velocity, below, yl, w):
-    def side(from_y):
-        def piece(from_w):
-            v = lax.dynamic_index_in_dim(columns, (from_y % 4) * WA + from_w % WA, 0, False)
-            return v.astype(F32).reshape(2, 2, 32).transpose(1, 2, 0)
-
-        return jnp.concatenate([piece(w + 31)[:, 30:], piece(w), piece(w + 1)[:, :2]], axis=1)
-
-    mid = jnp.concatenate([above, velocity, below], axis=1)
-    full = jnp.concatenate([side(yl + 3), mid, side(yl + 1)], axis=2)
-    moved = []
-    for s in range(2):
-        for b in (-1, 0, 1):
-            v = full[s]
-            moved.append(
-                jnp.concatenate(
-                    [v[:, 2 + b : 258 + b], v[:, 1 + b : 2 + b], v[:, 258 + b : 259 + b], jnp.zeros((36, 126), F32)],
-                    axis=1,
-                )
-            )
-    moved += [jnp.zeros((36, 384), F32)] * 2
-    return jnp.stack(moved, axis=1).reshape(288, 384)
 
 
 def lift_matrix(lift, kernels):
@@ -367,8 +388,8 @@
     for s in range(2):
         left, mid, right = taps[:, 3 * s], taps[:, 3 * s + 1], taps[:, 3 * s + 2]
         value = main[s] + m2[s, 0] * main[0] + m2[s, 1] * main[1] + mid[:, :256]
-        value = value + jnp.concatenate([right[:, 256:257], right[:, :255]], axis=1)
-        value = value + jnp.concatenate([left[:, 1:256], left[:, 257:258]], axis=1)
+        value = value + jnp.concatenate([right[:, 383:], right[:, :255]], axis=1)
+        value = value + left[:, 1:257]
         out.append(value)
     return jnp.stack(out)
 
@@ -420,7 +441,7 @@
     sign = jnp.where(x == 0, (1 - 2 * (col % 2)).astype(F32), 0.0)
     zero = jnp.where(x == 0, jnp.ones((1, 384), F32), 0.0)
     ky_lane = (x + 4 * yl + 16 * (4 * w + jnp.arange(128) // 32)).astype(F32)[None, :]
-    cols4 = jnp.asarray(np.concatenate([COL_ID, np.zeros(126, np.int64)]).astype(np.int32))[None, :]
+    cols4 = jnp.asarray(COL_ID.astype(np.int32))[None, :]
     turn4 = turns(klass, cols4 + 1024 * (step % 4) + 256 * yl + NY)
     lift18 = lift_matrix(lift_weight, kernels)
 
@@ -435,23 +456,28 @@
     sent3 = call(
         x_project, sds((256, 384), BF), got2.reshape(4, 64, 256), ky_lane, columns, tab["d1"], tab["tw1"], tab["kr"], tab["ik"], tab["tw2"], tab["d2"]
     )
+    sent3, above, below = lax.optimization_barrier((sent3, above, below))
     got3 = exchange(sent3.reshape(128, 2, 384), ("yl",) + IN_W)
     sent4 = call(y_inverse, sds((288, 384), F32), got3.reshape(4, 64, 384), turn4, zero, tab["tk"])
-    sent4, got3 = lax.optimization_barrier((sent4, got3))
     got4 = exchange(sent4.reshape(4, 72, 384), ("x",))
-    planes = velocity_planes(got3[:, :, 272:336], above, velocity, below, yl, w)
-
-    def last(got, planes, center, point, lift18, out_cols):
-        proj = (got[0] + got[1]) + (got[2] + got[3])
-        taps, packed = network(proj, planes, center, point, lift18, out_cols)
-        return proj, taps, packed
-
     point_f = point.astype(F32)
     out_cols = out_weight.astype(F32).T
+    center = velocity.reshape(64, 256)
+    near = [((yl + dy) % 4) * WA + (w + dw) % WA for dy in (3, 1) for dw in (31, 0, 1)]
+    planes, squash, mix4 = call_picked(
+        activations,
+        (sds((288, 384), F32), sds((34 * 64, 384), BF), sds((128, 48), BF)),
+        jnp.stack(near).astype(jnp.int32), got3, above, center, below, point_f, lift18,
+    )
+
+    def last(got, *rest):
+        proj = (got[0] + got[1]) + (got[2] + got[3])
+        return (proj,) + network(proj, *rest)
+
     proj, taps, packed = call(
         last,
         (sds((72, 384), F32), sds((256, 384), F32), sds((256, 128), F32)),
-        got4, planes, velocity.reshape(64, 256), point_f, lift18, out_cols,
+        got4, planes, squash, mix4, center, out_cols,
     )
     part = exchange(packed.reshape(16, 16, 128), ("yl", "yh", "c"))
     part = call(sum_and_spread, sds((512, 128), F32), part)

time: 126 us -> 123 us (0.976)
  local copies, waits for them, and re-layouts: 9.49 us -> 6.83 us
  Pallas kernels: 14.5 us -> 11.9 us
  starting transfers between devices: 45.6 us -> 47.9 us
    pallas_call x7, Pallas kernels: 14.5 us -> 9.91 us  [call(): pl.pallas_call(kernel, out_shape=out_shapes, compiler_params=pltpu.Compil...]
    all_to_all x6, starting transfers between devices: 40.1 us -> 42.4 us  [exchange(): return lax.all_to_all(value, axes, split_axis=0, concat_axis=0)]
    pallas_call x0 -> x1, Pallas kernels: none -> 1.94 us  [call_picked(): pl.pallas_call(kernel, in_specs=[pl.BlockSpec(memory_space=pltpu.SMEM)] +...]
    unnamed x39 -> x37, local copies, waits for them, and re-layouts: 4.27 us -> 3.49 us
  transfers between devices with their start and end apart: 8 -> 8, of which waited for: 6 -> 6; matrix products, arithmetic and copies ran while one was open for 7% -> 6% of each run, Pallas kernels for 2% -> 2%
where the time goes in v4:
time: 123 us; the launch traced here: 122 us
  waiting for transfers between devices  50.5 us (41%)
  starting transfers between devices  47.9 us (39%)
  Pallas kernels  11.9 us (10%)
  local copies, waits for them, and re-layouts  6.83 us (6%)
  other arithmetic  3.82 us (3%)
    all_to_all x6, waiting for transfers between devices, exchange(): return lax.all_to_all(value, axes, split_axis=0, concat_axis=0)  50.5 us
    all_to_all x6, starting transfers between devices, exchange(): return lax.all_to_all(value, axes, split_axis=0, concat_axis=0)  42.4 us
    pallas_call x7, Pallas kernels, call(): pl.pallas_call(kernel, out_shape=out_shapes, compiler_params=pltpu.Compil...  9.91 us
    ppermute x2, starting transfers between devices, from_row_neighbour(): return lax.ppermute(value, IN_W, [(i, (i + step) % WA) for i in range(WA)])  5.56 us
    unnamed x37, local copies, waits for them, and re-layouts  3.49 us
    another operation x2, other arithmetic, finish_velocity(): return jnp.stack(out)  3.32 us
  transfers between devices with their start and end apart: 8, of which 6 were waited for; matrix products, arithmetic and copies ran while one was open for 6% of the time, Pallas kernels for 2%

profile of v4, /device:TPU:64, one launch (start us, length us, event | category | flops | bytes accessed | tf_op | source)
XLA Modules:
  0.0 122.2 jit_solution(10876129880224994222)
XLA Ops:
  0.6 0.0 copy-start.13
  0.6 0.0 copy-start
  0.7 0.8 copy-done
  1.5 0.8 copy-done.9
  2.3 0.8 shard_map.182
  3.2 4.4 %all-to-all-start = ((f32[4,72,256]{2,1,0:T(8,128)}), f32[4,72,256]{2,1,0:T(8,128)S(1)}, u32[]{:S(2)}, u32[]{:S(2)}) async-start(f32[4,72,256]{2,1,0:T(8,128)} %bitcast.2), calls=%async_computation | async-start | bytes 589824 | tf_op jit(solution)/shard_map/all_to_all | solution.py:335
  7.6 0.1 broadcast_in_dim.40
  7.7 0.1 broadcast_in_dim.41
  7.8 0.7 copy.49
  8.5 0.2 fusion.16
  8.7 0.7 fusion.28
  9.4 5.2 %all-to-all-done.refs_0_ = f32[4,72,256]{2,1,0:T(8,128)S(1)} async-done(((f32[4,72,256]{2,1,0:T(8,128)}), f32[4,72,256]{2,1,0:T(8,128)S(1)}, u32[]{:S(2)}, u32[]{:S(2)}) %all-to-all-start) | async-done | bytes 294944 | tf_op jit(solution)/shard_map/all_to_all | solution.py:335
  14.6 1.0 copy-done.2
  15.7 1.8 %shard_map.183 = f32[128,2,256]{2,1,0:T(2,128)} custom-call(f32[4,72,256]{2,1,0:T(8,128)S(1)} %all-to-all-done.refs_0_, f32[2,16,256]{2,1,0:T(8,128)S(1)} %pad_maximum_fusion.2.refs_1_, f32[1,256]{1,0:T(1,128)S(1)} %broadcast_select_fusion.1.refs_2_, bf16[2,256,512]{2,1,0:T(8,128)(2,1)S(1)} %copy-done.2), custom_call_target="tpu_custom_call" | custom-call | tf_op jit(solution)/shard_map/pallas_call | solution.py:306
  17.5 16.6 %all-to-all-start.1 = ((f32[128,2,256]{2,1,0:T(2,128)}), f32[128,2,256]{2,1,0:T(2,128)S(1)}, u32[]{:S(2)}, u32[]{:S(2)}) async-start(f32[128,2,256]{2,1,0:T(2,128)} %shard_map.183), calls=%async_computation.1 | async-start | bytes 524288 | tf_op jit(solution)/shard_map/all_to_all | solution.py:335
  34.1 0.0 copy-done.13
  34.1 0.0 copy-start.11
  34.1 0.2 fusion.14
  34.3 2.1 %collective-permute-start = (f32[2,2,256]{2,1,0:T(2,128)S(1)}, f32[2,2,256]{2,1,0:T(2,128)S(1)}, u32[]{:S(2)}, u32[]{:S(2)}) collective-permute-start(f32[2,2,256]{2,1,0:T(2,128)S(1)} %get-tuple-element.22), channel_id=1, source_target_pairs={{0,1},{1,2},{2,3},{3,4},{4,5},{5,6},{6,7},{7,8},{8,9},{9,10},{10,1... | collective-permute-start | bytes 12296 | tf_op jit(solution)/shard_map/ppermute | solution.py:339
  36.4 3.5 %collective-permute-start.1 = (f32[2,2,256]{2,1,0:T(2,128)S(1)}, f32[2,2,256]{2,1,0:T(2,128)S(1)}, u32[]{:S(2)}, u32[]{:S(2)}) collective-permute-start(f32[2,2,256]{2,1,0:T(2,128)S(1)} %get-tuple-element.23), channel_id=1, source_target_pairs={{0,31},{1,0},{2,1},{3,2},{4,3},{5,4},{6,5},{7,6},{8,7},{9,8},{10,9... | collective-permute-start | bytes 12296 | tf_op jit(solution)/shard_map/ppermute | solution.py:339
  39.9 0.0 copy-start.4
  39.9 0.1 broadcast_select_fusion
  40.0 0.1 pad.4.refs_2_
  40.1 8.3 %all-to-all-done.1 = f32[128,2,256]{2,1,0:T(2,128)S(1)} async-done(((f32[128,2,256]{2,1,0:T(2,128)}), f32[128,2,256]{2,1,0:T(2,128)S(1)}, u32[]{:S(2)}, u32[]{:S(2)}) %all-to-all-start.1) | async-done | bytes 262176 | tf_op jit(solution)/shard_map/all_to_all | solution.py:335
  48.3 0.2 reshape.524.refs_0_
  48.5 0.0 copy-done.7
  48.5 0.0 copy-done.8
  48.5 0.0 copy-done.10
  48.6 0.0 copy-done.3
  48.6 0.0 copy-done.5
  48.6 0.0 copy-done.6
  48.6 0.9 shard_map.184
  49.5 0.0 copy-start.14
  49.5 0.0 collective-permute-done.refs_0_
  49.5 0.0 collective-permute-done.1.refs_2_
  49.5 0.8 reshape.525
  50.3 9.4 %all-to-all-start.2 = ((bf16[128,2,384]{2,1,0:T(2,128)(2,1)}), bf16[128,2,384]{2,1,0:T(2,128)(2,1)S(1)}, u32[]{:S(2)}, u32[]{:S(2)}) async-start(bf16[128,2,384]{2,1,0:T(2,128)(2,1)} %reshape.525), calls=%async_computation.2 | async-start | bytes 393216 | tf_op jit(solution)/shard_map/all_to_all | solution.py:335
  59.7 0.0 copy-done.11
  59.7 12.8 %all-to-all-done.2.picked_ref = bf16[128,2,384]{2,1,0:T(2,128)(2,1)S(1)} async-done(((bf16[128,2,384]{2,1,0:T(2,128)(2,1)}), bf16[128,2,384]{2,1,0:T(2,128)(2,1)S(1)}, u32[]{:S(2)}, u32[]{:S(2)}) %all-to-all-start.2) | async-done | bytes 196640 | tf_op jit(solution)/shard_map/all_to_all | solution.py:335
  72.6 0.1 reshape.526.refs_0_
  72.7 0.0 copy-done.4
  72.7 2.0 %shard_map.185 = f32[288,384]{1,0:T(8,128)} custom-call(bf16[4,64,384]{2,1,0:T(8,128)(2,1)S(1)} %reshape.526.refs_0_, f32[2,16,384]{2,1,0:T(8,128)S(1)} %pad_maximum_fusion.1.refs_1_, f32[1,384]{1,0:T(1,128)S(1)} %select_n.183.refs_2_, bf16[256,768]{1,0:T(8,128)(2,1)S(1)} %copy-done.4), custom_call_target="tpu_custom_call" | custom-call | tf_op jit(solution)/shard_map/pallas_call | solution.py:306
  74.7 3.5 %all-to-all-start.3 = ((f32[4,72,384]{2,1,0:T(8,128)}), f32[4,72,384]{2,1,0:T(8,128)S(1)}, u32[]{:S(2)}, u32[]{:S(2)}) async-start(f32[4,72,384]{2,1,0:T(8,128)} %bitcast.7), calls=%async_computation.3 | async-start | bytes 884736 | tf_op jit(solution)/shard_map/all_to_all | solution.py:335
  78.2 0.1 stack.70
  78.3 0.1 copy.20.refs_4_
  78.4 0.1 copy.21.refs_5_
  78.5 0.1 stack.34.index_ref
  78.6 0.0 copy-done.1
  78.6 1.9 %shard_map.186 = (f32[288,384]{1,0:T(8,128)S(1)}, bf16[2176,384]{1,0:T(8,128)(2,1)S(1)}, bf16[128,48]{1,0:T(8,128)(2,1)S(1)}) custom-call(s32[6]{0:T(128)S(1)} %stack.34.index_ref, bf16[128,2,384]{2,1,0:T(2,128)(2,1)S(1)} %all-to-all-done.2.picked_ref, f32[2,2,256]{2,1,0:T(2,128)S(1)} %collective-permute-done.refs_0_, f32[64,256]{1,0:T(8,128)S(1)} %bitcast.64, ...), custom_call_target="tpu_custom_call" | custom-call | tf_op jit(solution)/shard_map/pallas_call | solution.py:321
  80.5 6.7 %all-to-all-done.3.refs_0_ = f32[4,72,384]{2,1,0:T(8,128)S(1)} async-done(((f32[4,72,384]{2,1,0:T(8,128)}), f32[4,72,384]{2,1,0:T(8,128)S(1)}, u32[]{:S(2)}, u32[]{:S(2)}) %all-to-all-start.3) | async-done | bytes 442400 | tf_op jit(solution)/shard_map/all_to_all | solution.py:335
  87.3 2.7 %shard_map.187 = (f32[72,384]{1,0:T(8,128)S(1)}, f32[256,384]{1,0:T(8,128)S(1)}, f32[256,128]{1,0:T(8,128)}) custom-call(f32[4,72,384]{2,1,0:T(8,128)S(1)} %all-to-all-done.3.refs_0_, f32[288,384]{1,0:T(8,128)S(1)} %get-tuple-element.27.refs_1_, bf16[2176,384]{1,0:T(8,128)(2,1)S(1)} %get-tuple-element.28.refs_2_, ...), custom_call_target="tpu_custom_call" | custom-call | tf_op jit(solution)/shard_map/pallas_call | solution.py:306
  89.9 3.5 %all-to-all-start.4 = ((f32[16,16,128]{2,1,0:T(8,128)}), f32[16,16,128]{2,1,0:T(8,128)S(1)}, u32[]{:S(2)}, u32[]{:S(2)}) async-start(f32[16,16,128]{2,1,0:T(8,128)} %bitcast.29), calls=%async_computation.4 | async-start | bytes 262144 | tf_op jit(solution)/shard_map/all_to_all | solution.py:335
  93.4 0.1 fusion.31
  93.6 0.6 fusion.29
  94.2 8.0 %all-to-all-done.4.refs_0_ = f32[16,16,128]{2,1,0:T(8,128)S(1)} async-done(((f32[16,16,128]{2,1,0:T(8,128)}), f32[16,16,128]{2,1,0:T(8,128)S(1)}, u32[]{:S(2)}, u32[]{:S(2)}) %all-to-all-start.4) | async-done | bytes 131104 | tf_op jit(solution)/shard_map/all_to_all | solution.py:335
  102.1 0.7 shard_map.188
  102.9 5.0 %all-to-all-start.5 = ((f32[32,16,128]{2,1,0:T(8,128)}), f32[32,16,128]{2,1,0:T(8,128)S(1)}, u32[]{:S(2)}, u32[]{:S(2)}) async-start(f32[32,16,128]{2,1,0:T(8,128)} %bitcast.30), calls=%async_computation.5 | async-start | bytes 524288 | tf_op jit(solution)/shard_map/all_to_all | solution.py:335
  107.9 0.2 fusion.27
  108.1 0.1 slice.188
  108.2 0.1 slice.195
  108.3 2.7 %fusion.4 = (f32[1,32,256]{2,1,0:T(8,128)S(1)}, f32[1,32,256]{2,1,0:T(8,128)S(1)}) fusion(f32[32,384]{1,0:T(8,128)S(1)} %bitcast.79, f32[32,384]{1,0:T(8,128)S(1)} %bitcast.80, f32[32,255]{1,0:T(8,128)S(1)} %slice.189, f32[32,1]{1,0:T(8,128)S(1)} %slice.188, f32[72,384]{1,0:T(8,128)S(1)} %get-tuple-element.30, f32[]{:T(128)} %bitcast.17, f32[]{:T(128)} %bitcast.16, ...), kind=kLoop, calls=%fused_computation.18 | loop fusion | flops 131072 | bytes 327696 | tf_op jit(solution)/shard_map/stack | solution.py:394
  111.0 0.6 pad_maximum_fusion
  111.7 9.5 %all-to-all-done.5.refs_0_ = f32[32,16,128]{2,1,0:T(8,128)S(1)} async-done(((f32[32,16,128]{2,1,0:T(8,128)}), f32[32,16,128]{2,1,0:T(8,128)S(1)}, u32[]{:S(2)}, u32[]{:S(2)}) %all-to-all-start.5) | async-done | bytes 262176 | tf_op jit(solution)/shard_map/all_to_all | solution.py:335
  121.2 1.0 shard_map.189
  (37 shorter events, 0.2 us)
Async XLA Ops:
  0.6 33.4 %copy-start.13 = (s32[384]{0:T(512)S(1)}, s32[384]{0:T(512)}, u32[]{:S(2)}) copy-start(s32[384]{0:T(512)} %constant.203.clone) | copy-start | bytes 4612
  0.6 0.8 copy-start
  1.5 0.8 copy-start.9
  2.3 46.2 %copy-start.7 = (f32[2,32,256]{2,1,0:T(8,128)S(1)}, f32[2,32,256]{2,1,0:T(8,128)}, u32[]{:S(2)}) copy-start(f32[2,32,256]{2,1,0:T(8,128)} %constant.206.clone.refs_4_) | copy-start | bytes 196612
  2.3 46.2 %copy-start.8 = (f32[2,32,256]{2,1,0:T(8,128)S(1)}, f32[2,32,256]{2,1,0:T(8,128)}, u32[]{:S(2)}) copy-start(f32[2,32,256]{2,1,0:T(8,128)} %constant.209.clone.refs_7_) | copy-start | bytes 196612
  2.3 46.2 %copy-start.10 = (bf16[2,64,64]{2,1,0:T(8,128)(2,1)S(1)}, bf16[2,64,64]{2,1,0:T(8,128)(2,1)}, u32[]{:S(2)}) copy-start(bf16[2,64,64]{2,1,0:T(8,128)(2,1)} %constant.210.clone.refs_8_) | copy-start | bytes 49156
  3.2 45.4 %copy-start.3 = (bf16[2,256,512]{2,1,0:T(8,128)(2,1)S(1)}, bf16[2,256,512]{2,1,0:T(8,128)(2,1)}, u32[]{:S(2)}) copy-start(bf16[2,256,512]{2,1,0:T(8,128)(2,1)} %constant.208.clone.refs_6_) | copy-start | bytes 1572868
  3.2 45.4 %copy-start.5 = (bf16[2,256,256]{2,1,0:T(8,128)(2,1)S(1)}, bf16[2,256,256]{2,1,0:T(8,128)(2,1)}, u32[]{:S(2)}) copy-start(bf16[2,256,256]{2,1,0:T(8,128)(2,1)} %constant.207.clone.refs_5_) | copy-start | bytes 786436
  3.2 45.4 %copy-start.6 = (bf16[2,128,64]{2,1,0:T(8,128)(2,1)S(1)}, bf16[2,128,64]{2,1,0:T(8,128)(2,1)}, u32[]{:S(2)}) copy-start(bf16[2,128,64]{2,1,0:T(8,128)(2,1)} %constant.205.clone.refs_3_) | copy-start | bytes 98308
  3.2 11.4 %all-to-all-start = ((f32[4,72,256]{2,1,0:T(8,128)}), f32[4,72,256]{2,1,0:T(8,128)S(1)}, u32[]{:S(2)}, u32[]{:S(2)}) async-start(f32[4,72,256]{2,1,0:T(8,128)} %bitcast.2), calls=%async_computation | async-start | bytes 589824 | tf_op jit(solution)/shard_map/all_to_all | solution.py:335
  14.6 1.0 copy-start.2
  17.5 30.9 %all-to-all-start.1 = ((f32[128,2,256]{2,1,0:T(2,128)}), f32[128,2,256]{2,1,0:T(2,128)S(1)}, u32[]{:S(2)}, u32[]{:S(2)}) async-start(f32[128,2,256]{2,1,0:T(2,128)} %shard_map.183), calls=%async_computation.1 | async-start | bytes 524288 | tf_op jit(solution)/shard_map/all_to_all | solution.py:335
  34.1 25.6 %copy-start.11 = (f32[64,2]{0,1:T(2,128)S(1)}, f32[64,2]{0,1:T(2,128)}, u32[]{:S(2)}) copy-start(f32[64,2]{0,1:T(2,128)} %param.17) | copy-start | bytes 1540
  34.3 15.2 %collective-permute-start = (f32[2,2,256]{2,1,0:T(2,128)S(1)}, f32[2,2,256]{2,1,0:T(2,128)S(1)}, u32[]{:S(2)}, u32[]{:S(2)}) collective-permute-start(f32[2,2,256]{2,1,0:T(2,128)S(1)} %get-tuple-element.22), channel_id=1, source_target_pairs={{0,1},{1,2},{2,3},{3,4},{4,5},{5,6},{6,7},{7,8},{8,9},{9,10},{10,1... | collective-permute-start | bytes 12296 | tf_op jit(solution)/shard_map/ppermute | solution.py:339
  36.4 13.1 %collective-permute-start.1 = (f32[2,2,256]{2,1,0:T(2,128)S(1)}, f32[2,2,256]{2,1,0:T(2,128)S(1)}, u32[]{:S(2)}, u32[]{:S(2)}) collective-permute-start(f32[2,2,256]{2,1,0:T(2,128)S(1)} %get-tuple-element.23), channel_id=1, source_target_pairs={{0,31},{1,0},{2,1},{3,2},{4,3},{5,4},{6,5},{7,6},{8,7},{9,8},{10,9... | collective-permute-start | bytes 12296 | tf_op jit(solution)/shard_map/ppermute | solution.py:339
  39.9 32.7 %copy-start.4 = (bf16[256,768]{1,0:T(8,128)(2,1)S(1)}, bf16[256,768]{1,0:T(8,128)(2,1)}, u32[]{:S(2)}) copy-start(bf16[256,768]{1,0:T(8,128)(2,1)} %constant.211.clone.refs_3_) | copy-start | bytes 1179652
  49.5 28.6 %copy-start.14 = (bf16[2,64]{1,0:T(2,128)(2,1)S(1)}, bf16[2,64]{1,0:T(2,128)(2,1)}, u32[]{:S(2)}) copy-start(bf16[2,64]{1,0:T(2,128)(2,1)} %param.20) | copy-start | bytes 772
  50.3 28.3 %copy-start.12 = (bf16[1,64,64]{2,1,0:T(8,128)(2,1)S(1)}, bf16[1,64,64]{2,1,0:T(8,128)(2,1)}, u32[]{:S(2)}) copy-start(bf16[1,64,64]{2,1,0:T(8,128)(2,1)} %param.19) | copy-start | bytes 24580
  50.3 28.3 %copy-start.1 = (f32[2,32,256]{2,1,0:T(8,128)S(1)}, f32[2,32,256]{2,1,0:T(8,128)}, u32[]{:S(2)}) copy-start(f32[2,32,256]{2,1,0:T(8,128)} %param.15) | copy-start | bytes 196612
  50.3 22.3 %all-to-all-start.2 = ((bf16[128,2,384]{2,1,0:T(2,128)(2,1)}), bf16[128,2,384]{2,1,0:T(2,128)(2,1)S(1)}, u32[]{:S(2)}, u32[]{:S(2)}) async-start(bf16[128,2,384]{2,1,0:T(2,128)(2,1)} %reshape.525), calls=%async_computation.2 | async-start | bytes 393216 | tf_op jit(solution)/shard_map/all_to_all | solution.py:335
  74.7 12.6 %all-to-all-start.3 = ((f32[4,72,384]{2,1,0:T(8,128)}), f32[4,72,384]{2,1,0:T(8,128)S(1)}, u32[]{:S(2)}, u32[]{:S(2)}) async-start(f32[4,72,384]{2,1,0:T(8,128)} %bitcast.7), calls=%async_computation.3 | async-start | bytes 884736 | tf_op jit(solution)/shard_map/all_to_all | solution.py:335
  89.9 12.2 %all-to-all-start.4 = ((f32[16,16,128]{2,1,0:T(8,128)}), f32[16,16,128]{2,1,0:T(8,128)S(1)}, u32[]{:S(2)}, u32[]{:S(2)}) async-start(f32[16,16,128]{2,1,0:T(8,128)} %bitcast.29), calls=%async_computation.4 | async-start | bytes 262144 | tf_op jit(solution)/shard_map/all_to_all | solution.py:335
  102.9 18.3 %all-to-all-start.5 = ((f32[32,16,128]{2,1,0:T(8,128)}), f32[32,16,128]{2,1,0:T(8,128)S(1)}, u32[]{:S(2)}, u32[]{:S(2)}) async-start(f32[32,16,128]{2,1,0:T(8,128)} %bitcast.30), calls=%async_computation.5 | async-start | bytes 524288 | tf_op jit(solution)/shard_map/all_to_all | solution.py:335

commit v5 on v4

--- a/solution.py
+++ b/solution.py
@@ -306,7 +306,7 @@
     return pl.pallas_call(
         kernel,
         out_shape=out_shapes,
-        compiler_params=pltpu.CompilerParams(vmem_limit_bytes=40 * 1024 * 1024),
+        compiler_params=pltpu.CompilerParams(vmem_limit_bytes=12 * 1024 * 1024),
     )(*args)
 
 
@@ -323,7 +323,7 @@
         in_specs=[pl.BlockSpec(memory_space=pltpu.SMEM)] + [vmem] * (1 + len(args)),
         out_specs=[vmem] * len(out_shapes),
         out_shape=out_shapes,
-        compiler_params=pltpu.CompilerParams(vmem_limit_bytes=40 * 1024 * 1024),
+        compiler_params=pltpu.CompilerParams(vmem_limit_bytes=12 * 1024 * 1024),
     )(index, picked, *args)
 
 
@@ -448,17 +448,18 @@
     sent1 = call(pack_first, sds((288, 256), F32), velocity.reshape(64, 256), cotangent.reshape(64, 256))
     got1 = exchange(sent1.reshape(4, 72, 256), ("x",))
     spec = call(y_forward, sds((128, 2, 256), F32), got1, turn1, sign, tab["t1"])
-    spec, bottom, top = lax.optimization_barrier((spec, velocity[:, 30:], velocity[:, :2]))
+    spec, bottom = lax.optimization_barrier((spec, velocity[:, 30:]))
     got2 = exchange(spec, ("yl",) + IN_W)
     above = from_row_neighbour(bottom, 1)
-    below = from_row_neighbour(top, -1)
     columns = columns_to_send(got1, x, yl)
     sent3 = call(
         x_project, sds((256, 384), BF), got2.reshape(4, 64, 256), ky_lane, columns, tab["d1"], tab["tw1"], tab["kr"], tab["ik"], tab["tw2"], tab["d2"]
     )
-    sent3, above, below = lax.optimization_barrier((sent3, above, below))
+    sent3, above, top = lax.optimization_barrier((sent3, above, velocity[:, :2]))
+    below = from_row_neighbour(top, -1)
     got3 = exchange(sent3.reshape(128, 2, 384), ("yl",) + IN_W)
     sent4 = call(y_inverse, sds((288, 384), F32), got3.reshape(4, 64, 384), turn4, zero, tab["tk"])
+    sent4, below = lax.optimization_barrier((sent4, below))
     got4 = exchange(sent4.reshape(4, 72, 384), ("x",))
     point_f = point.astype(F32)
     out_cols = out_weight.astype(F32).T

time: 123 us -> 121 us (0.984)
  starting transfers between devices: 47.9 us -> 43.8 us
  waiting for transfers between devices: 50.5 us -> 52.2 us
    all_to_all x6, starting transfers between devices: 42.4 us -> 39.7 us  [exchange(): return lax.all_to_all(value, axes, split_axis=0, concat_axis=0)]
    all_to_all x6, waiting for transfers between devices: 50.5 us -> 52.2 us  [exchange(): return lax.all_to_all(value, axes, split_axis=0, concat_axis=0)]
    ppermute x2, starting transfers between devices: 5.56 us -> 4.07 us  [from_row_neighbour(): return lax.ppermute(value, IN_W, [(i, (i + step) % WA) for i in range(WA)])]
  transfers between devices with their start and end apart: 8 -> 8, of which waited for: 6 -> 6; matrix products, arithmetic and copies ran while one was open for 6% -> 6% of each run, Pallas kernels for 2% -> 4%
where the time goes in v5:
time: 121 us; the launch traced here: 120 us
  waiting for transfers between devices  52.2 us (43%)
  starting transfers between devices  43.8 us (36%)
  Pallas kernels  11.9 us (10%)
  local copies, waits for them, and re-layouts  6.82 us (6%)
  other arithmetic  3.82 us (3%)
    all_to_all x6, waiting for transfers between devices, exchange(): return lax.all_to_all(value, axes, split_axis=0, concat_axis=0)  52.2 us
    all_to_all x6, starting transfers between devices, exchange(): return lax.all_to_all(value, axes, split_axis=0, concat_axis=0)  39.7 us
    pallas_call x7, Pallas kernels, call(): pl.pallas_call(kernel, out_shape=out_shapes, compiler_params=pltpu.Compil...  9.92 us
    ppermute x2, starting transfers between devices, from_row_neighbour(): return lax.ppermute(value, IN_W, [(i, (i + step) % WA) for i in range(WA)])  4.07 us
    unnamed x37, local copies, waits for them, and re-layouts  3.49 us
    another operation x2, other arithmetic, finish_velocity(): return jnp.stack(out)  3.32 us
  transfers between devices with their start and end apart: 8, of which 6 were waited for; matrix products, arithmetic and copies ran while one was open for 6% of the time, Pallas kernels for 4%

profile of v5, /device:TPU:64, one launch (start us, length us, event | category | flops | bytes accessed | tf_op | source)
XLA Modules:
  0.0 119.7 jit_solution(17655922200081369426)
XLA Ops:
  0.6 0.0 copy-start.11
  0.6 0.0 copy-start
  0.7 0.8 copy-done
  1.5 0.8 copy-done.9
  2.3 0.8 shard_map.182
  3.2 4.4 %all-to-all-start = ((f32[4,72,256]{2,1,0:T(8,128)}), f32[4,72,256]{2,1,0:T(8,128)S(1)}, u32[]{:S(2)}, u32[]{:S(2)}) async-start(f32[4,72,256]{2,1,0:T(8,128)} %bitcast.2), calls=%async_computation | async-start | bytes 589824 | tf_op jit(solution)/shard_map/all_to_all | solution.py:335
  7.6 0.1 broadcast_in_dim.40
  7.7 0.1 broadcast_in_dim.41
  7.8 0.7 copy.49
  8.5 0.2 fusion.16
  8.7 0.7 fusion.28
  9.4 5.2 %all-to-all-done.refs_0_ = f32[4,72,256]{2,1,0:T(8,128)S(1)} async-done(((f32[4,72,256]{2,1,0:T(8,128)}), f32[4,72,256]{2,1,0:T(8,128)S(1)}, u32[]{:S(2)}, u32[]{:S(2)}) %all-to-all-start) | async-done | bytes 294944 | tf_op jit(solution)/shard_map/all_to_all | solution.py:335
  14.6 1.0 copy-done.2
  15.7 1.8 %shard_map.183 = f32[128,2,256]{2,1,0:T(2,128)} custom-call(f32[4,72,256]{2,1,0:T(8,128)S(1)} %all-to-all-done.refs_0_, f32[2,16,256]{2,1,0:T(8,128)S(1)} %pad_maximum_fusion.2.refs_1_, f32[1,256]{1,0:T(1,128)S(1)} %broadcast_select_fusion.1.refs_2_, bf16[2,256,512]{2,1,0:T(8,128)(2,1)S(1)} %copy-done.2), custom_call_target="tpu_custom_call" | custom-call | tf_op jit(solution)/shard_map/pallas_call | solution.py:306
  17.5 16.6 %all-to-all-start.1 = ((f32[128,2,256]{2,1,0:T(2,128)}), f32[128,2,256]{2,1,0:T(2,128)S(1)}, u32[]{:S(2)}, u32[]{:S(2)}) async-start(f32[128,2,256]{2,1,0:T(2,128)} %shard_map.183), calls=%async_computation.1 | async-start | bytes 524288 | tf_op jit(solution)/shard_map/all_to_all | solution.py:335
  34.1 0.0 copy-start.13
  34.1 0.0 copy-done.11
  34.1 2.1 %collective-permute-start = (f32[2,2,256]{2,1,0:T(2,128)S(1)}, f32[2,2,256]{2,1,0:T(2,128)S(1)}, u32[]{:S(2)}, u32[]{:S(2)}) collective-permute-start(f32[2,2,256]{2,1,0:T(2,128)S(1)} %get-tuple-element.23), channel_id=1, source_target_pairs={{0,1},{1,2},{2,3},{3,4},{4,5},{5,6},{6,7},{7,8},{8,9},{9,10},{10,1... | collective-permute-start | bytes 12296 | tf_op jit(solution)/shard_map/ppermute | solution.py:339
  36.2 0.1 broadcast_select_fusion
  36.3 0.1 pad.4.refs_2_
  36.4 12.0 %all-to-all-done.1 = f32[128,2,256]{2,1,0:T(2,128)S(1)} async-done(((f32[128,2,256]{2,1,0:T(2,128)}), f32[128,2,256]{2,1,0:T(2,128)S(1)}, u32[]{:S(2)}, u32[]{:S(2)}) %all-to-all-start.1) | async-done | bytes 262176 | tf_op jit(solution)/shard_map/all_to_all | solution.py:335
  48.3 0.2 reshape.524.refs_0_
  48.5 0.0 copy-done.7
  48.5 0.0 copy-done.8
  48.5 0.0 copy-done.10
  48.6 0.0 copy-done.3
  48.6 0.0 copy-done.5
  48.6 0.0 copy-done.6
  48.6 0.9 shard_map.184
  49.5 0.0 copy-start.14
  49.5 0.0 collective-permute-done.refs_0_
  49.5 0.8 reshape.525
  50.3 6.8 %all-to-all-start.2 = ((bf16[128,2,384]{2,1,0:T(2,128)(2,1)}), bf16[128,2,384]{2,1,0:T(2,128)(2,1)S(1)}, u32[]{:S(2)}, u32[]{:S(2)}) async-start(bf16[128,2,384]{2,1,0:T(2,128)(2,1)} %reshape.525), calls=%async_computation.2 | async-start | bytes 393216 | tf_op jit(solution)/shard_map/all_to_all | solution.py:335
  57.1 0.0 copy-done.13
  57.1 0.2 fusion.14
  57.3 2.0 %collective-permute-start.1 = (f32[2,2,256]{2,1,0:T(2,128)S(1)}, f32[2,2,256]{2,1,0:T(2,128)S(1)}, u32[]{:S(2)}, u32[]{:S(2)}) collective-permute-start(f32[2,2,256]{2,1,0:T(2,128)S(1)} %get-tuple-element.25), channel_id=1, source_target_pairs={{0,31},{1,0},{2,1},{3,2},{4,3},{5,4},{6,5},{7,6},{8,7},{9,8},{10,9... | collective-permute-start | bytes 12296 | tf_op jit(solution)/shard_map/ppermute | solution.py:339
  59.3 10.8 %all-to-all-done.2.picked_ref = bf16[128,2,384]{2,1,0:T(2,128)(2,1)S(1)} async-done(((bf16[128,2,384]{2,1,0:T(2,128)(2,1)}), bf16[128,2,384]{2,1,0:T(2,128)(2,1)S(1)}, u32[]{:S(2)}, u32[]{:S(2)}) %all-to-all-start.2) | async-done | bytes 196640 | tf_op jit(solution)/shard_map/all_to_all | solution.py:335
  70.1 0.1 reshape.526.refs_0_
  70.2 0.0 copy-done.4
  70.2 2.0 %shard_map.185 = f32[288,384]{1,0:T(8,128)} custom-call(bf16[4,64,384]{2,1,0:T(8,128)(2,1)S(1)} %reshape.526.refs_0_, f32[2,16,384]{2,1,0:T(8,128)S(1)} %pad_maximum_fusion.1.refs_1_, f32[1,384]{1,0:T(1,128)S(1)} %select_n.183.refs_2_, bf16[256,768]{1,0:T(8,128)(2,1)S(1)} %copy-done.4), custom_call_target="tpu_custom_call" | custom-call | tf_op jit(solution)/shard_map/pallas_call | solution.py:306
  72.2 0.0 collective-permute-done.1.refs_2_
  72.2 3.5 %all-to-all-start.3 = ((f32[4,72,384]{2,1,0:T(8,128)}), f32[4,72,384]{2,1,0:T(8,128)S(1)}, u32[]{:S(2)}, u32[]{:S(2)}) async-start(f32[4,72,384]{2,1,0:T(8,128)} %bitcast.7), calls=%async_computation.3 | async-start | bytes 884736 | tf_op jit(solution)/shard_map/all_to_all | solution.py:335
  75.7 0.0 copy-done.14
  75.8 0.1 stack.70
  75.9 0.1 copy.20.refs_4_
  76.0 0.1 copy.21.refs_5_
  76.1 0.1 stack.34.index_ref
  76.1 0.0 copy-done.12
  76.2 1.9 %shard_map.186 = (f32[288,384]{1,0:T(8,128)S(1)}, bf16[2176,384]{1,0:T(8,128)(2,1)S(1)}, bf16[128,48]{1,0:T(8,128)(2,1)S(1)}) custom-call(s32[6]{0:T(128)S(1)} %stack.34.index_ref, bf16[128,2,384]{2,1,0:T(2,128)(2,1)S(1)} %all-to-all-done.2.picked_ref, f32[2,2,256]{2,1,0:T(2,128)S(1)} %collective-permute-done.refs_0_, f32[64,256]{1,0:T(8,128)S(1)} %bitcast.64, ...), custom_call_target="tpu_custom_call" | custom-call | tf_op jit(solution)/shard_map/pallas_call | solution.py:321
  78.1 6.8 %all-to-all-done.3.refs_0_ = f32[4,72,384]{2,1,0:T(8,128)S(1)} async-done(((f32[4,72,384]{2,1,0:T(8,128)}), f32[4,72,384]{2,1,0:T(8,128)S(1)}, u32[]{:S(2)}, u32[]{:S(2)}) %all-to-all-start.3) | async-done | bytes 442400 | tf_op jit(solution)/shard_map/all_to_all | solution.py:335
  84.9 2.7 %shard_map.187 = (f32[72,384]{1,0:T(8,128)S(1)}, f32[256,384]{1,0:T(8,128)S(1)}, f32[256,128]{1,0:T(8,128)}) custom-call(f32[4,72,384]{2,1,0:T(8,128)S(1)} %all-to-all-done.3.refs_0_, f32[288,384]{1,0:T(8,128)S(1)} %get-tuple-element.29.refs_1_, bf16[2176,384]{1,0:T(8,128)(2,1)S(1)} %get-tuple-element.30.refs_2_, ...), custom_call_target="tpu_custom_call" | custom-call | tf_op jit(solution)/shard_map/pallas_call | solution.py:306
  87.5 3.5 %all-to-all-start.4 = ((f32[16,16,128]{2,1,0:T(8,128)}), f32[16,16,128]{2,1,0:T(8,128)S(1)}, u32[]{:S(2)}, u32[]{:S(2)}) async-start(f32[16,16,128]{2,1,0:T(8,128)} %bitcast.29), calls=%async_computation.4 | async-start | bytes 262144 | tf_op jit(solution)/shard_map/all_to_all | solution.py:335
  91.0 0.1 fusion.31
  91.2 0.6 fusion.29
  91.8 8.0 %all-to-all-done.4.refs_0_ = f32[16,16,128]{2,1,0:T(8,128)S(1)} async-done(((f32[16,16,128]{2,1,0:T(8,128)}), f32[16,16,128]{2,1,0:T(8,128)S(1)}, u32[]{:S(2)}, u32[]{:S(2)}) %all-to-all-start.4) | async-done | bytes 131104 | tf_op jit(solution)/shard_map/all_to_all | solution.py:335
  99.7 0.7 shard_map.188
  100.5 4.9 %all-to-all-start.5 = ((f32[32,16,128]{2,1,0:T(8,128)}), f32[32,16,128]{2,1,0:T(8,128)S(1)}, u32[]{:S(2)}, u32[]{:S(2)}) async-start(f32[32,16,128]{2,1,0:T(8,128)} %bitcast.30), calls=%async_computation.5 | async-start | bytes 524288 | tf_op jit(solution)/shard_map/all_to_all | solution.py:335
  105.4 0.2 fusion.27
  105.7 0.1 slice.188
  105.7 0.1 slice.195
  105.9 2.7 %fusion.4 = (f32[1,32,256]{2,1,0:T(8,128)S(1)}, f32[1,32,256]{2,1,0:T(8,128)S(1)}) fusion(f32[32,384]{1,0:T(8,128)S(1)} %bitcast.79, f32[32,384]{1,0:T(8,128)S(1)} %bitcast.80, f32[32,255]{1,0:T(8,128)S(1)} %slice.189, f32[32,1]{1,0:T(8,128)S(1)} %slice.188, f32[72,384]{1,0:T(8,128)S(1)} %get-tuple-element.32, f32[]{:T(128)} %bitcast.17, f32[]{:T(128)} %bitcast.16, ...), kind=kLoop, calls=%fused_computation.18 | loop fusion | flops 131072 | bytes 327696 | tf_op jit(solution)/shard_map/stack | solution.py:394
  108.6 0.6 pad_maximum_fusion
  109.2 9.5 %all-to-all-done.5.refs_0_ = f32[32,16,128]{2,1,0:T(8,128)S(1)} async-done(((f32[32,16,128]{2,1,0:T(8,128)}), f32[32,16,128]{2,1,0:T(8,128)S(1)}, u32[]{:S(2)}, u32[]{:S(2)}) %all-to-all-start.5) | async-done | bytes 262176 | tf_op jit(solution)/shard_map/all_to_all | solution.py:335
  118.7 1.0 shard_map.189
  (37 shorter events, 0.2 us)
Async XLA Ops:
  0.6 33.4 %copy-start.11 = (f32[64,2]{0,1:T(2,128)S(1)}, f32[64,2]{0,1:T(2,128)}, u32[]{:S(2)}) copy-start(f32[64,2]{0,1:T(2,128)} %param.17) | copy-start | bytes 1540
  0.6 0.8 copy-start
  1.5 0.8 copy-start.9
  2.3 46.2 %copy-start.7 = (f32[2,32,256]{2,1,0:T(8,128)S(1)}, f32[2,32,256]{2,1,0:T(8,128)}, u32[]{:S(2)}) copy-start(f32[2,32,256]{2,1,0:T(8,128)} %constant.206.clone.refs_4_) | copy-start | bytes 196612
  2.3 46.2 %copy-start.8 = (f32[2,32,256]{2,1,0:T(8,128)S(1)}, f32[2,32,256]{2,1,0:T(8,128)}, u32[]{:S(2)}) copy-start(f32[2,32,256]{2,1,0:T(8,128)} %constant.209.clone.refs_7_) | copy-start | bytes 196612
  2.3 46.2 %copy-start.10 = (bf16[2,64,64]{2,1,0:T(8,128)(2,1)S(1)}, bf16[2,64,64]{2,1,0:T(8,128)(2,1)}, u32[]{:S(2)}) copy-start(bf16[2,64,64]{2,1,0:T(8,128)(2,1)} %constant.210.clone.refs_8_) | copy-start | bytes 49156
  3.2 45.4 %copy-start.3 = (bf16[2,256,512]{2,1,0:T(8,128)(2,1)S(1)}, bf16[2,256,512]{2,1,0:T(8,128)(2,1)}, u32[]{:S(2)}) copy-start(bf16[2,256,512]{2,1,0:T(8,128)(2,1)} %constant.208.clone.refs_6_) | copy-start | bytes 1572868
  3.2 45.4 %copy-start.5 = (bf16[2,256,256]{2,1,0:T(8,128)(2,1)S(1)}, bf16[2,256,256]{2,1,0:T(8,128)(2,1)}, u32[]{:S(2)}) copy-start(bf16[2,256,256]{2,1,0:T(8,128)(2,1)} %constant.207.clone.refs_5_) | copy-start | bytes 786436
  3.2 45.4 %copy-start.6 = (bf16[2,128,64]{2,1,0:T(8,128)(2,1)S(1)}, bf16[2,128,64]{2,1,0:T(8,128)(2,1)}, u32[]{:S(2)}) copy-start(bf16[2,128,64]{2,1,0:T(8,128)(2,1)} %constant.205.clone.refs_3_) | copy-start | bytes 98308
  3.2 11.4 %all-to-all-start = ((f32[4,72,256]{2,1,0:T(8,128)}), f32[4,72,256]{2,1,0:T(8,128)S(1)}, u32[]{:S(2)}, u32[]{:S(2)}) async-start(f32[4,72,256]{2,1,0:T(8,128)} %bitcast.2), calls=%async_computation | async-start | bytes 589824 | tf_op jit(solution)/shard_map/all_to_all | solution.py:335
  14.6 1.0 copy-start.2
  17.5 30.9 %all-to-all-start.1 = ((f32[128,2,256]{2,1,0:T(2,128)}), f32[128,2,256]{2,1,0:T(2,128)S(1)}, u32[]{:S(2)}, u32[]{:S(2)}) async-start(f32[128,2,256]{2,1,0:T(2,128)} %shard_map.183), calls=%async_computation.1 | async-start | bytes 524288 | tf_op jit(solution)/shard_map/all_to_all | solution.py:335
  34.1 23.0 %copy-start.13 = (s32[384]{0:T(512)S(1)}, s32[384]{0:T(512)}, u32[]{:S(2)}) copy-start(s32[384]{0:T(512)} %constant.203.clone) | copy-start | bytes 4612
  34.1 15.4 %collective-permute-start = (f32[2,2,256]{2,1,0:T(2,128)S(1)}, f32[2,2,256]{2,1,0:T(2,128)S(1)}, u32[]{:S(2)}, u32[]{:S(2)}) collective-permute-start(f32[2,2,256]{2,1,0:T(2,128)S(1)} %get-tuple-element.23), channel_id=1, source_target_pairs={{0,1},{1,2},{2,3},{3,4},{4,5},{5,6},{6,7},{7,8},{8,9},{9,10},{10,1... | collective-permute-start | bytes 12296 | tf_op jit(solution)/shard_map/ppermute | solution.py:339
  36.4 33.8 %copy-start.4 = (bf16[256,768]{1,0:T(8,128)(2,1)S(1)}, bf16[256,768]{1,0:T(8,128)(2,1)}, u32[]{:S(2)}) copy-start(bf16[256,768]{1,0:T(8,128)(2,1)} %constant.211.clone.refs_3_) | copy-start | bytes 1179652
  49.5 26.2 %copy-start.14 = (bf16[2,64]{1,0:T(2,128)(2,1)S(1)}, bf16[2,64]{1,0:T(2,128)(2,1)}, u32[]{:S(2)}) copy-start(bf16[2,64]{1,0:T(2,128)(2,1)} %param.20) | copy-start | bytes 772
  50.3 25.9 %copy-start.12 = (bf16[1,64,64]{2,1,0:T(8,128)(2,1)S(1)}, bf16[1,64,64]{2,1,0:T(8,128)(2,1)}, u32[]{:S(2)}) copy-start(bf16[1,64,64]{2,1,0:T(8,128)(2,1)} %param.19) | copy-start | bytes 24580
  50.3 25.9 %copy-start.1 = (f32[2,32,256]{2,1,0:T(8,128)S(1)}, f32[2,32,256]{2,1,0:T(8,128)}, u32[]{:S(2)}) copy-start(f32[2,32,256]{2,1,0:T(8,128)} %param.15) | copy-start | bytes 196612
  50.3 19.8 %all-to-all-start.2 = ((bf16[128,2,384]{2,1,0:T(2,128)(2,1)}), bf16[128,2,384]{2,1,0:T(2,128)(2,1)S(1)}, u32[]{:S(2)}, u32[]{:S(2)}) async-start(bf16[128,2,384]{2,1,0:T(2,128)(2,1)} %reshape.525), calls=%async_computation.2 | async-start | bytes 393216 | tf_op jit(solution)/shard_map/all_to_all | solution.py:335
  57.3 15.0 %collective-permute-start.1 = (f32[2,2,256]{2,1,0:T(2,128)S(1)}, f32[2,2,256]{2,1,0:T(2,128)S(1)}, u32[]{:S(2)}, u32[]{:S(2)}) collective-permute-start(f32[2,2,256]{2,1,0:T(2,128)S(1)} %get-tuple-element.25), channel_id=1, source_target_pairs={{0,31},{1,0},{2,1},{3,2},{4,3},{5,4},{6,5},{7,6},{8,7},{9,8},{10,9... | collective-permute-start | bytes 12296 | tf_op jit(solution)/shard_map/ppermute | solution.py:339
  72.2 12.6 %all-to-all-start.3 = ((f32[4,72,384]{2,1,0:T(8,128)}), f32[4,72,384]{2,1,0:T(8,128)S(1)}, u32[]{:S(2)}, u32[]{:S(2)}) async-start(f32[4,72,384]{2,1,0:T(8,128)} %bitcast.7), calls=%async_computation.3 | async-start | bytes 884736 | tf_op jit(solution)/shard_map/all_to_all | solution.py:335
  87.5 12.2 %all-to-all-start.4 = ((f32[16,16,128]{2,1,0:T(8,128)}), f32[16,16,128]{2,1,0:T(8,128)S(1)}, u32[]{:S(2)}, u32[]{:S(2)}) async-start(f32[16,16,128]{2,1,0:T(8,128)} %bitcast.29), calls=%async_computation.4 | async-start | bytes 262144 | tf_op jit(solution)/shard_map/all_to_all | solution.py:335
  100.5 18.2 %all-to-all-start.5 = ((f32[32,16,128]{2,1,0:T(8,128)}), f32[32,16,128]{2,1,0:T(8,128)S(1)}, u32[]{:S(2)}, u32[]{:S(2)}) async-start(f32[32,16,128]{2,1,0:T(8,128)} %bitcast.30), calls=%async_computation.5 | async-start | bytes 524288 | tf_op jit(solution)/shard_map/all_to_all | solution.py:335

commit v6 on v5

--- a/solution.py
+++ b/solution.py
@@ -340,9 +340,30 @@
 
 
 def pack_first(vel, cotangent):
-    edges = jnp.concatenate([vel[:, 0:2], vel[:, 254:256], jnp.zeros((64, 124), F32)], axis=1).T[:8]
-    rows = jnp.concatenate([edges, jnp.zeros((8, 192), F32)], axis=1)
-    return jnp.concatenate([cotangent, rows] * 4, axis=0)
+    def kernel(vel_ref, cot_ref, out_ref, rows_ref, edge_ref, sems):
+        load = pltpu.make_async_copy(vel_ref, rows_ref, sems.at[0])
+        load.start()
+        moves = [pltpu.make_async_copy(cot_ref, out_ref.at[d, pl.ds(0, 64)], sems.at[1 + d]) for d in range(4)]
+        for move in moves:
+            move.start()
+        load.wait()
+        rows = rows_ref[...]
+        edges = jnp.concatenate([rows[:, 0:2], rows[:, 254:256], jnp.zeros((64, 124), F32)], axis=1).T[:8]
+        edge_ref[...] = jnp.concatenate([edges, jnp.zeros((8, 192), F32)], axis=1)
+        ends = [pltpu.make_async_copy(edge_ref, out_ref.at[d, pl.ds(64, 8)], sems.at[5 + d]) for d in range(4)]
+        for move in ends:
+            move.start()
+        for move in moves + ends:
+            move.wait()
+
+    anywhere = pl.BlockSpec(memory_space=pl.ANY)
+    return pl.pallas_call(
+        kernel,
+        in_specs=[anywhere, anywhere],
+        out_specs=anywhere,
+        out_shape=sds((4, 72, 256), F32),
+        scratch_shapes=[pltpu.VMEM((64, 256), F32), pltpu.VMEM((8, 256), F32), pltpu.SemaphoreType.DMA((9,))],
+    )(vel, cotangent)
 
 
 def sum_and_spread(got):
@@ -445,8 +466,7 @@
     turn4 = turns(klass, cols4 + 1024 * (step % 4) + 256 * yl + NY)
     lift18 = lift_matrix(lift_weight, kernels)
 
-    sent1 = call(pack_first, sds((288, 256), F32), velocity.reshape(64, 256), cotangent.reshape(64, 256))
-    got1 = exchange(sent1.reshape(4, 72, 256), ("x",))
+    got1 = exchange(pack_first(velocity.reshape(64, 256), cotangent.reshape(64, 256)), ("x",))
     spec = call(y_forward, sds((128, 2, 256), F32), got1, turn1, sign, tab["t1"])
     spec, bottom = lax.optimization_barrier((spec, velocity[:, 30:]))
     got2 = exchange(spec, ("yl",) + IN_W)

time: 121 us -> 126 us (1.041)
  Pallas kernels: 11.9 us -> 20.3 us
  local copies, waits for them, and re-layouts: 6.82 us -> 4.13 us
    pallas_call x0 -> x1, Pallas kernels: none -> 9.13 us  [pack_first(): pl.pallas_call(kernel, in_specs=[anywhere, anywhere], out_specs=anywhere,...]
    unnamed x37 -> x33, local copies, waits for them, and re-layouts: 3.49 us -> 0.8 us
    pallas_call x7 -> x6, Pallas kernels: 9.92 us -> 9.19 us  [call(): pl.pallas_call(kernel, out_shape=out_shapes, compiler_params=pltpu.Compil...]
where the time goes in v6:
time: 126 us; the launch traced here: 125 us
  waiting for transfers between devices  52.2 us (41%)
  starting transfers between devices  43.7 us (35%)
  Pallas kernels  20.3 us (16%)
  local copies, waits for them, and re-layouts  4.13 us (3%)
  other arithmetic  3.82 us (3%)
    all_to_all x6, waiting for transfers between devices, exchange(): return lax.all_to_all(value, axes, split_axis=0, concat_axis=0)  52.2 us
    all_to_all x6, starting transfers between devices, exchange(): return lax.all_to_all(value, axes, split_axis=0, concat_axis=0)  39.7 us
    pallas_call x6, Pallas kernels, call(): pl.pallas_call(kernel, out_shape=out_shapes, compiler_params=pltpu.Compil...  9.19 us
    pallas_call x1, Pallas kernels, pack_first(): pl.pallas_call(kernel, in_specs=[anywhere, anywhere], out_specs=anywhere,...  9.13 us
    ppermute x2, starting transfers between devices, from_row_neighbour(): return lax.ppermute(value, IN_W, [(i, (i + step) % WA) for i in range(WA)])  4.07 us
    another operation x2, other arithmetic, finish_velocity(): return jnp.stack(out)  3.33 us
  transfers between devices with their start and end apart: 8, of which 6 were waited for; matrix products, arithmetic and copies ran while one was open for 6% of the time, Pallas kernels for 4%

profile of v6, /device:TPU:64, one launch (start us, length us, event | category | flops | bytes accessed | tf_op | source)
XLA Modules:
  0.0 125.4 jit_solution(5808983127320663045)
XLA Ops:
  0.6 0.0 copy-start.1
  0.7 9.1 %shard_map.182 = f32[4,72,256]{2,1,0:T(8,128)} custom-call(f32[64,256]{1,0:T(8,128)} %bitcast.62, f32[64,256]{1,0:T(8,128)} %bitcast.79), custom_call_target="tpu_custom_call" | custom-call | tf_op jit(solution)/shard_map/pallas_call | solution.py:360
  9.8 0.0 copy-start.2
  9.8 0.0 copy-start.4
  9.8 0.0 copy-start.5
  9.8 0.0 copy-start.6
  9.8 0.0 copy-start.7
  9.9 0.0 copy-start.8
  9.9 4.4 %all-to-all-start = ((f32[4,72,256]{2,1,0:T(8,128)}), f32[4,72,256]{2,1,0:T(8,128)S(1)}, u32[]{:S(2)}, u32[]{:S(2)}) async-start(f32[4,72,256]{2,1,0:T(8,128)} %shard_map.182), calls=%async_computation | async-start | bytes 589824 | tf_op jit(solution)/shard_map/all_to_all | solution.py:335
  14.3 0.1 broadcast_in_dim.40
  14.4 0.1 broadcast_in_dim.41
  14.5 0.7 copy.49
  15.2 0.2 fusion.16
  15.4 0.7 fusion.28
  16.1 5.2 %all-to-all-done.refs_0_ = f32[4,72,256]{2,1,0:T(8,128)S(1)} async-done(((f32[4,72,256]{2,1,0:T(8,128)}), f32[4,72,256]{2,1,0:T(8,128)S(1)}, u32[]{:S(2)}, u32[]{:S(2)}) %all-to-all-start) | async-done | bytes 294944 | tf_op jit(solution)/shard_map/all_to_all | solution.py:335
  21.3 0.0 copy-done.1
  21.3 1.8 %shard_map.183 = f32[128,2,256]{2,1,0:T(2,128)} custom-call(f32[4,72,256]{2,1,0:T(8,128)S(1)} %all-to-all-done.refs_0_, f32[2,16,256]{2,1,0:T(8,128)S(1)} %pad_maximum_fusion.2.refs_1_, f32[1,256]{1,0:T(1,128)S(1)} %broadcast_select_fusion.1.refs_2_, bf16[2,256,512]{2,1,0:T(8,128)(2,1)S(1)} %copy-done.1), custom_call_target="tpu_custom_call" | custom-call | tf_op jit(solution)/shard_map/pallas_call | solution.py:306
  23.2 16.6 %all-to-all-start.1 = ((f32[128,2,256]{2,1,0:T(2,128)}), f32[128,2,256]{2,1,0:T(2,128)S(1)}, u32[]{:S(2)}, u32[]{:S(2)}) async-start(f32[128,2,256]{2,1,0:T(2,128)} %shard_map.183), calls=%async_computation.1 | async-start | bytes 524288 | tf_op jit(solution)/shard_map/all_to_all | solution.py:335
  39.7 0.0 copy-start.11
  39.8 2.1 %collective-permute-start = (f32[2,2,256]{2,1,0:T(2,128)S(1)}, f32[2,2,256]{2,1,0:T(2,128)S(1)}, u32[]{:S(2)}, u32[]{:S(2)}) collective-permute-start(f32[2,2,256]{2,1,0:T(2,128)S(1)} %get-tuple-element.23), channel_id=1, source_target_pairs={{0,1},{1,2},{2,3},{3,4},{4,5},{5,6},{6,7},{7,8},{8,9},{9,10},{10,1... | collective-permute-start | bytes 12296 | tf_op jit(solution)/shard_map/ppermute | solution.py:339
  41.9 0.1 broadcast_select_fusion
  42.0 0.1 pad.4.refs_2_
  42.1 12.0 %all-to-all-done.1 = f32[128,2,256]{2,1,0:T(2,128)S(1)} async-done(((f32[128,2,256]{2,1,0:T(2,128)}), f32[128,2,256]{2,1,0:T(2,128)S(1)}, u32[]{:S(2)}, u32[]{:S(2)}) %all-to-all-start.1) | async-done | bytes 262176 | tf_op jit(solution)/shard_map/all_to_all | solution.py:335
  54.0 0.2 reshape.520.refs_0_
  54.2 0.0 copy-done.2
  54.2 0.0 copy-done.4
  54.2 0.0 copy-done.5
  54.3 0.0 copy-done.6
  54.3 0.0 copy-done.7
  54.3 0.0 copy-done.8
  54.3 0.9 shard_map.184
  55.2 0.0 copy-start.12
  55.2 0.0 collective-permute-done.refs_0_
  55.2 0.8 reshape.521
  56.0 6.8 %all-to-all-start.2 = ((bf16[128,2,384]{2,1,0:T(2,128)(2,1)}), bf16[128,2,384]{2,1,0:T(2,128)(2,1)S(1)}, u32[]{:S(2)}, u32[]{:S(2)}) async-start(bf16[128,2,384]{2,1,0:T(2,128)(2,1)} %reshape.521), calls=%async_computation.2 | async-start | bytes 393216 | tf_op jit(solution)/shard_map/all_to_all | solution.py:335
  62.8 0.2 fusion.14
  63.0 2.0 %collective-permute-start.1 = (f32[2,2,256]{2,1,0:T(2,128)S(1)}, f32[2,2,256]{2,1,0:T(2,128)S(1)}, u32[]{:S(2)}, u32[]{:S(2)}) collective-permute-start(f32[2,2,256]{2,1,0:T(2,128)S(1)} %get-tuple-element.25), channel_id=1, source_target_pairs={{0,31},{1,0},{2,1},{3,2},{4,3},{5,4},{6,5},{7,6},{8,7},{9,8},{10,9... | collective-permute-start | bytes 12296 | tf_op jit(solution)/shard_map/ppermute | solution.py:339
  65.0 10.8 %all-to-all-done.2.picked_ref = bf16[128,2,384]{2,1,0:T(2,128)(2,1)S(1)} async-done(((bf16[128,2,384]{2,1,0:T(2,128)(2,1)}), bf16[128,2,384]{2,1,0:T(2,128)(2,1)S(1)}, u32[]{:S(2)}, u32[]{:S(2)}) %all-to-all-start.2) | async-done | bytes 196640 | tf_op jit(solution)/shard_map/all_to_all | solution.py:335
  75.8 0.1 reshape.522.refs_0_
  75.9 2.0 %shard_map.185 = f32[288,384]{1,0:T(8,128)} custom-call(bf16[4,64,384]{2,1,0:T(8,128)(2,1)S(1)} %reshape.522.refs_0_, f32[2,16,384]{2,1,0:T(8,128)S(1)} %pad_maximum_fusion.1.refs_1_, f32[1,384]{1,0:T(1,128)S(1)} %select_n.183.refs_2_, bf16[256,768]{1,0:T(8,128)(2,1)S(1)} %copy-done.3), custom_call_target="tpu_custom_call" | custom-call | tf_op jit(solution)/shard_map/pallas_call | solution.py:306
  78.0 0.0 collective-permute-done.1.refs_2_
  78.0 3.5 %all-to-all-start.3 = ((f32[4,72,384]{2,1,0:T(8,128)}), f32[4,72,384]{2,1,0:T(8,128)S(1)}, u32[]{:S(2)}, u32[]{:S(2)}) async-start(f32[4,72,384]{2,1,0:T(8,128)} %bitcast.6), calls=%async_computation.3 | async-start | bytes 884736 | tf_op jit(solution)/shard_map/all_to_all | solution.py:335
  81.4 0.0 copy-done.12
  81.5 0.1 stack.70
  81.6 0.1 copy.20.refs_4_
  81.7 0.1 copy.21.refs_5_
  81.8 0.1 stack.34.index_ref
  81.9 0.0 copy-done.10
  81.9 1.9 %shard_map.186 = (f32[288,384]{1,0:T(8,128)S(1)}, bf16[2176,384]{1,0:T(8,128)(2,1)S(1)}, bf16[128,48]{1,0:T(8,128)(2,1)S(1)}) custom-call(s32[6]{0:T(128)S(1)} %stack.34.index_ref, bf16[128,2,384]{2,1,0:T(2,128)(2,1)S(1)} %all-to-all-done.2.picked_ref, f32[2,2,256]{2,1,0:T(2,128)S(1)} %collective-permute-done.refs_0_, f32[64,256]{1,0:T(8,128)S(1)} %bitcast.63, ...), custom_call_target="tpu_custom_call" | custom-call | tf_op jit(solution)/shard_map/pallas_call | solution.py:321
  83.8 6.8 %all-to-all-done.3.refs_0_ = f32[4,72,384]{2,1,0:T(8,128)S(1)} async-done(((f32[4,72,384]{2,1,0:T(8,128)}), f32[4,72,384]{2,1,0:T(8,128)S(1)}, u32[]{:S(2)}, u32[]{:S(2)}) %all-to-all-start.3) | async-done | bytes 442400 | tf_op jit(solution)/shard_map/all_to_all | solution.py:335
  90.6 2.7 %shard_map.187 = (f32[72,384]{1,0:T(8,128)S(1)}, f32[256,384]{1,0:T(8,128)S(1)}, f32[256,128]{1,0:T(8,128)}) custom-call(f32[4,72,384]{2,1,0:T(8,128)S(1)} %all-to-all-done.3.refs_0_, f32[288,384]{1,0:T(8,128)S(1)} %get-tuple-element.29.refs_1_, bf16[2176,384]{1,0:T(8,128)(2,1)S(1)} %get-tuple-element.30.refs_2_, ...), custom_call_target="tpu_custom_call" | custom-call | tf_op jit(solution)/shard_map/pallas_call | solution.py:306
  93.3 3.5 %all-to-all-start.4 = ((f32[16,16,128]{2,1,0:T(8,128)}), f32[16,16,128]{2,1,0:T(8,128)S(1)}, u32[]{:S(2)}, u32[]{:S(2)}) async-start(f32[16,16,128]{2,1,0:T(8,128)} %bitcast.28), calls=%async_computation.4 | async-start | bytes 262144 | tf_op jit(solution)/shard_map/all_to_all | solution.py:335
  96.8 0.1 fusion.31
  96.9 0.6 fusion.29
  97.5 8.0 %all-to-all-done.4.refs_0_ = f32[16,16,128]{2,1,0:T(8,128)S(1)} async-done(((f32[16,16,128]{2,1,0:T(8,128)}), f32[16,16,128]{2,1,0:T(8,128)S(1)}, u32[]{:S(2)}, u32[]{:S(2)}) %all-to-all-start.4) | async-done | bytes 131104 | tf_op jit(solution)/shard_map/all_to_all | solution.py:335
  105.5 0.7 shard_map.188
  106.3 4.9 %all-to-all-start.5 = ((f32[32,16,128]{2,1,0:T(8,128)}), f32[32,16,128]{2,1,0:T(8,128)S(1)}, u32[]{:S(2)}, u32[]{:S(2)}) async-start(f32[32,16,128]{2,1,0:T(8,128)} %bitcast.29), calls=%async_computation.5 | async-start | bytes 524288 | tf_op jit(solution)/shard_map/all_to_all | solution.py:335
  111.2 0.2 fusion.27
  111.4 0.1 slice.188
  111.5 0.1 slice.195
  111.6 2.7 %fusion.4 = (f32[1,32,256]{2,1,0:T(8,128)S(1)}, f32[1,32,256]{2,1,0:T(8,128)S(1)}) fusion(f32[32,384]{1,0:T(8,128)S(1)} %bitcast.77, f32[32,384]{1,0:T(8,128)S(1)} %bitcast.78, f32[32,255]{1,0:T(8,128)S(1)} %slice.189, f32[32,1]{1,0:T(8,128)S(1)} %slice.188, f32[72,384]{1,0:T(8,128)S(1)} %get-tuple-element.32, f32[]{:T(128)} %bitcast.16, f32[]{:T(128)} %bitcast.15, ...), kind=kLoop, calls=%fused_computation.18 | loop fusion | flops 131072 | bytes 327696 | tf_op jit(solution)/shard_map/stack | solution.py:415
  114.3 0.6 pad_maximum_fusion
  114.9 9.5 %all-to-all-done.5.refs_0_ = f32[32,16,128]{2,1,0:T(8,128)S(1)} async-done(((f32[32,16,128]{2,1,0:T(8,128)}), f32[32,16,128]{2,1,0:T(8,128)S(1)}, u32[]{:S(2)}, u32[]{:S(2)}) %all-to-all-start.5) | async-done | bytes 262176 | tf_op jit(solution)/shard_map/all_to_all | solution.py:335
  124.5 1.0 shard_map.189
  (33 shorter events, 0.2 us)
Async XLA Ops:
  0.6 20.7 %copy-start.1 = (bf16[2,256,512]{2,1,0:T(8,128)(2,1)S(1)}, bf16[2,256,512]{2,1,0:T(8,128)(2,1)}, u32[]{:S(2)}) copy-start(bf16[2,256,512]{2,1,0:T(8,128)(2,1)} %constant.204.clone.refs_3_) | copy-start | bytes 1572868
  0.6 39.1 %copy-start.9 = (f32[64,2]{0,1:T(2,128)S(1)}, f32[64,2]{0,1:T(2,128)}, u32[]{:S(2)}) copy-start(f32[64,2]{0,1:T(2,128)} %param.17) | copy-start | bytes 1540
  9.8 44.4 %copy-start.2 = (bf16[2,256,512]{2,1,0:T(8,128)(2,1)S(1)}, bf16[2,256,512]{2,1,0:T(8,128)(2,1)}, u32[]{:S(2)}) copy-start(bf16[2,256,512]{2,1,0:T(8,128)(2,1)} %constant.208.clone.refs_6_) | copy-start | bytes 1572868
  9.8 44.4 %copy-start.4 = (bf16[2,256,256]{2,1,0:T(8,128)(2,1)S(1)}, bf16[2,256,256]{2,1,0:T(8,128)(2,1)}, u32[]{:S(2)}) copy-start(bf16[2,256,256]{2,1,0:T(8,128)(2,1)} %constant.207.clone.refs_5_) | copy-start | bytes 786436
  9.8 44.4 %copy-start.5 = (bf16[2,128,64]{2,1,0:T(8,128)(2,1)S(1)}, bf16[2,128,64]{2,1,0:T(8,128)(2,1)}, u32[]{:S(2)}) copy-start(bf16[2,128,64]{2,1,0:T(8,128)(2,1)} %constant.205.clone.refs_3_) | copy-start | bytes 98308
  9.8 44.4 %copy-start.6 = (f32[2,32,256]{2,1,0:T(8,128)S(1)}, f32[2,32,256]{2,1,0:T(8,128)}, u32[]{:S(2)}) copy-start(f32[2,32,256]{2,1,0:T(8,128)} %constant.206.clone.refs_4_) | copy-start | bytes 196612
  9.8 44.4 %copy-start.7 = (f32[2,32,256]{2,1,0:T(8,128)S(1)}, f32[2,32,256]{2,1,0:T(8,128)}, u32[]{:S(2)}) copy-start(f32[2,32,256]{2,1,0:T(8,128)} %constant.209.clone.refs_7_) | copy-start | bytes 196612
  9.9 44.4 %copy-start.8 = (bf16[2,64,64]{2,1,0:T(8,128)(2,1)S(1)}, bf16[2,64,64]{2,1,0:T(8,128)(2,1)}, u32[]{:S(2)}) copy-start(bf16[2,64,64]{2,1,0:T(8,128)(2,1)} %constant.210.clone.refs_8_) | copy-start | bytes 49156
  9.9 11.5 %all-to-all-start = ((f32[4,72,256]{2,1,0:T(8,128)}), f32[4,72,256]{2,1,0:T(8,128)S(1)}, u32[]{:S(2)}, u32[]{:S(2)}) async-start(f32[4,72,256]{2,1,0:T(8,128)} %shard_map.182), calls=%async_computation | async-start | bytes 589824 | tf_op jit(solution)/shard_map/all_to_all | solution.py:335
  23.2 30.9 %all-to-all-start.1 = ((f32[128,2,256]{2,1,0:T(2,128)}), f32[128,2,256]{2,1,0:T(2,128)S(1)}, u32[]{:S(2)}, u32[]{:S(2)}) async-start(f32[128,2,256]{2,1,0:T(2,128)} %shard_map.183), calls=%async_computation.1 | async-start | bytes 524288 | tf_op jit(solution)/shard_map/all_to_all | solution.py:335
  39.7 23.0 %copy-start.11 = (s32[384]{0:T(512)S(1)}, s32[384]{0:T(512)}, u32[]{:S(2)}) copy-start(s32[384]{0:T(512)} %constant.203.clone) | copy-start | bytes 4612
  39.8 15.4 %collective-permute-start = (f32[2,2,256]{2,1,0:T(2,128)S(1)}, f32[2,2,256]{2,1,0:T(2,128)S(1)}, u32[]{:S(2)}, u32[]{:S(2)}) collective-permute-start(f32[2,2,256]{2,1,0:T(2,128)S(1)} %get-tuple-element.23), channel_id=1, source_target_pairs={{0,1},{1,2},{2,3},{3,4},{4,5},{5,6},{6,7},{7,8},{8,9},{9,10},{10,1... | collective-permute-start | bytes 12296 | tf_op jit(solution)/shard_map/ppermute | solution.py:339
  42.1 33.9 %copy-start.3 = (bf16[256,768]{1,0:T(8,128)(2,1)S(1)}, bf16[256,768]{1,0:T(8,128)(2,1)}, u32[]{:S(2)}) copy-start(bf16[256,768]{1,0:T(8,128)(2,1)} %constant.211.clone.refs_3_) | copy-start | bytes 1179652
  55.2 26.2 %copy-start.12 = (bf16[2,64]{1,0:T(2,128)(2,1)S(1)}, bf16[2,64]{1,0:T(2,128)(2,1)}, u32[]{:S(2)}) copy-start(bf16[2,64]{1,0:T(2,128)(2,1)} %param.20) | copy-start | bytes 772
  56.0 25.9 %copy-start.10 = (bf16[1,64,64]{2,1,0:T(8,128)(2,1)S(1)}, bf16[1,64,64]{2,1,0:T(8,128)(2,1)}, u32[]{:S(2)}) copy-start(bf16[1,64,64]{2,1,0:T(8,128)(2,1)} %param.19) | copy-start | bytes 24580
  56.0 25.9 %copy-start = (f32[2,32,256]{2,1,0:T(8,128)S(1)}, f32[2,32,256]{2,1,0:T(8,128)}, u32[]{:S(2)}) copy-start(f32[2,32,256]{2,1,0:T(8,128)} %param.15) | copy-start | bytes 196612
  56.0 19.9 %all-to-all-start.2 = ((bf16[128,2,384]{2,1,0:T(2,128)(2,1)}), bf16[128,2,384]{2,1,0:T(2,128)(2,1)S(1)}, u32[]{:S(2)}, u32[]{:S(2)}) async-start(bf16[128,2,384]{2,1,0:T(2,128)(2,1)} %reshape.521), calls=%async_computation.2 | async-start | bytes 393216 | tf_op jit(solution)/shard_map/all_to_all | solution.py:335
  63.0 15.0 %collective-permute-start.1 = (f32[2,2,256]{2,1,0:T(2,128)S(1)}, f32[2,2,256]{2,1,0:T(2,128)S(1)}, u32[]{:S(2)}, u32[]{:S(2)}) collective-permute-start(f32[2,2,256]{2,1,0:T(2,128)S(1)} %get-tuple-element.25), channel_id=1, source_target_pairs={{0,31},{1,0},{2,1},{3,2},{4,3},{5,4},{6,5},{7,6},{8,7},{9,8},{10,9... | collective-permute-start | bytes 12296 | tf_op jit(solution)/shard_map/ppermute | solution.py:339
  78.0 12.6 %all-to-all-start.3 = ((f32[4,72,384]{2,1,0:T(8,128)}), f32[4,72,384]{2,1,0:T(8,128)S(1)}, u32[]{:S(2)}, u32[]{:S(2)}) async-start(f32[4,72,384]{2,1,0:T(8,128)} %bitcast.6), calls=%async_computation.3 | async-start | bytes 884736 | tf_op jit(solution)/shard_map/all_to_all | solution.py:335
  93.3 12.2 %all-to-all-start.4 = ((f32[16,16,128]{2,1,0:T(8,128)}), f32[16,16,128]{2,1,0:T(8,128)S(1)}, u32[]{:S(2)}, u32[]{:S(2)}) async-start(f32[16,16,128]{2,1,0:T(8,128)} %bitcast.28), calls=%async_computation.4 | async-start | bytes 262144 | tf_op jit(solution)/shard_map/all_to_all | solution.py:335
  106.3 18.2 %all-to-all-start.5 = ((f32[32,16,128]{2,1,0:T(8,128)}), f32[32,16,128]{2,1,0:T(8,128)S(1)}, u32[]{:S(2)}, u32[]{:S(2)}) async-start(f32[32,16,128]{2,1,0:T(8,128)} %bitcast.29), calls=%async_computation.5 | async-start | bytes 524288 | tf_op jit(solution)/shard_map/all_to_all | solution.py:335

commit v7 on v5

--- a/solution.py
+++ b/solution.py
@@ -340,9 +340,29 @@
 
 
 def pack_first(vel, cotangent):
-    edges = jnp.concatenate([vel[:, 0:2], vel[:, 254:256], jnp.zeros((64, 124), F32)], axis=1).T[:8]
-    rows = jnp.concatenate([edges, jnp.zeros((8, 192), F32)], axis=1)
-    return jnp.concatenate([cotangent, rows] * 4, axis=0)
+    def kernel(vel_ref, cot_ref, out_ref, rows_ref, cells_ref, sems):
+        first = pltpu.make_async_copy(vel_ref, rows_ref, sems.at[0])
+        second = pltpu.make_async_copy(cot_ref, cells_ref, sems.at[1])
+        first.start()
+        second.start()
+        first.wait()
+        second.wait()
+        rows = rows_ref[...]
+        edges = jnp.concatenate([rows[:, 0:2], rows[:, 254:256], jnp.zeros((64, 124), F32)], axis=1).T[:8]
+        edges = jnp.concatenate([edges, jnp.zeros((8, 192), F32)], axis=1)
+        cells = cells_ref[...]
+        for d in range(4):
+            out_ref[d, :64] = cells
+            out_ref[d, 64:] = edges
+
+    anywhere = pl.BlockSpec(memory_space=pl.ANY)
+    return pl.pallas_call(
+        kernel,
+        in_specs=[anywhere, anywhere],
+        out_specs=pl.BlockSpec(memory_space=pltpu.VMEM),
+        out_shape=sds((4, 72, 256), F32),
+        scratch_shapes=[pltpu.VMEM((64, 256), F32), pltpu.VMEM((64, 256), F32), pltpu.SemaphoreType.DMA((2,))],
+    )(vel, cotangent)
 
 
 def sum_and_spread(got):
@@ -445,8 +465,7 @@
     turn4 = turns(klass, cols4 + 1024 * (step % 4) + 256 * yl + NY)
     lift18 = lift_matrix(lift_weight, kernels)
 
-    sent1 = call(pack_first, sds((288, 256), F32), velocity.reshape(64, 256), cotangent.reshape(64, 256))
-    got1 = exchange(sent1.reshape(4, 72, 256), ("x",))
+    got1 = exchange(pack_first(velocity.reshape(64, 256), cotangent.reshape(64, 256)), ("x",))
     spec = call(y_forward, sds((128, 2, 256), F32), got1, turn1, sign, tab["t1"])
     spec, bottom = lax.optimization_barrier((spec, velocity[:, 30:]))
     got2 = exchange(spec, ("yl",) + IN_W)

time: 121 us -> 119 us (0.983)
  local copies, waits for them, and re-layouts: 6.82 us -> 4.13 us
    unnamed x37 -> x33, local copies, waits for them, and re-layouts: 3.49 us -> 0.8 us
    pallas_call x0 -> x1, Pallas kernels: none -> 1.79 us  [pack_first(): pl.pallas_call(kernel, in_specs=[anywhere, anywhere], out_specs=pl.BlockS...]
    pallas_call x7 -> x6, Pallas kernels: 9.92 us -> 9.19 us  [call(): pl.pallas_call(kernel, out_shape=out_shapes, compiler_params=pltpu.Compil...]
where the time goes in v7:
time: 119 us; the launch traced here: 118 us
  waiting for transfers between devices  52.2 us (44%)
  starting transfers between devices  43.7 us (37%)
  Pallas kernels  12.9 us (11%)
  local copies, waits for them, and re-layouts  4.13 us (3%)
  other arithmetic  3.82 us (3%)
    all_to_all x6, waiting for transfers between devices, exchange(): return lax.all_to_all(value, axes, split_axis=0, concat_axis=0)  52.2 us
    all_to_all x6, starting transfers between devices, exchange(): return lax.all_to_all(value, axes, split_axis=0, concat_axis=0)  39.7 us
    pallas_call x6, Pallas kernels, call(): pl.pallas_call(kernel, out_shape=out_shapes, compiler_params=pltpu.Compil...  9.19 us
    ppermute x2, starting transfers between devices, from_row_neighbour(): return lax.ppermute(value, IN_W, [(i, (i + step) % WA) for i in range(WA)])  4.07 us
    another operation x2, other arithmetic, finish_velocity(): return jnp.stack(out)  3.33 us
  transfers between devices with their start and end apart: 8, of which 6 were waited for; matrix products, arithmetic and copies ran while one was open for 6% of the time, Pallas kernels for 4%

profile of v7, /device:TPU:64, one launch (start us, length us, event | category | flops | bytes accessed | tf_op | source)
XLA Modules:
  0.0 118.1 jit_solution(524997312703622266)
XLA Ops:
  0.6 0.0 copy-start.1
  0.6 0.0 copy-start.9
  0.7 1.8 %shard_map.182 = f32[4,72,256]{2,1,0:T(8,128)} custom-call(f32[64,256]{1,0:T(8,128)} %bitcast.62, f32[64,256]{1,0:T(8,128)} %bitcast.79), custom_call_target="tpu_custom_call" | custom-call | tf_op jit(solution)/shard_map/pallas_call | solution.py:359
  2.5 0.0 copy-start.2
  2.5 0.0 copy-start.4
  2.5 0.0 copy-start.5
  2.5 0.0 copy-start.6
  2.5 0.0 copy-start.7
  2.5 0.0 copy-start.8
  2.5 4.4 %all-to-all-start = ((f32[4,72,256]{2,1,0:T(8,128)}), f32[4,72,256]{2,1,0:T(8,128)S(1)}, u32[]{:S(2)}, u32[]{:S(2)}) async-start(f32[4,72,256]{2,1,0:T(8,128)} %shard_map.182), calls=%async_computation | async-start | bytes 589824 | tf_op jit(solution)/shard_map/all_to_all | solution.py:335
  7.0 0.1 broadcast_in_dim.40
  7.1 0.1 broadcast_in_dim.41
  7.2 0.7 copy.49
  7.9 0.2 fusion.16
  8.0 0.7 fusion.28
  8.8 5.2 %all-to-all-done.refs_0_ = f32[4,72,256]{2,1,0:T(8,128)S(1)} async-done(((f32[4,72,256]{2,1,0:T(8,128)}), f32[4,72,256]{2,1,0:T(8,128)S(1)}, u32[]{:S(2)}, u32[]{:S(2)}) %all-to-all-start) | async-done | bytes 294944 | tf_op jit(solution)/shard_map/all_to_all | solution.py:335
  14.0 0.0 copy-done.1
  14.0 1.8 %shard_map.183 = f32[128,2,256]{2,1,0:T(2,128)} custom-call(f32[4,72,256]{2,1,0:T(8,128)S(1)} %all-to-all-done.refs_0_, f32[2,16,256]{2,1,0:T(8,128)S(1)} %pad_maximum_fusion.2.refs_1_, f32[1,256]{1,0:T(1,128)S(1)} %broadcast_select_fusion.1.refs_2_, bf16[2,256,512]{2,1,0:T(8,128)(2,1)S(1)} %copy-done.1), custom_call_target="tpu_custom_call" | custom-call | tf_op jit(solution)/shard_map/pallas_call | solution.py:306
  15.8 16.6 %all-to-all-start.1 = ((f32[128,2,256]{2,1,0:T(2,128)}), f32[128,2,256]{2,1,0:T(2,128)S(1)}, u32[]{:S(2)}, u32[]{:S(2)}) async-start(f32[128,2,256]{2,1,0:T(2,128)} %shard_map.183), calls=%async_computation.1 | async-start | bytes 524288 | tf_op jit(solution)/shard_map/all_to_all | solution.py:335
  32.4 0.0 copy-start.11
  32.4 0.0 copy-done.9
  32.5 2.1 %collective-permute-start = (f32[2,2,256]{2,1,0:T(2,128)S(1)}, f32[2,2,256]{2,1,0:T(2,128)S(1)}, u32[]{:S(2)}, u32[]{:S(2)}) collective-permute-start(f32[2,2,256]{2,1,0:T(2,128)S(1)} %get-tuple-element.23), channel_id=1, source_target_pairs={{0,1},{1,2},{2,3},{3,4},{4,5},{5,6},{6,7},{7,8},{8,9},{9,10},{10,1... | collective-permute-start | bytes 12296 | tf_op jit(solution)/shard_map/ppermute | solution.py:339
  34.6 0.1 broadcast_select_fusion
  34.7 0.1 pad.4.refs_2_
  34.7 12.0 %all-to-all-done.1 = f32[128,2,256]{2,1,0:T(2,128)S(1)} async-done(((f32[128,2,256]{2,1,0:T(2,128)}), f32[128,2,256]{2,1,0:T(2,128)S(1)}, u32[]{:S(2)}, u32[]{:S(2)}) %all-to-all-start.1) | async-done | bytes 262176 | tf_op jit(solution)/shard_map/all_to_all | solution.py:335
  46.7 0.2 reshape.520.refs_0_
  46.9 0.0 copy-done.2
  46.9 0.0 copy-done.4
  46.9 0.0 copy-done.5
  46.9 0.0 copy-done.6
  46.9 0.0 copy-done.7
  46.9 0.9 shard_map.184
  47.9 0.0 copy-start.12
  47.9 0.0 collective-permute-done.refs_0_
  47.9 0.8 reshape.521
  48.6 6.8 %all-to-all-start.2 = ((bf16[128,2,384]{2,1,0:T(2,128)(2,1)}), bf16[128,2,384]{2,1,0:T(2,128)(2,1)S(1)}, u32[]{:S(2)}, u32[]{:S(2)}) async-start(bf16[128,2,384]{2,1,0:T(2,128)(2,1)} %reshape.521), calls=%async_computation.2 | async-start | bytes 393216 | tf_op jit(solution)/shard_map/all_to_all | solution.py:335
  55.4 0.2 fusion.14
  55.6 2.0 %collective-permute-start.1 = (f32[2,2,256]{2,1,0:T(2,128)S(1)}, f32[2,2,256]{2,1,0:T(2,128)S(1)}, u32[]{:S(2)}, u32[]{:S(2)}) collective-permute-start(f32[2,2,256]{2,1,0:T(2,128)S(1)} %get-tuple-element.25), channel_id=1, source_target_pairs={{0,31},{1,0},{2,1},{3,2},{4,3},{5,4},{6,5},{7,6},{8,7},{9,8},{10,9... | collective-permute-start | bytes 12296 | tf_op jit(solution)/shard_map/ppermute | solution.py:339
  57.7 10.8 %all-to-all-done.2.picked_ref = bf16[128,2,384]{2,1,0:T(2,128)(2,1)S(1)} async-done(((bf16[128,2,384]{2,1,0:T(2,128)(2,1)}), bf16[128,2,384]{2,1,0:T(2,128)(2,1)S(1)}, u32[]{:S(2)}, u32[]{:S(2)}) %all-to-all-start.2) | async-done | bytes 196640 | tf_op jit(solution)/shard_map/all_to_all | solution.py:335
  68.5 0.1 reshape.522.refs_0_
  68.6 2.0 %shard_map.185 = f32[288,384]{1,0:T(8,128)} custom-call(bf16[4,64,384]{2,1,0:T(8,128)(2,1)S(1)} %reshape.522.refs_0_, f32[2,16,384]{2,1,0:T(8,128)S(1)} %pad_maximum_fusion.1.refs_1_, f32[1,384]{1,0:T(1,128)S(1)} %select_n.183.refs_2_, bf16[256,768]{1,0:T(8,128)(2,1)S(1)} %copy-done.3), custom_call_target="tpu_custom_call" | custom-call | tf_op jit(solution)/shard_map/pallas_call | solution.py:306
  70.6 0.0 collective-permute-done.1.refs_2_
  70.6 3.5 %all-to-all-start.3 = ((f32[4,72,384]{2,1,0:T(8,128)}), f32[4,72,384]{2,1,0:T(8,128)S(1)}, u32[]{:S(2)}, u32[]{:S(2)}) async-start(f32[4,72,384]{2,1,0:T(8,128)} %bitcast.6), calls=%async_computation.3 | async-start | bytes 884736 | tf_op jit(solution)/shard_map/all_to_all | solution.py:335
  74.2 0.1 stack.70
  74.2 0.1 copy.20.refs_4_
  74.3 0.1 copy.21.refs_5_
  74.4 0.1 stack.34.index_ref
  74.5 0.0 copy-done
  74.5 1.9 %shard_map.186 = (f32[288,384]{1,0:T(8,128)S(1)}, bf16[2176,384]{1,0:T(8,128)(2,1)S(1)}, bf16[128,48]{1,0:T(8,128)(2,1)S(1)}) custom-call(s32[6]{0:T(128)S(1)} %stack.34.index_ref, bf16[128,2,384]{2,1,0:T(2,128)(2,1)S(1)} %all-to-all-done.2.picked_ref, f32[2,2,256]{2,1,0:T(2,128)S(1)} %collective-permute-done.refs_0_, f32[64,256]{1,0:T(8,128)S(1)} %bitcast.63, ...), custom_call_target="tpu_custom_call" | custom-call | tf_op jit(solution)/shard_map/pallas_call | solution.py:321
  76.5 6.8 %all-to-all-done.3.refs_0_ = f32[4,72,384]{2,1,0:T(8,128)S(1)} async-done(((f32[4,72,384]{2,1,0:T(8,128)}), f32[4,72,384]{2,1,0:T(8,128)S(1)}, u32[]{:S(2)}, u32[]{:S(2)}) %all-to-all-start.3) | async-done | bytes 442400 | tf_op jit(solution)/shard_map/all_to_all | solution.py:335
  83.3 2.7 %shard_map.187 = (f32[72,384]{1,0:T(8,128)S(1)}, f32[256,384]{1,0:T(8,128)S(1)}, f32[256,128]{1,0:T(8,128)}) custom-call(f32[4,72,384]{2,1,0:T(8,128)S(1)} %all-to-all-done.3.refs_0_, f32[288,384]{1,0:T(8,128)S(1)} %get-tuple-element.29.refs_1_, bf16[2176,384]{1,0:T(8,128)(2,1)S(1)} %get-tuple-element.30.refs_2_, ...), custom_call_target="tpu_custom_call" | custom-call | tf_op jit(solution)/shard_map/pallas_call | solution.py:306
  86.0 3.5 %all-to-all-start.4 = ((f32[16,16,128]{2,1,0:T(8,128)}), f32[16,16,128]{2,1,0:T(8,128)S(1)}, u32[]{:S(2)}, u32[]{:S(2)}) async-start(f32[16,16,128]{2,1,0:T(8,128)} %bitcast.28), calls=%async_computation.4 | async-start | bytes 262144 | tf_op jit(solution)/shard_map/all_to_all | solution.py:335
  89.5 0.1 fusion.31
  89.6 0.6 fusion.29
  90.2 8.0 %all-to-all-done.4.refs_0_ = f32[16,16,128]{2,1,0:T(8,128)S(1)} async-done(((f32[16,16,128]{2,1,0:T(8,128)}), f32[16,16,128]{2,1,0:T(8,128)S(1)}, u32[]{:S(2)}, u32[]{:S(2)}) %all-to-all-start.4) | async-done | bytes 131104 | tf_op jit(solution)/shard_map/all_to_all | solution.py:335
  98.2 0.7 shard_map.188
  98.9 4.9 %all-to-all-start.5 = ((f32[32,16,128]{2,1,0:T(8,128)}), f32[32,16,128]{2,1,0:T(8,128)S(1)}, u32[]{:S(2)}, u32[]{:S(2)}) async-start(f32[32,16,128]{2,1,0:T(8,128)} %bitcast.29), calls=%async_computation.5 | async-start | bytes 524288 | tf_op jit(solution)/shard_map/all_to_all | solution.py:335
  103.8 0.2 fusion.27
  104.1 0.1 slice.188
  104.2 0.1 slice.195
  104.3 2.7 %fusion.4 = (f32[1,32,256]{2,1,0:T(8,128)S(1)}, f32[1,32,256]{2,1,0:T(8,128)S(1)}) fusion(f32[32,384]{1,0:T(8,128)S(1)} %bitcast.77, f32[32,384]{1,0:T(8,128)S(1)} %bitcast.78, f32[32,255]{1,0:T(8,128)S(1)} %slice.189, f32[32,1]{1,0:T(8,128)S(1)} %slice.188, f32[72,384]{1,0:T(8,128)S(1)} %get-tuple-element.32, f32[]{:T(128)} %bitcast.16, f32[]{:T(128)} %bitcast.15, ...), kind=kLoop, calls=%fused_computation.18 | loop fusion | flops 131072 | bytes 327696 | tf_op jit(solution)/shard_map/stack | solution.py:414
  107.0 0.6 pad_maximum_fusion
  107.6 9.5 %all-to-all-done.5.refs_0_ = f32[32,16,128]{2,1,0:T(8,128)S(1)} async-done(((f32[32,16,128]{2,1,0:T(8,128)}), f32[32,16,128]{2,1,0:T(8,128)S(1)}, u32[]{:S(2)}, u32[]{:S(2)}) %all-to-all-start.5) | async-done | bytes 262176 | tf_op jit(solution)/shard_map/all_to_all | solution.py:335
  117.1 1.0 shard_map.189
  (33 shorter events, 0.2 us)
Async XLA Ops:
  0.6 13.4 %copy-start.1 = (bf16[2,256,512]{2,1,0:T(8,128)(2,1)S(1)}, bf16[2,256,512]{2,1,0:T(8,128)(2,1)}, u32[]{:S(2)}) copy-start(bf16[2,256,512]{2,1,0:T(8,128)(2,1)} %constant.204.clone.refs_3_) | copy-start | bytes 1572868
  0.6 31.8 %copy-start.9 = (f32[64,2]{0,1:T(2,128)S(1)}, f32[64,2]{0,1:T(2,128)}, u32[]{:S(2)}) copy-start(f32[64,2]{0,1:T(2,128)} %param.17) | copy-start | bytes 1540
  2.5 44.4 %copy-start.2 = (bf16[2,256,512]{2,1,0:T(8,128)(2,1)S(1)}, bf16[2,256,512]{2,1,0:T(8,128)(2,1)}, u32[]{:S(2)}) copy-start(bf16[2,256,512]{2,1,0:T(8,128)(2,1)} %constant.208.clone.refs_6_) | copy-start | bytes 1572868
  2.5 44.4 %copy-start.4 = (bf16[2,256,256]{2,1,0:T(8,128)(2,1)S(1)}, bf16[2,256,256]{2,1,0:T(8,128)(2,1)}, u32[]{:S(2)}) copy-start(bf16[2,256,256]{2,1,0:T(8,128)(2,1)} %constant.207.clone.refs_5_) | copy-start | bytes 786436
  2.5 44.4 %copy-start.5 = (bf16[2,128,64]{2,1,0:T(8,128)(2,1)S(1)}, bf16[2,128,64]{2,1,0:T(8,128)(2,1)}, u32[]{:S(2)}) copy-start(bf16[2,128,64]{2,1,0:T(8,128)(2,1)} %constant.205.clone.refs_3_) | copy-start | bytes 98308
  2.5 44.4 %copy-start.6 = (f32[2,32,256]{2,1,0:T(8,128)S(1)}, f32[2,32,256]{2,1,0:T(8,128)}, u32[]{:S(2)}) copy-start(f32[2,32,256]{2,1,0:T(8,128)} %constant.206.clone.refs_4_) | copy-start | bytes 196612
  2.5 44.4 %copy-start.7 = (f32[2,32,256]{2,1,0:T(8,128)S(1)}, f32[2,32,256]{2,1,0:T(8,128)}, u32[]{:S(2)}) copy-start(f32[2,32,256]{2,1,0:T(8,128)} %constant.209.clone.refs_7_) | copy-start | bytes 196612
  2.5 44.4 %copy-start.8 = (bf16[2,64,64]{2,1,0:T(8,128)(2,1)S(1)}, bf16[2,64,64]{2,1,0:T(8,128)(2,1)}, u32[]{:S(2)}) copy-start(bf16[2,64,64]{2,1,0:T(8,128)(2,1)} %constant.210.clone.refs_8_) | copy-start | bytes 49156
  2.5 11.5 %all-to-all-start = ((f32[4,72,256]{2,1,0:T(8,128)}), f32[4,72,256]{2,1,0:T(8,128)S(1)}, u32[]{:S(2)}, u32[]{:S(2)}) async-start(f32[4,72,256]{2,1,0:T(8,128)} %shard_map.182), calls=%async_computation | async-start | bytes 589824 | tf_op jit(solution)/shard_map/all_to_all | solution.py:335
  15.8 30.9 %all-to-all-start.1 = ((f32[128,2,256]{2,1,0:T(2,128)}), f32[128,2,256]{2,1,0:T(2,128)S(1)}, u32[]{:S(2)}, u32[]{:S(2)}) async-start(f32[128,2,256]{2,1,0:T(2,128)} %shard_map.183), calls=%async_computation.1 | async-start | bytes 524288 | tf_op jit(solution)/shard_map/all_to_all | solution.py:335
  32.4 23.0 %copy-start.11 = (s32[384]{0:T(512)S(1)}, s32[384]{0:T(512)}, u32[]{:S(2)}) copy-start(s32[384]{0:T(512)} %constant.203.clone) | copy-start | bytes 4612
  32.5 15.4 %collective-permute-start = (f32[2,2,256]{2,1,0:T(2,128)S(1)}, f32[2,2,256]{2,1,0:T(2,128)S(1)}, u32[]{:S(2)}, u32[]{:S(2)}) collective-permute-start(f32[2,2,256]{2,1,0:T(2,128)S(1)} %get-tuple-element.23), channel_id=1, source_target_pairs={{0,1},{1,2},{2,3},{3,4},{4,5},{5,6},{6,7},{7,8},{8,9},{9,10},{10,1... | collective-permute-start | bytes 12296 | tf_op jit(solution)/shard_map/ppermute | solution.py:339
  34.7 33.9 %copy-start.3 = (bf16[256,768]{1,0:T(8,128)(2,1)S(1)}, bf16[256,768]{1,0:T(8,128)(2,1)}, u32[]{:S(2)}) copy-start(bf16[256,768]{1,0:T(8,128)(2,1)} %constant.211.clone.refs_3_) | copy-start | bytes 1179652
  47.9 26.2 %copy-start.12 = (bf16[2,64]{1,0:T(2,128)(2,1)S(1)}, bf16[2,64]{1,0:T(2,128)(2,1)}, u32[]{:S(2)}) copy-start(bf16[2,64]{1,0:T(2,128)(2,1)} %param.20) | copy-start | bytes 772
  48.6 25.9 %copy-start.10 = (bf16[1,64,64]{2,1,0:T(8,128)(2,1)S(1)}, bf16[1,64,64]{2,1,0:T(8,128)(2,1)}, u32[]{:S(2)}) copy-start(bf16[1,64,64]{2,1,0:T(8,128)(2,1)} %param.19) | copy-start | bytes 24580
  48.6 25.9 %copy-start = (f32[2,32,256]{2,1,0:T(8,128)S(1)}, f32[2,32,256]{2,1,0:T(8,128)}, u32[]{:S(2)}) copy-start(f32[2,32,256]{2,1,0:T(8,128)} %param.15) | copy-start | bytes 196612
  48.6 19.9 %all-to-all-start.2 = ((bf16[128,2,384]{2,1,0:T(2,128)(2,1)}), bf16[128,2,384]{2,1,0:T(2,128)(2,1)S(1)}, u32[]{:S(2)}, u32[]{:S(2)}) async-start(bf16[128,2,384]{2,1,0:T(2,128)(2,1)} %reshape.521), calls=%async_computation.2 | async-start | bytes 393216 | tf_op jit(solution)/shard_map/all_to_all | solution.py:335
  55.6 15.0 %collective-permute-start.1 = (f32[2,2,256]{2,1,0:T(2,128)S(1)}, f32[2,2,256]{2,1,0:T(2,128)S(1)}, u32[]{:S(2)}, u32[]{:S(2)}) collective-permute-start(f32[2,2,256]{2,1,0:T(2,128)S(1)} %get-tuple-element.25), channel_id=1, source_target_pairs={{0,31},{1,0},{2,1},{3,2},{4,3},{5,4},{6,5},{7,6},{8,7},{9,8},{10,9... | collective-permute-start | bytes 12296 | tf_op jit(solution)/shard_map/ppermute | solution.py:339
  70.6 12.6 %all-to-all-start.3 = ((f32[4,72,384]{2,1,0:T(8,128)}), f32[4,72,384]{2,1,0:T(8,128)S(1)}, u32[]{:S(2)}, u32[]{:S(2)}) async-start(f32[4,72,384]{2,1,0:T(8,128)} %bitcast.6), calls=%async_computation.3 | async-start | bytes 884736 | tf_op jit(solution)/shard_map/all_to_all | solution.py:335
  86.0 12.2 %all-to-all-start.4 = ((f32[16,16,128]{2,1,0:T(8,128)}), f32[16,16,128]{2,1,0:T(8,128)S(1)}, u32[]{:S(2)}, u32[]{:S(2)}) async-start(f32[16,16,128]{2,1,0:T(8,128)} %bitcast.28), calls=%async_computation.4 | async-start | bytes 262144 | tf_op jit(solution)/shard_map/all_to_all | solution.py:335
  98.9 18.2 %all-to-all-start.5 = ((f32[32,16,128]{2,1,0:T(8,128)}), f32[32,16,128]{2,1,0:T(8,128)S(1)}, u32[]{:S(2)}, u32[]{:S(2)}) async-start(f32[32,16,128]{2,1,0:T(8,128)} %bitcast.29), calls=%async_computation.5 | async-start | bytes 524288 | tf_op jit(solution)/shard_map/all_to_all | solution.py:335
